TPU v7x, 512 devices: a whole 4x8x8 slice. The times are simulated.
512 devices in a mesh: state: 64 (over y_hi, z, core), basis: 8 (over y_lo, x).
Axes of the slice: x: 4, y: 8 (y_hi: 4, y_lo: 2; y = y_hi * 2 + y_lo), z: 8, core: 2. Of those that a mesh axis runs over, the one named last changes fastest.
Arguments:
- upper_coef: bfloat16 [24576, 16384], P('basis', 'state'), may hold values from -6 to 6
- lower_state_store: bfloat16 [24576, 8192], P('basis', 'state'), may hold values from -0.0390625 to 0.0390625
- owners: int32 [4], replicated, may hold values from 0 to 63, as said below
- dipole: bfloat16 [192, 3, 128, 128], P('basis'), may hold values from -0.3125 to 0.3125
- offsets: int32 [192, 3], P('basis'), may hold values from -2 to 2
- lower_energy: float32 [512], P('basis'), may hold values from 0 to 2
- upper_energy: float32 [16384], P('state'), may hold values from 2.5 to 5
Outputs:
- moments: float32 [512, 16384], P('basis', 'state')
- intensity: float32 [512, 16384], P('basis', 'state')
Inputs may be any that keep to these rules, and one draw needn't show every extreme that they name: owners are distinct state indices.
All inputs are finite; a program needn't handle non-finite values.
Results may differ from a plain program's by a relative error of at most 0.009.
Values may be sent and summed in bfloat16 or wider, within the bound.
No kernel may reach another device: no remote copies, remote signals or barrier semaphores. Data moves between devices by JAX's collectives and lax.ppermute only.
A program may use at most 128 MiB of HBM per device.

v0:
```python
import jax
import jax.numpy as jnp
from jax import lax
from jax.sharding import PartitionSpec as P

BS = 128
COLUMN_BLOCKS = 3
REACH = 2
PANELS = 4


def broadcast(value, axis, root):
    mine = lax.axis_index(axis) == root
    return lax.psum(jnp.where(mine, value, jnp.zeros_like(value)), axis)


def padded(cells, sides, width):
    for axis, dim in sides:
        count = lax.axis_size(axis)
        ends = count - 1
        head = lax.slice_in_dim(cells, 0, width, axis=dim)
        tail = lax.slice_in_dim(cells, cells.shape[dim] - width, cells.shape[dim], axis=dim)
        cells = jnp.concatenate(
            [
                lax.ppermute(tail, axis, [(i, (i + 1) % count) for i in range(ends)]),
                cells,
                lax.ppermute(head, axis, [((i + 1) % count, i) for i in range(ends)]),
            ],
            axis=dim,
        )
    return cells


def on_device(upper_coef, lower_state_store, owners, dipole, offsets, lower_energy, upper_energy):
    nblk_local = dipole.shape[0]
    up_local = upper_coef.shape[1]
    pieces = []
    for panel_id in range(PANELS):
        pieces.append(broadcast(lower_state_store, "state", owners[panel_id]))
    panels = jnp.concatenate(pieces, axis=1)
    lower_cols = panels.shape[1]
    destination_rows = jnp.arange(nblk_local, dtype=jnp.int32)[:, None] + offsets + REACH
    widened_rows = padded(panels, (("basis", 0),), REACH * BS)
    blocked = widened_rows.reshape(nblk_local + 2 * REACH, BS, lower_cols)
    picked_entries = blocked[destination_rows]
    half = jnp.zeros((nblk_local, BS, lower_cols), jnp.float32)
    for block_index_list in range(COLUMN_BLOCKS):
        half = half + jnp.einsum(
            "udz,udq->uzq",
            dipole[:, block_index_list],
            picked_entries[:, block_index_list],
            preferred_element_type=jnp.float32,
        )
    half_low = half.astype(jnp.bfloat16)
    coef_blocks = upper_coef.reshape(nblk_local, BS, up_local)
    partial_value = jnp.einsum(
        "cjl,cju->lu", half_low, coef_blocks, preferred_element_type=jnp.float32
    )
    moments = lax.psum_scatter(partial_value, "basis", scatter_dimension=0, tiled=True)
    nu = upper_energy[None, :] - lower_energy[:, None]
    intensity = moments * moments * nu * jnp.exp(-lower_energy)[:, None] * (1.0 - jnp.exp(-nu))
    return (moments, intensity)


def solution(mesh):
    placed = (
        P("basis", "state"),
        P("basis", "state"),
        P(),
        P("basis", None, None, None),
        P("basis", None),
        P("basis"),
        P("state"),
    )
    return jax.shard_map(
        on_device,
        mesh=mesh,
        in_specs=placed,
        out_specs=(P("basis", "state"), P("basis", "state")),
        check_vma=False,
    )
```

profile of v0, /device:TPU:1, one launch (start us, length us, event | category | flops | bytes accessed | tf_op | source)
XLA Modules:
  0.0 680.2 jit_solution(6098897502795110964)
XLA Ops:
  7.2 0.0 copy-start
  7.2 0.0 all-reduce.3.cloned.1.call-start
  7.2 1.5 fusion.22
  11.2 2.8 broadcast_select_fusion
  14.1 0.0 all-reduce.3.cloned.1.call-update
  14.1 0.0 reduce-scatter.2.cloned.1.call-start
  14.2 573.2 %all-reduce.3.cloned.1.call-done = (bf16[3072,128]{1,0:T(8,128)(2,1)}, bf16[3072,128]{1,0:T(8,128)(2,1)}, bf16[3072,128]{1,0:T(8,128)(2,1)}, bf16[3072,128]{1,0:T(8,128)(2,1)}) async-done(((bf16[3072,128]{1,0:T(8,128)(2,1)}, bf16[3072,128]{1,0:T(8,128)(2,1)}, bf16[3072,128]{1,0:T(8,128)(2,1)}, bf16[3072,128]{1,0:T(8,128)(2,1)}), (bf16[3072,128]{1,0:T(8,128)(2,1)}, bf16[3072,128]{1,0:T(8,128)(2,1)}, ...) | async-done | bytes 3145744 | tf_op jit(solution)/shard_map/psum | solution.py:14
  587.4 0.0 copy-start.3
  587.4 0.0 copy-start.2
  587.4 1.4 constant_dynamic-update-slice_fusion.3
  588.8 0.0 copy-start.4
  588.8 1.3 constant_dynamic-update-slice_fusion.2
  590.1 0.0 copy-done.3
  590.1 0.2 constant_dynamic-update-slice_fusion.1
  590.3 0.0 copy-done.2
  590.3 0.2 constant_dynamic-update-slice_fusion
  590.5 0.0 copy-start.1
  590.5 1.6 copy-done.1
  592.2 3.2 collective-permute-start
  595.4 1.3 collective-permute-start.1
  596.7 0.0 copy-done.4
  596.7 0.1 copy.10
  596.8 0.1 reshape.17
  596.9 3.7 collective-permute-done
  600.6 3.8 collective-permute-done.1
  604.4 3.4 pad_maximum_fusion
  607.8 8.0 %gather_fusion = bf16[72,128,512]{2,1,0:T(8,128)(2,1)} fusion(bf16[28,128,512]{2,1,0:T(8,128)(2,1)} %bitcast.41, s32[1024]{0:T(1024)S(1)} %pad_clamp_fusion), kind=kCustom, calls=%fused_computation | custom fusion | bytes 18874656 | tf_op jit(solution)/shard_map/gather | solution.py:45
  615.9 5.8 fusion.3
  621.7 5.8 fusion.4
  627.4 0.0 copy-done
  627.4 0.0 copy-start.6
  627.4 0.0 copy-start.5
  627.4 8.8 %fusion.6 = f32[512,256]{1,0:T(8,128)} fusion(bf16[24,128,256]{2,1,0:T(8,128)(2,1)S(1)} %bitcast.40, f32[24,512,128]{2,1,0:T(8,128)} %fusion.3, f32[24,512,128]{2,1,0:T(8,128)} %fusion.4, bf16[24,3,128,512]{3,2,1,0:T(8,128)(2,1)} %bitcast.44, bf16[24,3,128,128]{3,2,1,0:T(8,128)(2,1)} %param.10), kind=kOutput, calls=%fused_computation.11 | convolution fusion | flops 1212678144 | bytes 18612224 | tf_op jit(solution)/shard_map/cjl,cju->lu/dot_general | solution.py:56
  636.2 0.0 reduce-scatter.2.cloned.1.call-update
  636.2 0.0 copy-done.6
  636.2 35.6 %reduce-scatter.2.cloned.1.call-done = f32[64,256]{1,0:T(8,128)} async-done(((f32[512,256]{1,0:T(8,128)}), f32[64,256]{1,0:T(8,128)}) %reduce-scatter.2.cloned.1.call-update) | async-done | bytes 65552 | tf_op jit(solution)/shard_map/reduce_scatter | solution.py:59
  671.8 0.0 copy-done.5
  671.8 1.6 fusion.18
  (4 shorter events, 0.1 us)
Async XLA Ops:
  7.2 620.3 %copy-start = (bf16[3072,256]{1,0:T(8,128)(2,1)S(1)}, bf16[3072,256]{1,0:T(8,128)(2,1)}, u32[]{:S(2)}) copy-start(bf16[3072,256]{1,0:T(8,128)(2,1)} %param.7) | copy-start | bytes 4718596
  7.2 580.2 %all-reduce.3.cloned.1.call-start = ((), (), s32[]{:S(2)}) async-start(), calls=%async_computation.2 | async-start | bytes 6291456 | tf_op jit(solution)/shard_map/psum | solution.py:14
  14.1 657.7 %reduce-scatter.2.cloned.1.call-start = ((), (), s32[]{:S(2)}) async-start(), calls=%async_computation.1 | async-start | bytes 589824 | tf_op jit(solution)/shard_map/reduce_scatter | solution.py:59
  587.4 2.7 copy-start.3
  587.4 2.9 copy-start.2
  588.8 7.9 %copy-start.4 = (s32[24,3]{0,1:T(4,128)S(1)}, s32[24,3]{0,1:T(4,128)}, u32[]{:S(2)}) copy-start(s32[24,3]{0,1:T(4,128)} %param.11) | copy-start | bytes 868
  590.5 1.6 copy-start.1
  592.2 8.4 %collective-permute-start = (bf16[256,512]{1,0:T(8,128)(2,1)S(1)}, bf16[256,512]{1,0:T(8,128)(2,1)S(1)}, u32[]{:S(2)}, u32[]{:S(2)}) collective-permute-start(bf16[256,512]{1,0:T(8,128)(2,1)S(1)} %get-tuple-element.6), channel_id=1, source_target_pairs={{0,1},{1,2},{2,3},{3,4},{4,5},{5,6},{6,7},{8,9},{9,10},{10,11},{11... | collective-permute-start | bytes 786440 | tf_op jit(solution)/shard_map/ppermute | solution.py:25
  595.4 9.1 %collective-permute-start.1 = (bf16[256,512]{1,0:T(8,128)(2,1)S(1)}, bf16[256,512]{1,0:T(8,128)(2,1)S(1)}, u32[]{:S(2)}, u32[]{:S(2)}) collective-permute-start(bf16[256,512]{1,0:T(8,128)(2,1)S(1)} %get-tuple-element.7), channel_id=1, source_target_pairs={{1,0},{2,1},{3,2},{4,3},{5,4},{6,5},{7,6},{9,8},{10,9},{11,10},{12... | collective-permute-start | bytes 786440 | tf_op jit(solution)/shard_map/ppermute | solution.py:27
  627.4 8.8 %copy-start.6 = (f32[64]{0:T(128)S(1)}, f32[64]{0:T(128)}, u32[]{:S(2)}) copy-start(f32[64]{0:T(128)} %param.12) | copy-start | bytes 772
  627.4 44.4 %copy-start.5 = (f32[256]{0:T(256)S(1)}, f32[256]{0:T(256)}, u32[]{:S(2)}) copy-start(f32[256]{0:T(256)} %param.13) | copy-start | bytes 3076
Sparse Core Ops, SparseCore 0:
  14.2 573.0 all-reduce.2
  636.3 35.4 reduce-scatter.1
where the time goes:
time: 684 us; the launch traced here: 680 us
  waiting for transfers between devices  616 us (90%)
  matrix products  20.3 us (3%)
  between operations  16.7 us (2%)
  local copies, waits for them, and re-layouts  14.4 us (2%)
  other arithmetic  7.83 us (1%)
    psum x1, waiting for transfers between devices, broadcast(): return lax.psum(jnp.where(mine, value, jnp.zeros_like(value)), axis)  573 us
    reduce_scatter x1, waiting for transfers between devices, on_device(): lax.psum_scatter(partial_value, 'basis', scatter_dimension=0, tiled=True)  35.6 us
  transfers between devices with their start and end apart: 4, of which 4 were waited for; matrix products, arithmetic and copies ran while one was open for 0% of the time, Pallas kernels for 0%

commit v1 on v0

v1 whole, which is shorter than its diff:
```python
import jax
import jax.numpy as jnp
from jax import lax
from jax.sharding import Mesh
from jax.sharding import PartitionSpec as P

BS = 128
REACH = 2
PANELS = 4
BF16 = jnp.bfloat16
F32 = jnp.float32

SIZES = {"yhi": 4, "z": 8, "core": 2, "ylo": 2, "x": 4}
STATE = ("yhi", "z", "core")
BASIS = ("ylo", "x")
GATHER_ORDER = ("core", "z", "yhi")


def own_half(store, dipole, offsets):
    nblk = dipole.shape[0]
    count = lax.axis_size(BASIS)
    width = REACH * BS
    up = lax.ppermute(store[-width:], BASIS, [(i, i + 1) for i in range(count - 1)])
    down = lax.ppermute(store[:width], BASIS, [(i + 1, i) for i in range(count - 1)])
    blocked = jnp.concatenate([up, store, down], axis=0).reshape(nblk + 2 * REACH, BS, -1)
    rows = jnp.arange(nblk, dtype=jnp.int32)[:, None] + offsets + REACH
    picked = blocked[rows]
    half = jnp.einsum("ckdz,ckdq->czq", dipole, picked, preferred_element_type=F32)
    return half.astype(BF16).reshape(store.shape)


def on_device(upper_coef, store, owners, dipole, offsets, lower_energy, upper_energy):
    half = own_half(store, dipole, offsets)
    pieces = lax.all_to_all(half, GATHER_ORDER, 0, 0, tiled=True)
    members = lax.axis_size(GATHER_ORDER)
    pieces = pieces.reshape(members, -1, half.shape[1])
    core = owners % 2
    z = (owners // 2) % SIZES["z"]
    yhi = owners // (2 * SIZES["z"])
    source = (core * SIZES["z"] + z) * SIZES["yhi"] + yhi
    chunk = jnp.concatenate(
        [lax.dynamic_index_in_dim(pieces, source[p], 0, keepdims=False) for p in range(PANELS)],
        axis=1,
    )
    chunk = lax.all_gather(chunk, "yhi", axis=0, tiled=True)
    chunk = lax.all_gather(chunk, "z", axis=0, tiled=True)
    other = lax.ppermute(chunk, "core", [(0, 1), (1, 0)])
    first = lax.axis_index("core") == 0
    rows = chunk.shape[0]
    mine = lax.axis_index("core") * rows
    theirs = rows - mine
    dims = (((0,), (0,)), ((), ()))
    share = lax.dot_general(
        chunk, lax.dynamic_slice_in_dim(upper_coef, mine, rows, 0), dims, preferred_element_type=F32
    ) + lax.dot_general(
        other, lax.dynamic_slice_in_dim(upper_coef, theirs, rows, 0), dims, preferred_element_type=F32
    )
    shares = lax.all_to_all(share.astype(BF16), BASIS, 0, 0, tiled=True)
    shares = shares.reshape(lax.axis_size(BASIS), -1, share.shape[1])
    moments = jnp.sum(shares.astype(F32), axis=0)
    nu = upper_energy[None, :] - lower_energy[:, None]
    intensity = moments * moments * nu * jnp.exp(-lower_energy)[:, None] * (1.0 - jnp.exp(-nu))
    return moments, intensity


def solution(mesh):
    fine = Mesh(mesh.devices.reshape(tuple(SIZES.values())), tuple(SIZES))
    placed = (
        P(BASIS, STATE),
        P(BASIS, STATE),
        P(),
        P(BASIS, None, None, None),
        P(BASIS, None),
        P(BASIS),
        P(STATE),
    )
    return jax.shard_map(
        on_device,
        mesh=fine,
        in_specs=placed,
        out_specs=(P(BASIS, STATE), P(BASIS, STATE)),
        check_vma=False,
    )
```

time: 684 us -> 150 us (0.22)
  waiting for transfers between devices: 616 us -> 64.6 us
  starting transfers between devices: 4.56 us -> 35 us
  blocking collectives: 0 us -> 12.4 us
  matrix products: 20.3 us -> 8.5 us
  local copies, waits for them, and re-layouts: 14.4 us -> 4.34 us
    psum x1 -> x0, waiting for transfers between devices: 573 us -> none  [broadcast(): return lax.psum(jnp.where(mine, value, jnp.zeros_like(value)), axis)]
    all_gather x0 -> x1, waiting for transfers between devices: none -> 37.3 us  [on_device(): chunk = lax.all_gather(chunk, 'z', axis=0, tiled=True)]
    reduce_scatter x1 -> x0, waiting for transfers between devices: 35.6 us -> none  [on_device(): lax.psum_scatter(partial_value, 'basis', scatter_dimension=0, tiled=True)]
    all_to_all x0 -> x2, waiting for transfers between devices: none -> 23.5 us  [the longest x1 17.3 us: on_device(): pieces = lax.all_to_all(half, GATHER_ORDER, 0, 0, tiled=True)]
    all_to_all x0 -> x2, starting transfers between devices: none -> 23.2 us  [the longest x1 18.3 us: on_device(): pieces = lax.all_to_all(half, GATHER_ORDER, 0, 0, tiled=True)]
    all_gather x0 -> x1, blocking collectives: none -> 12.4 us  [on_device(): chunk = lax.all_gather(chunk, 'yhi', axis=0, tiled=True)]
    dot_general x3, matrix products: 20.3 us -> 8.5 us  [the longest x1 3.44 us: own_half(): jnp.einsum('ckdz,ckdq->czq', dipole, picked, preferred_element_type=F32)]
    ppermute x2 -> x3, starting transfers between devices: 4.48 us -> 11.7 us  [the longest x1 6.47 us: on_device(): other = lax.ppermute(chunk, 'core', [(0, 1), (1, 0)])]
  transfers between devices with their start and end apart: 4 -> 6, of which waited for: 4 -> 5; matrix products, arithmetic and copies ran while one was open for 0% -> 3% of each run, Pallas kernels for 0% -> 0%
where the time goes in v1:
time: 150 us; the launch traced here: 149 us
  waiting for transfers between devices  64.6 us (43%)
  starting transfers between devices  35 us (23%)
  between operations  21.6 us (14%)
  blocking collectives  12.4 us (8%)
  matrix products  8.5 us (6%)
  local copies, waits for them, and re-layouts  4.34 us (3%)
  other arithmetic  2.68 us (2%)
    all_gather x1, waiting for transfers between devices, on_device(): chunk = lax.all_gather(chunk, 'z', axis=0, tiled=True)  37.3 us
    all_to_all x1, starting transfers between devices, on_device(): pieces = lax.all_to_all(half, GATHER_ORDER, 0, 0, tiled=True)  18.3 us
    all_to_all x1, waiting for transfers between devices, on_device(): pieces = lax.all_to_all(half, GATHER_ORDER, 0, 0, tiled=True)  17.3 us
    all_gather x1, blocking collectives, on_device(): chunk = lax.all_gather(chunk, 'yhi', axis=0, tiled=True)  12.4 us
    ppermute x1, starting transfers between devices, on_device(): other = lax.ppermute(chunk, 'core', [(0, 1), (1, 0)])  6.47 us
    all_to_all x1, waiting for transfers between devices, on_device(): shares = lax.all_to_all(share.astype(BF16), BASIS, 0, 0, tiled=True)  6.19 us
    all_to_all x1, starting transfers between devices, on_device(): shares = lax.all_to_all(share.astype(BF16), BASIS, 0, 0, tiled=True)  4.9 us
    ppermute x1, starting transfers between devices, own_half(): lax.ppermute(store[-width:], BASIS, [(i, i + 1) for i in range(count - 1)])  3.95 us
  transfers between devices with their start and end apart: 6, of which 5 were waited for; matrix products, arithmetic and copies ran while one was open for 3% of the time, Pallas kernels for 0%

profile of v1, /device:TPU:1, one launch (start us, length us, event | category | flops | bytes accessed | tf_op | source)
XLA Modules:
  0.0 149.2 jit_solution(1490781244707199702)
XLA Ops:
  7.2 0.0 copy-start
  7.2 1.0 fusion.13
  8.2 3.9 %collective-permute-start = (bf16[256,128]{1,0:T(8,128)(2,1)S(1)}, bf16[256,128]{1,0:T(8,128)(2,1)S(1)}, u32[]{:S(2)}, u32[]{:S(2)}) collective-permute-start(bf16[256,128]{1,0:T(8,128)(2,1)S(1)} %get-tuple-element.6), channel_id=1, source_target_pairs={{0,1},{1,2},{2,3},{3,4},{4,5},{5,6},{6,7},{8,9},{9,10},{10,11},{11... | collective-permute-start | bytes 196616 | tf_op jit(solution)/shard_map/ppermute | solution.py:23
  12.2 1.3 collective-permute-start.1
  13.5 0.7 compare_select_fusion
  14.2 0.1 copy.11
  14.3 0.1 reshape.25
  14.4 0.0 collective-permute-done
  14.4 2.8 %collective-permute-done.1 = bf16[256,128]{1,0:T(8,128)(2,1)S(1)} collective-permute-done((bf16[256,128]{1,0:T(8,128)(2,1)S(1)}, bf16[256,128]{1,0:T(8,128)(2,1)S(1)}, u32[]{:S(2)}, u32[]{:S(2)}) %collective-permute-start.1) | collective-permute-done | bytes 65568 | tf_op jit(solution)/shard_map/ppermute | solution.py:24
  17.2 1.2 pad_maximum_fusion
  18.4 2.5 %gather_fusion = bf16[72,128,128]{2,1,0:T(8,128)(2,1)} fusion(bf16[28,128,128]{2,1,0:T(8,128)(2,1)S(1)} %bitcast.25, s32[1024]{0:T(1024)S(1)} %pad_clamp_fusion), kind=kCustom, calls=%fused_computation | custom fusion | bytes 4718880 | tf_op jit(solution)/shard_map/gather | solution.py:27
  20.8 0.0 copy-done
  20.8 0.0 copy-start.5
  20.9 3.4 %bitcast_convert_fusion = bf16[24,128,128]{1,2,0:T(8,128)(2,1)} fusion(bf16[24,3,128,128]{3,2,1,0:T(8,128)(2,1)} %bitcast.26, bf16[24,3,128,128]{3,2,1,0:T(8,128)(2,1)S(1)} %copy-done), kind=kOutput, calls=%fused_computation.1 | convolution fusion | flops 302383104 | bytes 5505024 | tf_op jit(solution)/shard_map/ckdz,ckdq->czq/dot_general | solution.py:28
  24.3 18.3 %all-to-all-start = ((bf16[64,48,128]{2,1,0:T(8,128)(2,1)}), bf16[64,48,128]{2,1,0:T(8,128)(2,1)S(1)}, u32[]{:S(2)}, u32[]{:S(2)}) async-start(bf16[64,48,128]{2,1,0:T(8,128)(2,1)} %bitcast.5), calls=%async_computation | async-start | bytes 1572864 | tf_op jit(solution)/shard_map/all_to_all | solution.py:34
  42.6 0.0 all-gather.2.cloned.1.call-start
  42.7 0.0 copy-done.5
  42.7 0.6 fusion.14
  50.8 17.3 %all-to-all-done = bf16[64,48,128]{2,1,0:T(8,128)(2,1)S(1)} async-done(((bf16[64,48,128]{2,1,0:T(8,128)(2,1)}), bf16[64,48,128]{2,1,0:T(8,128)(2,1)S(1)}, u32[]{:S(2)}, u32[]{:S(2)}) %all-to-all-start) | async-done | bytes 786464 | tf_op jit(solution)/shard_map/all_to_all | solution.py:34
  68.1 12.4 %all_gather.6 = bf16[192,512]{1,0:T(8,128)(2,1)} all-gather(bf16[48,512]{1,0:T(8,128)(2,1)S(1)} %pad_maximum_fusion.1), channel_id=1, replica_groups=mesh['yhi'=4,'z'=8,'core'=2,'ylo'=2,'x'=4] {'yhi'}, dimensions={0}, use_global_device_ids=true | all-gather | bytes 245760 | tf_op jit(solution)/shard_map/all_gather | solution.py:45
  80.6 0.0 all-gather.2.cloned.1.call-update
  80.6 37.3 %all-gather.2.cloned.1.call-done = bf16[1536,512]{1,0:T(8,128)(2,1)} async-done(((bf16[192,512]{1,0:T(8,128)(2,1)}), bf16[1536,512]{1,0:T(8,128)(2,1)}) %all-gather.2.cloned.1.call-update) | async-done | bytes 1572880 | tf_op jit(solution)/shard_map/all_gather | solution.py:46
  117.9 6.5 %collective-permute-start.2 = (bf16[1536,512]{1,0:T(8,128)(2,1)}, bf16[1536,512]{1,0:T(8,128)(2,1)}, u32[]{:S(2)}, u32[]{:S(2)}) collective-permute-start(bf16[1536,512]{1,0:T(8,128)(2,1)} %all-gather.2.cloned.1.call-done), channel_id=1, source_target_pairs={{0,8},{8,0},{1,9},{9,1},{2,10},{10,2},{3,11},{11,3},{4,12},{12,4},... | collective-permute-start | bytes 4718600 | tf_op jit(solution)/shard_map/ppermute | solution.py:47
  124.4 0.0 copy-start.4
  124.4 2.3 %fusion.2 = f32[512,256]{1,0:T(8,128)S(1)} fusion(bf16[1536,512]{1,0:T(8,128)(2,1)} %all-gather.2.cloned.1.call-done, bf16[3072,256]{1,0:T(8,128)(2,1)} %param.7, s32[]{:T(128)S(6)} %select_n.50), kind=kOutput, calls=%fused_computation.6 | convolution fusion | flops 402653184 | bytes 2883588 | tf_op jit(solution)/shard_map/dot_general | solution.py:53
  126.7 0.0 copy-start.3
  126.7 0.0 copy-start.2
  126.7 1.0 collective-permute-done.2
  127.7 0.0 copy-done.4
  127.7 2.7 %fusion = bf16[512,256]{1,0:T(8,128)(2,1)} fusion(f32[512,256]{1,0:T(8,128)S(1)} %fusion.2, bf16[1536,512]{1,0:T(8,128)(2,1)} %collective-permute-done.2, bf16[3072,256]{1,0:T(8,128)(2,1)S(1)} %copy-done.4, s32[]{:T(128)S(6)} %select_n.51), kind=kOutput, calls=%fused_computation.3 | convolution fusion | flops 402915328 | bytes 3145732 | tf_op jit(solution)/shard_map/dot_general | solution.py:55
  130.4 4.9 %all-to-all-start.1 = ((bf16[8,64,256]{2,1,0:T(8,128)(2,1)}), bf16[8,64,256]{2,1,0:T(8,128)(2,1)S(1)}, u32[]{:S(2)}, u32[]{:S(2)}) async-start(bf16[8,64,256]{2,1,0:T(8,128)(2,1)} %bitcast.14), calls=%async_computation.1 | async-start | bytes 524288 | tf_op jit(solution)/shard_map/all_to_all | solution.py:58
  135.3 0.0 copy-done.3
  135.4 6.2 %all-to-all-done.1 = bf16[8,64,256]{2,1,0:T(8,128)(2,1)S(1)} async-done(((bf16[8,64,256]{2,1,0:T(8,128)(2,1)}), bf16[8,64,256]{2,1,0:T(8,128)(2,1)S(1)}, u32[]{:S(2)}, u32[]{:S(2)}) %all-to-all-start.1) | async-done | bytes 262176 | tf_op jit(solution)/shard_map/all_to_all | solution.py:58
  141.6 0.0 copy-done.2
  141.6 0.0 copy-start.1
  141.6 0.7 fusion.5
  142.3 0.0 copy-done.1
  (6 shorter events, 0.1 us)
Async XLA Ops:
  7.2 13.7 %copy-start = (bf16[24,3,128,128]{3,2,1,0:T(8,128)(2,1)S(1)}, bf16[24,3,128,128]{3,2,1,0:T(8,128)(2,1)}, u32[]{:S(2)}) copy-start(bf16[24,3,128,128]{3,2,1,0:T(8,128)(2,1)} %param.10) | copy-start | bytes 7077892
  8.2 6.1 %collective-permute-start = (bf16[256,128]{1,0:T(8,128)(2,1)S(1)}, bf16[256,128]{1,0:T(8,128)(2,1)S(1)}, u32[]{:S(2)}, u32[]{:S(2)}) collective-permute-start(bf16[256,128]{1,0:T(8,128)(2,1)S(1)} %get-tuple-element.6), channel_id=1, source_target_pairs={{0,1},{1,2},{2,3},{3,4},{4,5},{5,6},{6,7},{8,9},{9,10},{10,11},{11... | collective-permute-start | bytes 196616 | tf_op jit(solution)/shard_map/ppermute | solution.py:23
  12.2 5.0 %collective-permute-start.1 = (bf16[256,128]{1,0:T(8,128)(2,1)S(1)}, bf16[256,128]{1,0:T(8,128)(2,1)S(1)}, u32[]{:S(2)}, u32[]{:S(2)}) collective-permute-start(bf16[256,128]{1,0:T(8,128)(2,1)S(1)} %get-tuple-element.7), channel_id=1, source_target_pairs={{1,0},{2,1},{3,2},{4,3},{5,4},{6,5},{7,6},{9,8},{10,9},{11,10},{12... | collective-permute-start | bytes 196616 | tf_op jit(solution)/shard_map/ppermute | solution.py:24
  20.8 21.8 %copy-start.5 = (s32[4]{0:T(128)S(1)}, s32[4]{0:T(128)}, u32[]{:S(2)}) copy-start(s32[4]{0:T(128)} %param.9) | copy-start | bytes 52
  24.3 43.8 %all-to-all-start = ((bf16[64,48,128]{2,1,0:T(8,128)(2,1)}), bf16[64,48,128]{2,1,0:T(8,128)(2,1)S(1)}, u32[]{:S(2)}, u32[]{:S(2)}) async-start(bf16[64,48,128]{2,1,0:T(8,128)(2,1)} %bitcast.5), calls=%async_computation | async-start | bytes 1572864 | tf_op jit(solution)/shard_map/all_to_all | solution.py:34
  42.6 75.2 %all-gather.2.cloned.1.call-start = ((), (), s32[]{:S(2)}) async-start(), calls=%async_computation.2 | async-start | bytes 1769472 | tf_op jit(solution)/shard_map/all_gather | solution.py:46
  117.9 9.8 %collective-permute-start.2 = (bf16[1536,512]{1,0:T(8,128)(2,1)}, bf16[1536,512]{1,0:T(8,128)(2,1)}, u32[]{:S(2)}, u32[]{:S(2)}) collective-permute-start(bf16[1536,512]{1,0:T(8,128)(2,1)} %all-gather.2.cloned.1.call-done), channel_id=1, source_target_pairs={{0,8},{8,0},{1,9},{9,1},{2,10},{10,2},{3,11},{11,3},{4,12},{12,4},... | collective-permute-start | bytes 4718600 | tf_op jit(solution)/shard_map/ppermute | solution.py:47
  124.4 3.4 %copy-start.4 = (bf16[3072,256]{1,0:T(8,128)(2,1)S(1)}, bf16[3072,256]{1,0:T(8,128)(2,1)}, u32[]{:S(2)}) copy-start(bf16[3072,256]{1,0:T(8,128)(2,1)} %param.7) | copy-start | bytes 4718596
  126.7 8.6 %copy-start.3 = (f32[64]{0:T(128)S(1)}, f32[64]{0:T(128)}, u32[]{:S(2)}) copy-start(f32[64]{0:T(128)} %param.12) | copy-start | bytes 772
  126.7 14.9 %copy-start.2 = (f32[256]{0:T(256)S(1)}, f32[256]{0:T(256)}, u32[]{:S(2)}) copy-start(f32[256]{0:T(256)} %param.13) | copy-start | bytes 3076
  130.4 11.1 %all-to-all-start.1 = ((bf16[8,64,256]{2,1,0:T(8,128)(2,1)}), bf16[8,64,256]{2,1,0:T(8,128)(2,1)S(1)}, u32[]{:S(2)}, u32[]{:S(2)}) async-start(bf16[8,64,256]{2,1,0:T(8,128)(2,1)} %bitcast.14), calls=%async_computation.1 | async-start | bytes 524288 | tf_op jit(solution)/shard_map/all_to_all | solution.py:58
  141.6 0.7 copy-start.1
Sparse Core Ops, SparseCore 0:
  80.7 37.1 all-gather.1

commit v2 on v1

v2 whole, which is shorter than its diff:
```python
import jax
import jax.numpy as jnp
from jax import lax
from jax.sharding import Mesh
from jax.sharding import PartitionSpec as P

BS = 128
REACH = 2
PANELS = 4
BF16 = jnp.bfloat16
F32 = jnp.float32

SIZES = {"yhi": 4, "z": 8, "core": 2, "ylo": 2, "x": 4}
STATE = ("yhi", "z", "core")
BASIS = ("ylo", "x")
CHIPS = ("z", "yhi")


def chip_half(store, dipole, offsets, core):
    rows, width = store.shape
    ncol = dipole.shape[0] // 2
    reach = REACH * BS
    inside = rows // 2 + reach
    count = lax.axis_size(BASIS)
    swap = [(0, 1), (1, 0)]

    def member(basis, kind):
        return basis + count * kind

    own_pairs = [(member(b, 0), member(b + 1, 0)) for b in range(count - 1)]
    own_pairs += [(member(b + 1, 1), member(b, 1)) for b in range(count - 1)]
    other_pairs = [(member(b, 1), member(b + 1, 0)) for b in range(count - 1)]
    other_pairs += [(member(b + 1, 0), member(b, 1)) for b in range(count - 1)]
    span = rows - reach
    axes = ("core",) + BASIS
    own_edge = lax.ppermute(
        lax.dynamic_slice_in_dim(store, (1 - core) * span, reach, 0), axes, own_pairs
    )
    other_edge = lax.ppermute(
        lax.dynamic_slice_in_dim(store, core * span, reach, 0), axes, other_pairs
    )
    step = rows - inside
    other = lax.ppermute(
        lax.dynamic_slice_in_dim(store, (1 - core) * step, inside, 0), "core", swap
    )
    own = lax.dynamic_slice_in_dim(store, core * step, inside, 0)
    near = jnp.concatenate(
        [jnp.concatenate([own, other], 1), jnp.concatenate([own_edge, other_edge], 1)], 0
    )
    blocks = near.reshape(-1, BS, 2 * width)
    nblocks = blocks.shape[0]
    local_dipole = lax.dynamic_slice_in_dim(dipole, core * ncol, ncol, 0)
    local_offsets = lax.dynamic_slice_in_dim(offsets, core * ncol, ncol, 0)
    place = jnp.arange(ncol, dtype=jnp.int32)[:, None] + local_offsets + core * REACH
    picked = blocks[place % nblocks]
    half = jnp.einsum("ckdz,ckdq->czq", local_dipole, picked, preferred_element_type=F32)
    return half.astype(BF16).reshape(ncol * BS, 2 * width)


def on_device(upper_coef, store, owners, dipole, offsets, lower_energy, upper_energy):
    core = lax.axis_index("core")
    width = store.shape[1]
    half = chip_half(store, dipole, offsets, core)
    chips = lax.axis_size(CHIPS)
    rows = half.shape[0]

    pieces = lax.all_to_all(half, CHIPS, 0, 0, tiled=True)
    pieces = pieces.reshape(chips, rows // chips, 2 * width)

    sent = lax.dynamic_slice_in_dim(upper_coef, (1 - core) * rows, rows, 0)
    kept = lax.dynamic_slice_in_dim(upper_coef, core * rows, rows, 0)
    got = lax.ppermute(sent, "core", [(0, 1), (1, 0)])
    first = core == 0
    upper = jnp.concatenate([jnp.where(first, kept, got), jnp.where(first, got, kept)], 1)

    chip = (owners // 2) % SIZES["z"] * SIZES["yhi"] + owners // (2 * SIZES["z"])
    side = jnp.where(owners % 2 == core, 0, width)
    chunk = jnp.concatenate(
        [
            lax.dynamic_slice(pieces, (chip[p], 0, side[p]), (1, rows // chips, width))[0]
            for p in range(PANELS)
        ],
        axis=1,
    )
    copies = jnp.broadcast_to(chunk[None], (chips,) + chunk.shape)
    gathered = lax.all_to_all(copies, CHIPS, 0, 0, tiled=True).reshape(rows, PANELS * width)

    share = lax.dot_general(
        gathered, upper, (((0,), (0,)), ((), ())), preferred_element_type=F32
    ).astype(BF16)
    lowers, uppers = share.shape
    share = jnp.concatenate([share[:, : uppers // 2], share[:, uppers // 2 :]], 0)
    shares = lax.all_to_all(share, ("core",) + BASIS, 0, 0, tiled=True)
    shares = shares.reshape(2 * lax.axis_size(BASIS), -1, uppers // 2)
    moments = jnp.sum(shares.astype(F32), axis=0)
    nu = upper_energy[None, :] - lower_energy[:, None]
    intensity = moments * moments * nu * jnp.exp(-lower_energy)[:, None] * (1.0 - jnp.exp(-nu))
    return moments, intensity


def solution(mesh):
    fine = Mesh(mesh.devices.reshape(tuple(SIZES.values())), tuple(SIZES))
    placed = (
        P(BASIS, STATE),
        P(BASIS, STATE),
        P(),
        P(BASIS, None, None, None),
        P(BASIS, None),
        P(BASIS),
        P(STATE),
    )
    return jax.shard_map(
        on_device,
        mesh=fine,
        in_specs=placed,
        out_specs=(P(BASIS, STATE), P(BASIS, STATE)),
        check_vma=False,
    )
```

time: 150 us -> 143 us (0.953)
  starting transfers between devices: 35 us -> 49.6 us
  blocking collectives: 12.4 us -> 0 us
  waiting for transfers between devices: 64.6 us -> 55.1 us
  between operations: 21.6 us -> 16 us
  local copies, waits for them, and re-layouts: 4.34 us -> 9.67 us
  other arithmetic: 2.68 us -> 5.59 us
  matrix products: 8.5 us -> 5.82 us
    all_gather x1 -> x0, waiting for transfers between devices: 37.3 us -> none  [on_device(): chunk = lax.all_gather(chunk, 'z', axis=0, tiled=True)]
    all_to_all x2 -> x3, waiting for transfers between devices: 23.5 us -> 49.4 us  [the longest x1 31.8 us: on_device(): lax.all_to_all(copies, CHIPS, 0, 0, tiled=True)]
    all_gather x1 -> x0, blocking collectives: 12.4 us -> none  [on_device(): chunk = lax.all_gather(chunk, 'yhi', axis=0, tiled=True)]
    all_to_all x2 -> x3, starting transfers between devices: 23.2 us -> 35.7 us  [the longest x1 14.5 us: on_device(): shares = lax.all_to_all(share, ('core',) + BASIS, 0, 0, tiled=True)]
    dynamic_slice x0 -> x3, local copies, waits for them, and re-layouts: none -> 4.22 us  [the longest x1 2.14 us: chip_half(): own = lax.dynamic_slice_in_dim(store, core * step, inside, 0)]
    dot_general x3 -> x2, matrix products: 8.5 us -> 5.82 us  [the longest x1 3.21 us: chip_half(): jnp.einsum('ckdz,ckdq->czq', local_dipole, picked, preferred_element_type...]
    ppermute x3 -> x4, starting transfers between devices: 11.7 us -> 13.9 us  [the longest x1 8.77 us: chip_half(): lax.ppermute(lax.dynamic_slice_in_dim(store, (1 - core) * step, inside, 0...]
    select_n x1 -> x3, other arithmetic: 0.69 us -> 2.66 us  [the longest x1 2.55 us: on_device(): jnp.where(first, kept, got)]
  transfers between devices with their start and end apart: 6 -> 7, of which waited for: 5 -> 6; matrix products, arithmetic and copies ran while one was open for 3% -> 4% of each run, Pallas kernels for 0% -> 0%
where the time goes in v2:
time: 143 us; the launch traced here: 142 us
  waiting for transfers between devices  55.1 us (39%)
  starting transfers between devices  49.6 us (35%)
  between operations  16 us (11%)
  local copies, waits for them, and re-layouts  9.67 us (7%)
  matrix products  5.82 us (4%)
  other arithmetic  5.59 us (4%)
    all_to_all x1, waiting for transfers between devices, on_device(): lax.all_to_all(copies, CHIPS, 0, 0, tiled=True)  31.8 us
    all_to_all x1, starting transfers between devices, on_device(): shares = lax.all_to_all(share, ('core',) + BASIS, 0, 0, tiled=True)  14.5 us
    all_to_all x1, starting transfers between devices, on_device(): pieces = lax.all_to_all(half, CHIPS, 0, 0, tiled=True)  11.8 us
    all_to_all x1, waiting for transfers between devices, on_device(): shares = lax.all_to_all(share, ('core',) + BASIS, 0, 0, tiled=True)  10.5 us
    all_to_all x1, starting transfers between devices, on_device(): lax.all_to_all(copies, CHIPS, 0, 0, tiled=True)  9.4 us
    ppermute x1, starting transfers between devices, chip_half(): lax.ppermute(lax.dynamic_slice_in_dim(store, (1 - core) * step, inside, 0...  8.77 us
    all_to_all x1, waiting for transfers between devices, on_device(): pieces = lax.all_to_all(half, CHIPS, 0, 0, tiled=True)  7.1 us
    dot_general x1, matrix products, chip_half(): jnp.einsum('ckdz,ckdq->czq', local_dipole, picked, preferred_element_type...  3.21 us
  transfers between devices with their start and end apart: 7, of which 6 were waited for; matrix products, arithmetic and copies ran while one was open for 4% of the time, Pallas kernels for 0%

profile of v2, /device:TPU:1, one launch (start us, length us, event | category | flops | bytes accessed | tf_op | source)
XLA Modules:
  0.0 141.8 jit_solution(4761233185765374233)
XLA Ops:
  0.6 0.0 copy-start
  0.6 0.0 copy-start.3
  0.7 2.1 %constant_dynamic-slice_fusion.5 = (bf16[1792,128]{1,0:T(8,128)(2,1)}, bf16[1792,128]{1,0:T(8,128)(2,1)S(1)}) fusion(bf16[3072,128]{1,0:T(8,128)(2,1)} %param.8, s32[]{:T(128)S(6)} %select_n.91, s32[]{:T(128)S(6)} %select_n.92), kind=kLoop, calls=%fused_computation.34 | loop fusion | bytes 1835016 | tf_op jit(solution)/shard_map/dynamic_slice | solution.py:46
  2.8 8.8 %collective-permute-start = (bf16[1792,128]{1,0:T(8,128)(2,1)S(1)}, bf16[1792,128]{1,0:T(8,128)(2,1)S(1)}, u32[]{:S(2)}, u32[]{:S(2)}) collective-permute-start(bf16[1792,128]{1,0:T(8,128)(2,1)S(1)} %get-tuple-element.9), channel_id=1, source_target_pairs={{0,8},{8,0},{1,9},{9,1},{2,10},{10,2},{3,11},{11,3},{4,12},{12,4},... | collective-permute-start | bytes 1376264 | tf_op jit(solution)/shard_map/ppermute | solution.py:43
  11.6 0.9 constant_dynamic-slice_fusion.3
  12.5 1.3 collective-permute-start.1
  13.8 1.9 %collective-permute-start.2 = (bf16[256,128]{1,0:T(8,128)(2,1)S(1)}, bf16[256,128]{1,0:T(8,128)(2,1)S(1)}, u32[]{:S(2)}, u32[]{:S(2)}) collective-permute-start(bf16[256,128]{1,0:T(8,128)(2,1)S(1)} %get-tuple-element.11), channel_id=1, source_target_pairs={{8,1},{9,2},{10,3},{11,4},{12,5},{13,6},{14,7},{1,8},{2,9},{3,10},... | collective-permute-start | bytes 196616 | tf_op jit(solution)/shard_map/ppermute | solution.py:39
  15.7 0.0 copy-done.3
  15.7 0.1 compare_select_fusion
  15.8 0.1 copy.12
  15.9 0.1 reshape.30
  16.0 1.5 %collective-permute-done.1 = bf16[256,128]{1,0:T(8,128)(2,1)S(1)} collective-permute-done((bf16[256,128]{1,0:T(8,128)(2,1)S(1)}, bf16[256,128]{1,0:T(8,128)(2,1)S(1)}, u32[]{:S(2)}, u32[]{:S(2)}) %collective-permute-start.1) | collective-permute-done | bytes 65568 | tf_op jit(solution)/shard_map/ppermute | solution.py:36
  17.5 1.9 %collective-permute-done.2 = bf16[256,128]{1,0:T(8,128)(2,1)S(1)} collective-permute-done((bf16[256,128]{1,0:T(8,128)(2,1)S(1)}, bf16[256,128]{1,0:T(8,128)(2,1)S(1)}, u32[]{:S(2)}, u32[]{:S(2)}) %collective-permute-start.2) | collective-permute-done | bytes 65568 | tf_op jit(solution)/shard_map/ppermute | solution.py:39
  19.4 0.0 collective-permute-done
  19.4 0.0 copy-start.1
  19.4 0.8 copy-done.1
  20.1 1.3 maximum_maximum_fusion
  21.4 2.3 %gather_fusion = bf16[36,128,256]{2,1,0:T(8,128)(2,1)} fusion(bf16[16,128,256]{2,1,0:T(8,128)(2,1)S(1)} %bitcast.26, s32[1024]{0:T(1024)S(1)} %pad_clamp_fusion), kind=kCustom, calls=%fused_computation | custom fusion | bytes 4718736 | tf_op jit(solution)/shard_map/gather | solution.py:55
  23.7 0.0 copy-done
  23.7 0.0 copy-start.6
  23.7 3.2 %bitcast_convert_fusion = bf16[12,128,256]{2,1,0:T(8,128)(2,1)} fusion(bf16[12,3,128,256]{3,2,1,0:T(8,128)(2,1)} %bitcast.27, bf16[24,3,128,128]{3,2,1,0:T(8,128)(2,1)S(1)} %copy-done, s32[]{:T(128)S(6)} %select_n.90), kind=kOutput, calls=%fused_computation.5 | convolution fusion | flops 302383104 | bytes 4325380 | tf_op jit(solution)/shard_map/ckdz,ckdq->czq/dot_general | solution.py:56
  26.9 11.8 %all-to-all-start = ((bf16[32,48,256]{2,1,0:T(8,128)(2,1)}), bf16[32,48,256]{2,1,0:T(8,128)(2,1)S(1)}, u32[]{:S(2)}, u32[]{:S(2)}) async-start(bf16[32,48,256]{2,1,0:T(8,128)(2,1)} %bitcast.4), calls=%async_computation | async-start | bytes 1572864 | tf_op jit(solution)/shard_map/all_to_all | solution.py:67
  38.8 0.0 copy-done.6
  38.8 0.7 fusion.21
  54.6 7.1 %all-to-all-done = bf16[32,48,256]{2,1,0:T(8,128)(2,1)S(1)} async-done(((bf16[32,48,256]{2,1,0:T(8,128)(2,1)}), bf16[32,48,256]{2,1,0:T(8,128)(2,1)S(1)}, u32[]{:S(2)}, u32[]{:S(2)}) %all-to-all-start) | async-done | bytes 786464 | tf_op jit(solution)/shard_map/all_to_all | solution.py:67
  61.7 0.1 dynamic-slice_bitcast_fusion.3
  61.9 1.3 broadcast_in_dim.12
  63.2 9.4 %all-to-all-start.1 = ((bf16[32,48,512]{2,1,0:T(8,128)(2,1)}), bf16[32,48,512]{2,1,0:T(8,128)(2,1)}, u32[]{:S(2)}, u32[]{:S(2)}) async-start(bf16[32,48,512]{2,1,0:T(8,128)(2,1)} %broadcast_in_dim.12), calls=%async_computation.1 | async-start | bytes 3145728 | tf_op jit(solution)/shard_map/all_to_all | solution.py:86
  72.6 1.2 constant_dynamic-slice_fusion
  73.8 1.9 %collective-permute-start.3 = (bf16[1536,256]{1,0:T(8,128)(2,1)S(1)}, bf16[1536,256]{1,0:T(8,128)(2,1)}, u32[]{:S(2)}, u32[]{:S(2)}) collective-permute-start(bf16[1536,256]{1,0:T(8,128)(2,1)S(1)} %constant_dynamic-slice_fusion), channel_id=1, source_target_pairs={{0,8},{8,0},{1,9},{9,1},{2,10},{10,2},{3,11},{11,3},{4,12},{12,4},... | collective-permute-start | bytes 2359304 | tf_op jit(solution)/shard_map/ppermute | solution.py:72
  75.7 2.4 %collective-permute-done.3 = bf16[1536,256]{1,0:T(8,128)(2,1)} collective-permute-done((bf16[1536,256]{1,0:T(8,128)(2,1)S(1)}, bf16[1536,256]{1,0:T(8,128)(2,1)}, u32[]{:S(2)}, u32[]{:S(2)}) %collective-permute-start.3) | collective-permute-done | bytes 786464 | tf_op jit(solution)/shard_map/ppermute | solution.py:72
  78.1 2.6 %broadcast_select_fusion.1 = (bf16[1536,256]{1,0:T(8,128)(2,1)S(1)}, bf16[1536,256]{1,0:T(8,128)(2,1)}) fusion(bf16[1536,256]{1,0:T(8,128)(2,1)} %collective-permute-done.3, pred[]{:T(512)S(6)} %eq.16, bf16[3072,256]{1,0:T(8,128)(2,1)} %param.7, s32[]{:T(128)S(6)} %select_n.111), kind=kLoop, calls=%fused_computation.11 | loop fusion | flops 786432 | bytes 3145733 | tf_op jit(solution)/shard_map/jit(_where)/select_n | solution.py:74
  80.7 31.8 %all-to-all-done.1 = bf16[32,48,512]{2,1,0:T(8,128)(2,1)} async-done(((bf16[32,48,512]{2,1,0:T(8,128)(2,1)}), bf16[32,48,512]{2,1,0:T(8,128)(2,1)}, u32[]{:S(2)}, u32[]{:S(2)}) %all-to-all-start.1) | async-done | bytes 1572896 | tf_op jit(solution)/shard_map/all_to_all | solution.py:86
  112.4 2.6 %fusion.4 = bf16[512,512]{1,0:T(8,128)(2,1)S(1)} fusion(bf16[1536,512]{1,0:T(8,128)(2,1)} %bitcast.17, bf16[1536,256]{1,0:T(8,128)(2,1)} %get-tuple-element.3, bf16[1536,256]{1,0:T(8,128)(2,1)S(1)} %get-tuple-element.2), kind=kOutput, calls=%fused_computation.6 | convolution fusion | flops 808714240 | bytes 3670016 | tf_op jit(solution)/shard_map/dot_general | solution.py:88
  115.0 0.0 copy-start.5
  115.0 0.0 copy-start.4
  115.1 0.8 pad_maximum_fusion
  115.9 14.5 %all-to-all-start.2 = ((bf16[16,64,256]{2,1,0:T(8,128)(2,1)}), bf16[16,64,256]{2,1,0:T(8,128)(2,1)S(1)}, u32[]{:S(2)}, u32[]{:S(2)}) async-start(bf16[16,64,256]{2,1,0:T(8,128)(2,1)} %bitcast.18), calls=%async_computation.2 | async-start | bytes 1048576 | tf_op jit(solution)/shard_map/all_to_all | solution.py:93
  130.4 0.0 copy-done.5
  130.4 10.5 %all-to-all-done.2 = bf16[16,64,256]{2,1,0:T(8,128)(2,1)S(1)} async-done(((bf16[16,64,256]{2,1,0:T(8,128)(2,1)}), bf16[16,64,256]{2,1,0:T(8,128)(2,1)S(1)}, u32[]{:S(2)}, u32[]{:S(2)}) %all-to-all-start.2) | async-done | bytes 524320 | tf_op jit(solution)/shard_map/all_to_all | solution.py:93
  141.0 0.1 convert_reduce_fusion
  141.0 0.0 copy-done.4
  141.1 0.0 copy-start.2
  141.1 0.7 fusion.9
  141.8 0.0 copy-done.2
  (5 shorter events, 0.1 us)
Async XLA Ops:
  0.6 23.1 %copy-start = (bf16[24,3,128,128]{3,2,1,0:T(8,128)(2,1)S(1)}, bf16[24,3,128,128]{3,2,1,0:T(8,128)(2,1)}, u32[]{:S(2)}) copy-start(bf16[24,3,128,128]{3,2,1,0:T(8,128)(2,1)} %param.10) | copy-start | bytes 7077892
  0.6 15.1 %copy-start.3 = (s32[24,3]{0,1:T(4,128)S(1)}, s32[24,3]{0,1:T(4,128)}, u32[]{:S(2)}) copy-start(s32[24,3]{0,1:T(4,128)} %param.11) | copy-start | bytes 868
  2.8 16.6 %collective-permute-start = (bf16[1792,128]{1,0:T(8,128)(2,1)S(1)}, bf16[1792,128]{1,0:T(8,128)(2,1)S(1)}, u32[]{:S(2)}, u32[]{:S(2)}) collective-permute-start(bf16[1792,128]{1,0:T(8,128)(2,1)S(1)} %get-tuple-element.9), channel_id=1, source_target_pairs={{0,8},{8,0},{1,9},{9,1},{2,10},{10,2},{3,11},{11,3},{4,12},{12,4},... | collective-permute-start | bytes 1376264 | tf_op jit(solution)/shard_map/ppermute | solution.py:43
  12.5 5.0 %collective-permute-start.1 = (bf16[256,128]{1,0:T(8,128)(2,1)S(1)}, bf16[256,128]{1,0:T(8,128)(2,1)S(1)}, u32[]{:S(2)}, u32[]{:S(2)}) collective-permute-start(bf16[256,128]{1,0:T(8,128)(2,1)S(1)} %get-tuple-element.10), channel_id=1, source_target_pairs={{0,1},{1,2},{2,3},{3,4},{4,5},{5,6},{6,7},{9,8},{10,9},{11,10},{12... | collective-permute-start | bytes 196616 | tf_op jit(solution)/shard_map/ppermute | solution.py:36
  13.8 5.6 %collective-permute-start.2 = (bf16[256,128]{1,0:T(8,128)(2,1)S(1)}, bf16[256,128]{1,0:T(8,128)(2,1)S(1)}, u32[]{:S(2)}, u32[]{:S(2)}) collective-permute-start(bf16[256,128]{1,0:T(8,128)(2,1)S(1)} %get-tuple-element.11), channel_id=1, source_target_pairs={{8,1},{9,2},{10,3},{11,4},{12,5},{13,6},{14,7},{1,8},{2,9},{3,10},... | collective-permute-start | bytes 196616 | tf_op jit(solution)/shard_map/ppermute | solution.py:39
  19.4 0.8 copy-start.1
  23.7 15.0 %copy-start.6 = (s32[4]{0:T(128)S(1)}, s32[4]{0:T(128)}, u32[]{:S(2)}) copy-start(s32[4]{0:T(128)} %param.9) | copy-start | bytes 52
  26.9 34.8 %all-to-all-start = ((bf16[32,48,256]{2,1,0:T(8,128)(2,1)}), bf16[32,48,256]{2,1,0:T(8,128)(2,1)S(1)}, u32[]{:S(2)}, u32[]{:S(2)}) async-start(bf16[32,48,256]{2,1,0:T(8,128)(2,1)} %bitcast.4), calls=%async_computation | async-start | bytes 1572864 | tf_op jit(solution)/shard_map/all_to_all | solution.py:67
  63.2 49.2 %all-to-all-start.1 = ((bf16[32,48,512]{2,1,0:T(8,128)(2,1)}), bf16[32,48,512]{2,1,0:T(8,128)(2,1)}, u32[]{:S(2)}, u32[]{:S(2)}) async-start(bf16[32,48,512]{2,1,0:T(8,128)(2,1)} %broadcast_in_dim.12), calls=%async_computation.1 | async-start | bytes 3145728 | tf_op jit(solution)/shard_map/all_to_all | solution.py:86
  73.8 4.3 %collective-permute-start.3 = (bf16[1536,256]{1,0:T(8,128)(2,1)S(1)}, bf16[1536,256]{1,0:T(8,128)(2,1)}, u32[]{:S(2)}, u32[]{:S(2)}) collective-permute-start(bf16[1536,256]{1,0:T(8,128)(2,1)S(1)} %constant_dynamic-slice_fusion), channel_id=1, source_target_pairs={{0,8},{8,0},{1,9},{9,1},{2,10},{10,2},{3,11},{11,3},{4,12},{12,4},... | collective-permute-start | bytes 2359304 | tf_op jit(solution)/shard_map/ppermute | solution.py:72
  115.0 15.4 %copy-start.5 = (f32[64]{0:T(128)S(1)}, f32[64]{0:T(128)}, u32[]{:S(2)}) copy-start(f32[64]{0:T(128)} %param.12) | copy-start | bytes 772
  115.0 26.0 %copy-start.4 = (f32[256]{0:T(256)S(1)}, f32[256]{0:T(256)}, u32[]{:S(2)}) copy-start(f32[256]{0:T(256)} %param.13) | copy-start | bytes 3076
  115.9 25.0 %all-to-all-start.2 = ((bf16[16,64,256]{2,1,0:T(8,128)(2,1)}), bf16[16,64,256]{2,1,0:T(8,128)(2,1)S(1)}, u32[]{:S(2)}, u32[]{:S(2)}) async-start(bf16[16,64,256]{2,1,0:T(8,128)(2,1)} %bitcast.18), calls=%async_computation.2 | async-start | bytes 1048576 | tf_op jit(solution)/shard_map/all_to_all | solution.py:93
  141.1 0.7 copy-start.2

commit v3 on v2

v3 whole, which is shorter than its diff:
```python
import functools

import jax
import jax.numpy as jnp
from jax import lax
from jax.experimental import pallas as pl
from jax.experimental.pallas import tpu as pltpu
from jax.sharding import Mesh
from jax.sharding import PartitionSpec as P

BS = 128
REACH = 2
PANELS = 4
BF16 = jnp.bfloat16
F32 = jnp.float32

SIZES = {"yhi": 4, "z": 8, "core": 2, "ylo": 2, "x": 4}
STATE = ("yhi", "z", "core")
BASIS = ("ylo", "x")
CHIPS = ("z", "yhi")
SWAP = [(0, 1), (1, 0)]

VMEM = pl.BlockSpec(memory_space=pltpu.VMEM)
HBM = pl.BlockSpec(memory_space=pltpu.HBM)
SMEM = pl.BlockSpec(memory_space=pltpu.SMEM)


def half_kernel(
    core_ref, offsets_ref, store, other, own_edge, other_edge, dipole, half, own, terms_in, near,
    own_sem, dipole_sem,
):
    nblk, terms = dipole.shape[0], dipole.shape[1]
    width = own.shape[1]
    first = core_ref[0] * (nblk // 2)
    own_copy = pltpu.make_async_copy(store, own, own_sem)
    own_copy.start()
    copies = [
        pltpu.make_async_copy(dipole.at[first + j], terms_in.at[j], dipole_sem.at[j])
        for j in range(nblk // 2)
    ]
    for copy in copies:
        copy.start()
    own_copy.wait()

    for j in range(nblk // 2):
        column = first + j
        for k in range(terms):
            block = column + offsets_ref[column, k]
            inside = (block >= 0) & (block < nblk)
            rows = pl.ds(k * BS, BS)

            @pl.when(inside)
            def _():
                source = pl.ds(pl.multiple_of(jnp.clip(block, 0, nblk - 1) * BS, BS), BS)
                near[j % 2, rows, :width] = own[source, :]
                near[j % 2, rows, width:] = other[source, :]

            @pl.when(jnp.logical_not(inside))
            def _():
                place = jnp.where(block < 0, block + REACH, block - nblk)
                source = pl.ds(pl.multiple_of(jnp.clip(place, 0, REACH - 1) * BS, BS), BS)
                near[j % 2, rows, :width] = own_edge[source, :]
                near[j % 2, rows, width:] = other_edge[source, :]

        copies[j].wait()
        half[pl.ds(j * BS, BS), :] = lax.dot_general(
            terms_in[j].reshape(terms * BS, BS),
            near[j % 2],
            (((0,), (0,)), ((), ())),
            preferred_element_type=F32,
        ).astype(BF16)


def chip_half(store, dipole, offsets, core):
    rows, width = store.shape
    reach = REACH * BS
    count = lax.axis_size(BASIS)

    def member(basis, kind):
        return basis + count * kind

    own_pairs = [(member(b, 0), member(b + 1, 0)) for b in range(count - 1)]
    own_pairs += [(member(b + 1, 1), member(b, 1)) for b in range(count - 1)]
    other_pairs = [(member(b, 1), member(b + 1, 0)) for b in range(count - 1)]
    other_pairs += [(member(b + 1, 0), member(b, 1)) for b in range(count - 1)]
    axes = ("core",) + BASIS
    low, high = store[:reach], store[rows - reach :]
    first = core == 0
    own_edge = lax.ppermute(jnp.where(first, high, low), axes, own_pairs)
    other_edge = lax.ppermute(jnp.where(first, low, high), axes, other_pairs)
    other = lax.ppermute(store, "core", SWAP)
    nblk, terms = offsets.shape
    return pl.pallas_call(
        half_kernel,
        out_shape=jax.ShapeDtypeStruct((nblk // 2 * BS, 2 * width), BF16),
        in_specs=[SMEM, SMEM, HBM, VMEM, VMEM, VMEM, HBM],
        out_specs=VMEM,
        scratch_shapes=[
            pltpu.VMEM(store.shape, BF16),
            pltpu.VMEM((nblk // 2,) + dipole.shape[1:], BF16),
            pltpu.VMEM((2, terms * BS, 2 * width), BF16),
            pltpu.SemaphoreType.DMA,
            pltpu.SemaphoreType.DMA((nblk // 2,)),
        ],
        compiler_params=pltpu.CompilerParams(vmem_limit_bytes=12 << 20),
        cost_estimate=pl.CostEstimate(
            flops=nblk * terms * BS * BS * 2 * width, bytes_accessed=6 << 20, transcendentals=0
        ),
    )(core.reshape(1), offsets, store, other, own_edge, other_edge, dipole)


def pick_kernel(core_ref, owners_ref, pieces, along, copies, chunk):
    width = pieces.shape[2] // 2
    split = along.shape[0]
    for p in range(PANELS):
        owner = owners_ref[p]
        chip = (owner // 2) % SIZES["z"] * SIZES["yhi"] + owner // (2 * SIZES["z"])
        piece = pieces[chip]
        mine = owner % 2 == core_ref[0]
        chunk[:, pl.ds(p * width, width)] = jnp.where(mine, piece[:, :width], piece[:, width:])
    along[...] = chunk[:split]
    for i in range(copies.shape[0]):
        copies[i] = chunk[split:]


def on_device(upper_coef, store, owners, dipole, offsets, lower_energy, upper_energy):
    core = lax.axis_index("core")
    width = store.shape[1]
    half = chip_half(store, dipole, offsets, core)
    nz, ny = SIZES["z"], SIZES["yhi"]
    rows = half.shape[0]
    piece = rows // (nz * ny)
    split = piece // 2

    pieces = lax.all_to_all(half, CHIPS, 0, 0, tiled=True).reshape(nz * ny, piece, 2 * width)

    lowers = PANELS * width
    along, copies = pl.pallas_call(
        pick_kernel,
        out_shape=(
            jax.ShapeDtypeStruct((split, lowers), BF16),
            jax.ShapeDtypeStruct((nz, piece - split, lowers), BF16),
        ),
        in_specs=[SMEM, SMEM, VMEM],
        out_specs=(VMEM, VMEM),
        scratch_shapes=[pltpu.VMEM((piece, lowers), BF16)],
        compiler_params=pltpu.CompilerParams(vmem_limit_bytes=8 << 20),
        cost_estimate=pl.CostEstimate(flops=0, bytes_accessed=1 << 20, transcendentals=0),
    )(core.reshape(1), owners, pieces)

    b = lax.all_to_all(copies.reshape(-1, lowers), "z", 0, 0, tiled=True)
    a = lax.all_gather(along, "yhi", axis=0, tiled=True)
    a, b = lax.optimization_barrier((a, b))
    b = jnp.broadcast_to(b[None], (ny,) + b.shape).reshape(-1, lowers)
    b = lax.all_to_all(b, "yhi", 0, 0, tiled=True)
    a = lax.all_gather(a, "z", axis=0, tiled=True)

    sent = lax.dynamic_slice_in_dim(upper_coef, (1 - core) * rows, rows, 0)
    kept = lax.dynamic_slice_in_dim(upper_coef, core * rows, rows, 0)
    got = lax.ppermute(sent, "core", SWAP)
    first = core == 0
    upper = jnp.concatenate([jnp.where(first, kept, got), jnp.where(first, got, kept)], 1)
    uppers = upper_coef.shape[1]
    upper = upper.reshape(nz, ny, piece, 2 * uppers)
    upper_a = upper[:, :, :split].reshape(-1, 2 * uppers)
    upper_b = jnp.swapaxes(upper[:, :, split:], 0, 1).reshape(-1, 2 * uppers)
    dot = functools.partial(
        lax.dot_general,
        dimension_numbers=(((0,), (0,)), ((), ())),
        preferred_element_type=F32,
    )
    share = (dot(a, upper_a) + dot(b, upper_b)).astype(BF16)
    share = jnp.concatenate([share[:, :uppers], share[:, uppers:]], 0)
    shares = lax.all_to_all(share, ("core",) + BASIS, 0, 0, tiled=True)
    shares = shares.reshape(2 * lax.axis_size(BASIS), -1, uppers)
    moments = jnp.sum(shares.astype(F32), axis=0)
    nu = upper_energy[None, :] - lower_energy[:, None]
    intensity = moments * moments * nu * jnp.exp(-lower_energy)[:, None] * (1.0 - jnp.exp(-nu))
    return moments, intensity


def solution(mesh):
    fine = Mesh(mesh.devices.reshape(tuple(SIZES.values())), tuple(SIZES))
    placed = (
        P(BASIS, STATE),
        P(BASIS, STATE),
        P(),
        P(BASIS, None, None, None),
        P(BASIS, None),
        P(BASIS),
        P(STATE),
    )
    return jax.shard_map(
        on_device,
        mesh=fine,
        in_specs=placed,
        out_specs=(P(BASIS, STATE), P(BASIS, STATE)),
        check_vma=False,
    )
```

time: 143 us -> 138 us (0.965)
  blocking collectives: 0 us -> 35.9 us
  waiting for transfers between devices: 55.1 us -> 34.4 us
  between operations: 16 us -> 0.83 us
  Pallas kernels: 0 us -> 8.26 us
  local copies, waits for them, and re-layouts: 9.67 us -> 4.84 us
  matrix products: 5.82 us -> 1.19 us
  starting transfers between devices: 49.6 us -> 47.1 us
    all_gather x0 -> x2, blocking collectives: none -> 35.9 us  [the longest x1 22.6 us: on_device(): a = lax.all_gather(a, 'z', axis=0, tiled=True)]
    all_to_all x2 -> x3, waiting for transfers between devices: 38.9 us -> 21 us  [the longest x1 21 us: on_device(): lax.all_to_all(half, CHIPS, 0, 0, tiled=True)]
    pallas_call x0 -> x2, Pallas kernels: none -> 8.26 us  [the longest x1 6.98 us: chip_half(): pl.pallas_call(half_kernel, out_shape=jax.ShapeDtypeStruct((nblk // 2 * B...]
    dot_general x2, matrix products: 5.82 us -> 1.19 us  [on_device(): share = (dot(a, upper_a) + dot(b, upper_b)).astype(BF16)]
    dynamic_slice x2 -> x0, local copies, waits for them, and re-layouts: 3.03 us -> none  [the longest x1 2.14 us: chip_half(): own = lax.dynamic_slice_in_dim(store, core * step, inside, 0)]
    ppermute x4, waiting for transfers between devices: 5.74 us -> 2.9 us  [the longest x1 1.87 us: chip_half(): other_edge = lax.ppermute(jnp.where(first, low, high), axes, other_pairs)]
    unnamed x14 -> x15, local copies, waits for them, and re-layouts: 0.81 us -> 3.59 us
    gather x1 -> x0, local copies, waits for them, and re-layouts: 2.31 us -> none  [chip_half(): picked = blocks[place % nblocks]]
  transfers between devices with their start and end apart: 7 -> 8, of which waited for: 6 -> 4; matrix products, arithmetic and copies ran while one was open for 4% -> 3% of each run, Pallas kernels for 0% -> 1%
where the time goes in v3:
time: 138 us; the launch traced here: 137 us
  starting transfers between devices  47.1 us (34%)
  blocking collectives  35.9 us (26%)
  waiting for transfers between devices  34.4 us (25%)
  Pallas kernels  8.26 us (6%)
  local copies, waits for them, and re-layouts  4.84 us (4%)
  other arithmetic  4.32 us (3%)
    all_gather x1, blocking collectives, on_device(): a = lax.all_gather(a, 'z', axis=0, tiled=True)  22.6 us
    all_to_all x1, waiting for transfers between devices, on_device(): lax.all_to_all(half, CHIPS, 0, 0, tiled=True)  21 us
    all_gather x1, blocking collectives, on_device(): a = lax.all_gather(along, 'yhi', axis=0, tiled=True)  13.3 us
    all_to_all x1, starting transfers between devices, on_device(): shares = lax.all_to_all(share, ('core',) + BASIS, 0, 0, tiled=True)  12.6 us
    all_to_all x1, starting transfers between devices, on_device(): lax.all_to_all(half, CHIPS, 0, 0, tiled=True)  11.9 us
    all_to_all x1, waiting for transfers between devices, on_device(): shares = lax.all_to_all(share, ('core',) + BASIS, 0, 0, tiled=True)  10.5 us
    ppermute x1, starting transfers between devices, chip_half(): other = lax.ppermute(store, 'core', SWAP)  8.79 us
    pallas_call x1, Pallas kernels, chip_half(): pl.pallas_call(half_kernel, out_shape=jax.ShapeDtypeStruct((nblk // 2 * B...  6.98 us
  transfers between devices with their start and end apart: 8, of which 4 were waited for; matrix products, arithmetic and copies ran while one was open for 3% of the time, Pallas kernels for 1%

profile of v3, /device:TPU:1, one launch (start us, length us, event | category | flops | bytes accessed | tf_op | source)
XLA Modules:
  0.0 136.9 jit_solution(48733830750431731)
XLA Ops:
  0.6 8.8 %collective-permute-start = (bf16[3072,128]{1,0:T(8,128)(2,1)}, bf16[3072,128]{1,0:T(8,128)(2,1)S(1)}, u32[]{:S(2)}, u32[]{:S(2)}) collective-permute-start(bf16[3072,128]{1,0:T(8,128)(2,1)} %store.1), channel_id=1, source_target_pairs={{0,8},{8,0},{1,9},{9,1},{2,10},{10,2},{3,11},{11,3},{4,12},{12,4},... | collective-permute-start | bytes 2359304 | tf_op jit(solution)/shard_map/ppermute | solution.py:91
  9.4 0.9 broadcast_select_fusion.2
  10.3 1.3 collective-permute-start.1
  11.6 1.9 %collective-permute-start.2 = (bf16[256,128]{1,0:T(8,128)(2,1)S(1)}, bf16[256,128]{1,0:T(8,128)(2,1)S(1)}, u32[]{:S(2)}, u32[]{:S(2)}) collective-permute-start(bf16[256,128]{1,0:T(8,128)(2,1)S(1)} %get-tuple-element.14), channel_id=1, source_target_pairs={{8,1},{9,2},{10,3},{11,4},{12,5},{13,6},{14,7},{1,8},{2,9},{3,10},... | collective-permute-start | bytes 196616 | tf_op jit(solution)/shard_map/ppermute | solution.py:90
  13.6 0.8 copy.11.offsets_ref
  14.3 1.0 collective-permute-done.1.own_edge
  15.3 1.9 %collective-permute-done.2.other_edge = bf16[256,128]{1,0:T(8,128)(2,1)S(1)} collective-permute-done((bf16[256,128]{1,0:T(8,128)(2,1)S(1)}, bf16[256,128]{1,0:T(8,128)(2,1)S(1)}, u32[]{:S(2)}, u32[]{:S(2)}) %collective-permute-start.2) | collective-permute-done | bytes 65568 | tf_op jit(solution)/shard_map/ppermute | solution.py:90
  17.2 0.0 collective-permute-done.other
  17.2 0.0 copy-start
  17.2 1.7 %copy-done = bf16[24,3,128,128]{3,2,1,0:T(8,128)(2,1)S(1)} copy-done((bf16[24,3,128,128]{3,2,1,0:T(8,128)(2,1)S(1)}, bf16[24,3,128,128]{3,2,1,0:T(8,128)(2,1)}, u32[]{:S(2)}) %copy-start) | copy-done | bytes 2359320
  18.9 0.0 copy-start.1
  18.9 1.1 copy-done.1
  20.0 7.0 %shard_map.86 = bf16[1536,256]{1,0:T(8,128)(2,1)} custom-call(s32[1]{0:T(128)} %bitcast.core_ref, s32[24,3]{1,0:T(8,128)S(1)} %copy.11.offsets_ref, bf16[3072,128]{1,0:T(8,128)(2,1)S(1)} %copy-done.1, bf16[3072,128]{1,0:T(8,128)(2,1)S(1)} %collective-permute-done.other, bf16[256,128]{1,0:T(8,128)(2,1)S(1)} %collective-permute-done.1.own_edge, ...), custom_call_target="tpu_custom_call" | custom-call | flops 301989888 | bytes 6291456 | tf_op jit(solution)/shard_map/pallas_call | solution.py:93
  27.0 0.0 copy-start.3
  27.0 0.0 copy-start.2
  27.0 11.9 %all-to-all-start = ((bf16[32,48,256]{2,1,0:T(8,128)(2,1)}), bf16[32,48,256]{2,1,0:T(8,128)(2,1)S(1)}, u32[]{:S(2)}, u32[]{:S(2)}) async-start(bf16[32,48,256]{2,1,0:T(8,128)(2,1)} %bitcast.1), calls=%async_computation | async-start | bytes 1572864 | tf_op jit(solution)/shard_map/all_to_all | solution.py:135
  39.0 0.0 copy-done.3
  39.0 0.1 constant_dynamic-slice_fusion
  39.0 1.9 %collective-permute-start.3 = (bf16[1536,256]{1,0:T(8,128)(2,1)S(1)}, bf16[1536,256]{1,0:T(8,128)(2,1)}, u32[]{:S(2)}, u32[]{:S(2)}) collective-permute-start(bf16[1536,256]{1,0:T(8,128)(2,1)S(1)} %constant_dynamic-slice_fusion), channel_id=1, source_target_pairs={{0,8},{8,0},{1,9},{9,1},{2,10},{10,2},{3,11},{11,3},{4,12},{12,4},... | collective-permute-start | bytes 2359304 | tf_op jit(solution)/shard_map/ppermute | solution.py:160
  41.0 21.0 %all-to-all-done.pieces = bf16[32,48,256]{2,1,0:T(8,128)(2,1)S(1)} async-done(((bf16[32,48,256]{2,1,0:T(8,128)(2,1)}), bf16[32,48,256]{2,1,0:T(8,128)(2,1)S(1)}, u32[]{:S(2)}, u32[]{:S(2)}) %all-to-all-start) | async-done | bytes 786464 | tf_op jit(solution)/shard_map/all_to_all | solution.py:135
  61.9 0.0 copy-done.2
  61.9 1.3 shard_map.87
  63.2 4.3 %all-to-all-start.1 = ((bf16[8,24,512]{2,1,0:T(8,128)(2,1)}), bf16[8,24,512]{2,1,0:T(8,128)(2,1)S(1)}, u32[]{:S(2)}, u32[]{:S(2)}) async-start(bf16[8,24,512]{2,1,0:T(8,128)(2,1)} %get-tuple-element.7), calls=%async_computation.1 | async-start | bytes 393216 | tf_op jit(solution)/shard_map/all_to_all | solution.py:151
  67.6 0.0 collective-permute-done.3
  67.6 1.7 %broadcast_select_fusion.1 = (bf16[1536,256]{1,0:T(8,128)(2,1)S(1)}, bf16[1536,256]{1,0:T(8,128)(2,1)S(1)}) fusion(bf16[1536,256]{1,0:T(8,128)(2,1)} %collective-permute-done.3, pred[]{:T(512)S(6)} %eq.4, bf16[3072,256]{1,0:T(8,128)(2,1)} %param.7, s32[]{:T(128)S(6)} %select_n.34), kind=kLoop, calls=%fused_computation.6 | loop fusion | flops 786432 | bytes 3145733 | tf_op jit(solution)/shard_map/jit(_where)/select_n | solution.py:162
  69.2 13.3 %all_gather.6 = bf16[96,512]{1,0:T(8,128)(2,1)S(1)} all-gather(bf16[24,512]{1,0:T(8,128)(2,1)S(1)} %get-tuple-element.6), channel_id=1, replica_groups=mesh['yhi'=4,'z'=8,'core'=2,'ylo'=2,'x'=4] {'yhi'}, dimensions={0}, use_global_device_ids=true | all-gather | bytes 122880 | tf_op jit(solution)/shard_map/all_gather | solution.py:152
  82.5 0.0 all-to-all-done.1
  82.5 0.9 broadcast_in_dim.2
  83.5 4.4 %all-to-all-start.2 = ((bf16[4,192,512]{2,1,0:T(8,128)(2,1)}), bf16[4,192,512]{2,1,0:T(8,128)(2,1)S(1)}, u32[]{:S(2)}, u32[]{:S(2)}) async-start(bf16[4,192,512]{2,1,0:T(8,128)(2,1)} %broadcast_in_dim.2), calls=%async_computation.2 | async-start | bytes 1572864 | tf_op jit(solution)/shard_map/all_to_all | solution.py:155
  87.8 0.1 pad_maximum_fusion
  88.0 0.2 slice_bitcast_fusion
  88.1 0.1 copy.12
  88.2 22.6 %all_gather.7 = bf16[768,512]{1,0:T(8,128)(2,1)S(1)} all-gather(bf16[96,512]{1,0:T(8,128)(2,1)S(1)} %all_gather.6), channel_id=1, replica_groups=mesh['yhi'=4,'z'=8,'core'=2,'ylo'=2,'x'=4] {'z'}, dimensions={0}, use_global_device_ids=true | all-gather | bytes 884736 | tf_op jit(solution)/shard_map/all_gather | solution.py:156
  110.8 0.6 fusion.6
  111.4 0.0 all-to-all-done.2
  111.4 0.6 fusion
  112.0 0.0 copy-start.6
  112.1 0.0 copy-start.5
  112.1 0.8 pad_maximum_fusion.1
  112.9 12.6 %all-to-all-start.3 = ((bf16[16,64,256]{2,1,0:T(8,128)(2,1)}), bf16[16,64,256]{2,1,0:T(8,128)(2,1)S(1)}, u32[]{:S(2)}, u32[]{:S(2)}) async-start(bf16[16,64,256]{2,1,0:T(8,128)(2,1)} %bitcast.8), calls=%async_computation.3 | async-start | bytes 1048576 | tf_op jit(solution)/shard_map/all_to_all | solution.py:174
  125.5 0.0 copy-done.6
  125.5 10.5 %all-to-all-done.3 = bf16[16,64,256]{2,1,0:T(8,128)(2,1)S(1)} async-done(((bf16[16,64,256]{2,1,0:T(8,128)(2,1)}), bf16[16,64,256]{2,1,0:T(8,128)(2,1)S(1)}, u32[]{:S(2)}, u32[]{:S(2)}) %all-to-all-start.3) | async-done | bytes 524320 | tf_op jit(solution)/shard_map/all_to_all | solution.py:174
  136.0 0.1 convert_reduce_fusion
  136.1 0.0 copy-done.5
  136.1 0.0 copy-start.4
  136.1 0.7 fusion.2
  136.8 0.0 copy-done.4
  (2 shorter events, 0.0 us)
Async XLA Ops:
  0.6 16.6 %collective-permute-start = (bf16[3072,128]{1,0:T(8,128)(2,1)}, bf16[3072,128]{1,0:T(8,128)(2,1)S(1)}, u32[]{:S(2)}, u32[]{:S(2)}) collective-permute-start(bf16[3072,128]{1,0:T(8,128)(2,1)} %store.1), channel_id=1, source_target_pairs={{0,8},{8,0},{1,9},{9,1},{2,10},{10,2},{3,11},{11,3},{4,12},{12,4},... | collective-permute-start | bytes 2359304 | tf_op jit(solution)/shard_map/ppermute | solution.py:91
  10.3 5.0 %collective-permute-start.1 = (bf16[256,128]{1,0:T(8,128)(2,1)S(1)}, bf16[256,128]{1,0:T(8,128)(2,1)S(1)}, u32[]{:S(2)}, u32[]{:S(2)}) collective-permute-start(bf16[256,128]{1,0:T(8,128)(2,1)S(1)} %get-tuple-element.15), channel_id=1, source_target_pairs={{0,1},{1,2},{2,3},{3,4},{4,5},{5,6},{6,7},{9,8},{10,9},{11,10},{12... | collective-permute-start | bytes 196616 | tf_op jit(solution)/shard_map/ppermute | solution.py:89
  11.6 5.6 %collective-permute-start.2 = (bf16[256,128]{1,0:T(8,128)(2,1)S(1)}, bf16[256,128]{1,0:T(8,128)(2,1)S(1)}, u32[]{:S(2)}, u32[]{:S(2)}) collective-permute-start(bf16[256,128]{1,0:T(8,128)(2,1)S(1)} %get-tuple-element.14), channel_id=1, source_target_pairs={{8,1},{9,2},{10,3},{11,4},{12,5},{13,6},{14,7},{1,8},{2,9},{3,10},... | collective-permute-start | bytes 196616 | tf_op jit(solution)/shard_map/ppermute | solution.py:90
  17.2 1.7 %copy-start = (bf16[24,3,128,128]{3,2,1,0:T(8,128)(2,1)S(1)}, bf16[24,3,128,128]{3,2,1,0:T(8,128)(2,1)}, u32[]{:S(2)}) copy-start(bf16[24,3,128,128]{3,2,1,0:T(8,128)(2,1)} %dipole.1) | copy-start | bytes 7077892
  18.9 1.1 copy-start.1
  27.0 12.0 %copy-start.3 = (bf16[3072,256]{1,0:T(8,128)(2,1)S(1)}, bf16[3072,256]{1,0:T(8,128)(2,1)}, u32[]{:S(2)}) copy-start(bf16[3072,256]{1,0:T(8,128)(2,1)} %param.7) | copy-start | bytes 4718596
  27.0 34.9 %copy-start.2 = (s32[4]{0:T(128)S(1)}, s32[4]{0:T(128)}, u32[]{:S(2)}) copy-start(s32[4]{0:T(128)} %owners_ref.1) | copy-start | bytes 52
  27.0 34.9 %all-to-all-start = ((bf16[32,48,256]{2,1,0:T(8,128)(2,1)}), bf16[32,48,256]{2,1,0:T(8,128)(2,1)S(1)}, u32[]{:S(2)}, u32[]{:S(2)}) async-start(bf16[32,48,256]{2,1,0:T(8,128)(2,1)} %bitcast.1), calls=%async_computation | async-start | bytes 1572864 | tf_op jit(solution)/shard_map/all_to_all | solution.py:135
  39.0 28.5 %collective-permute-start.3 = (bf16[1536,256]{1,0:T(8,128)(2,1)S(1)}, bf16[1536,256]{1,0:T(8,128)(2,1)}, u32[]{:S(2)}, u32[]{:S(2)}) collective-permute-start(bf16[1536,256]{1,0:T(8,128)(2,1)S(1)} %constant_dynamic-slice_fusion), channel_id=1, source_target_pairs={{0,8},{8,0},{1,9},{9,1},{2,10},{10,2},{3,11},{11,3},{4,12},{12,4},... | collective-permute-start | bytes 2359304 | tf_op jit(solution)/shard_map/ppermute | solution.py:160
  63.2 19.3 %all-to-all-start.1 = ((bf16[8,24,512]{2,1,0:T(8,128)(2,1)}), bf16[8,24,512]{2,1,0:T(8,128)(2,1)S(1)}, u32[]{:S(2)}, u32[]{:S(2)}) async-start(bf16[8,24,512]{2,1,0:T(8,128)(2,1)} %get-tuple-element.7), calls=%async_computation.1 | async-start | bytes 393216 | tf_op jit(solution)/shard_map/all_to_all | solution.py:151
  83.5 27.9 %all-to-all-start.2 = ((bf16[4,192,512]{2,1,0:T(8,128)(2,1)}), bf16[4,192,512]{2,1,0:T(8,128)(2,1)S(1)}, u32[]{:S(2)}, u32[]{:S(2)}) async-start(bf16[4,192,512]{2,1,0:T(8,128)(2,1)} %broadcast_in_dim.2), calls=%async_computation.2 | async-start | bytes 1572864 | tf_op jit(solution)/shard_map/all_to_all | solution.py:155
  112.0 13.5 %copy-start.6 = (f32[64]{0:T(128)S(1)}, f32[64]{0:T(128)}, u32[]{:S(2)}) copy-start(f32[64]{0:T(128)} %param.12) | copy-start | bytes 772
  112.1 24.0 %copy-start.5 = (f32[256]{0:T(256)S(1)}, f32[256]{0:T(256)}, u32[]{:S(2)}) copy-start(f32[256]{0:T(256)} %param.13) | copy-start | bytes 3076
  112.9 23.1 %all-to-all-start.3 = ((bf16[16,64,256]{2,1,0:T(8,128)(2,1)}), bf16[16,64,256]{2,1,0:T(8,128)(2,1)S(1)}, u32[]{:S(2)}, u32[]{:S(2)}) async-start(bf16[16,64,256]{2,1,0:T(8,128)(2,1)} %bitcast.8), calls=%async_computation.3 | async-start | bytes 1048576 | tf_op jit(solution)/shard_map/all_to_all | solution.py:174
  136.1 0.7 copy-start.4

commit v4 on v3

v4 whole, which is shorter than its diff:
```python
import jax
import jax.numpy as jnp
from jax import lax
from jax.experimental import pallas as pl
from jax.experimental.pallas import tpu as pltpu
from jax.sharding import Mesh
from jax.sharding import PartitionSpec as P

BS = 128
REACH = 2
PANELS = 4
BF16 = jnp.bfloat16
F32 = jnp.float32

SIZES = {"yhi": 4, "zhi": 4, "zlo": 2, "core": 2, "ylo": 2, "x": 4}
STATE = ("yhi", "zhi", "zlo", "core")
BASIS = ("ylo", "x")
SHARED = ("core", "zlo")
GATHER = ("zhi", "yhi")
CHIPS = ("zlo",) + GATHER
SWAP = [(0, 1), (1, 0)]

VMEM = pl.BlockSpec(memory_space=pltpu.VMEM)
HBM = pl.BlockSpec(memory_space=pltpu.HBM)
SMEM = pl.BlockSpec(memory_space=pltpu.SMEM)


def half_kernel(
    core_ref, offsets_ref, store, other, own_edge, other_edge, dipole, half, near, terms_in,
    near_sem, dipole_sem,
):
    nblk, terms = dipole.shape[0], dipole.shape[1]
    rows, width = store.shape
    reach = REACH * BS
    core = core_ref[0]
    first = core * (nblk // 2)
    edge = pl.ds(pl.multiple_of(core * (reach + rows), BS), reach)
    middle = pl.ds(reach, rows)
    left, right = pl.ds(0, width), pl.ds(width, width)
    fills = [
        pltpu.make_async_copy(source, near.at[place, lanes], near_sem.at[i])
        for i, (source, place, lanes) in enumerate(
            [
                (store, middle, left),
                (other, middle, right),
                (own_edge, edge, left),
                (other_edge, edge, right),
            ]
        )
    ]
    copies = [
        pltpu.make_async_copy(dipole.at[first + j], terms_in.at[j], dipole_sem.at[j])
        for j in range(nblk // 2)
    ]
    for copy in fills + copies:
        copy.start()
    for copy in fills:
        copy.wait()

    for j in range(nblk // 2):
        column = first + j
        blocks = []
        for k in range(terms):
            block = column + offsets_ref[column, k] + REACH
            blocks.append(near[pl.ds(pl.multiple_of(block * BS, BS), BS), :])
        copies[j].wait()
        half[pl.ds(j * BS, BS), :] = lax.dot_general(
            terms_in[j].reshape(terms * BS, BS),
            jnp.concatenate(blocks, axis=0),
            (((0,), (0,)), ((), ())),
            preferred_element_type=F32,
        ).astype(BF16)


def chip_half(store, dipole, offsets, core):
    rows, width = store.shape
    reach = REACH * BS
    count = lax.axis_size(BASIS)

    def member(basis, kind):
        return basis + count * kind

    own_pairs = [(member(b, 0), member(b + 1, 0)) for b in range(count - 1)]
    own_pairs += [(member(b + 1, 1), member(b, 1)) for b in range(count - 1)]
    other_pairs = [(member(b, 1), member(b + 1, 0)) for b in range(count - 1)]
    other_pairs += [(member(b + 1, 0), member(b, 1)) for b in range(count - 1)]
    axes = ("core",) + BASIS
    low, high = store[:reach], store[rows - reach :]
    first = core == 0
    own_edge = lax.ppermute(jnp.where(first, high, low), axes, own_pairs)
    other_edge = lax.ppermute(jnp.where(first, low, high), axes, other_pairs)
    other = lax.ppermute(store, "core", SWAP)
    nblk, terms = offsets.shape
    return pl.pallas_call(
        half_kernel,
        out_shape=jax.ShapeDtypeStruct((nblk // 2 * BS, 2 * width), BF16),
        in_specs=[SMEM, SMEM, HBM, HBM, HBM, HBM, HBM],
        out_specs=VMEM,
        scratch_shapes=[
            pltpu.VMEM((rows + 2 * reach, 2 * width), BF16),
            pltpu.VMEM((nblk // 2,) + dipole.shape[1:], BF16),
            pltpu.SemaphoreType.DMA((4,)),
            pltpu.SemaphoreType.DMA((nblk // 2,)),
        ],
        compiler_params=pltpu.CompilerParams(vmem_limit_bytes=12 << 20),
        cost_estimate=pl.CostEstimate(
            flops=nblk * terms * BS * BS * 2 * width, bytes_accessed=6 << 20, transcendentals=0
        ),
    )(core.reshape(1), offsets, store, other, own_edge, other_edge, dipole)


def pick_kernel(core_ref, owners_ref, pieces, copies, chunk):
    width = pieces.shape[2] // 2
    for p in range(PANELS):
        owner = owners_ref[p]
        zlo, zhi, yhi = owner // 2 % 2, owner // 4 % SIZES["zhi"], owner // 16
        piece = pieces[(zlo * SIZES["zhi"] + zhi) * SIZES["yhi"] + yhi]
        mine = owner % 2 == core_ref[0]
        chunk[:, pl.ds(p * width, width)] = jnp.where(mine, piece[:, :width], piece[:, width:])
    for i in range(copies.shape[0]):
        copies[i] = chunk[...]


def on_device(upper_coef, store, owners, dipole, offsets, lower_energy, upper_energy):
    core = lax.axis_index("core")
    width = store.shape[1]
    uppers = upper_coef.shape[1]
    upper = lax.all_to_all(upper_coef, SHARED, 0, 0, tiled=True)
    upper = upper.reshape(2, 2, -1, uppers)

    half = chip_half(store, dipole, offsets, core)
    half, upper = lax.optimization_barrier((half, upper))
    chips, peers = lax.axis_size(CHIPS), lax.axis_size(GATHER)
    rows = half.shape[0] // chips
    lowers = PANELS * width
    pieces = lax.all_to_all(half, CHIPS, 0, 0, tiled=True).reshape(chips, rows, 2 * width)

    copies = pl.pallas_call(
        pick_kernel,
        out_shape=jax.ShapeDtypeStruct((peers, rows, lowers), BF16),
        in_specs=[SMEM, SMEM, VMEM],
        out_specs=VMEM,
        scratch_shapes=[pltpu.VMEM((rows, lowers), BF16)],
        compiler_params=pltpu.CompilerParams(vmem_limit_bytes=8 << 20),
        cost_estimate=pl.CostEstimate(flops=0, bytes_accessed=1 << 20, transcendentals=0),
    )(core.reshape(1), owners, pieces)
    gathered = lax.all_to_all(copies.reshape(-1, lowers), GATHER, 0, 0, tiled=True)

    def share(kind, member):
        rhs = lax.dynamic_index_in_dim(upper, kind, 0, keepdims=False)[member]
        return lax.dot_general(
            gathered, rhs, (((0,), (0,)), ((), ())), preferred_element_type=F32
        )

    received = [
        lax.ppermute(share(1 - core, m).astype(BF16), "core", SWAP) for m in range(2)
    ]
    added = [(share(core, m) + received[m].astype(F32)).astype(BF16) for m in range(2)]
    shares = lax.all_to_all(jnp.concatenate(added, 0), ("zlo",) + BASIS, 0, 0, tiled=True)
    shares = shares.reshape(2 * lax.axis_size(BASIS), -1, uppers)
    moments = jnp.sum(shares.astype(F32), axis=0)
    nu = upper_energy[None, :] - lower_energy[:, None]
    intensity = moments * moments * nu * jnp.exp(-lower_energy)[:, None] * (1.0 - jnp.exp(-nu))
    return moments, intensity


def solution(mesh):
    fine = Mesh(mesh.devices.reshape(tuple(SIZES.values())), tuple(SIZES))
    placed = (
        P(BASIS, STATE),
        P(BASIS, STATE),
        P(),
        P(BASIS, None, None, None),
        P(BASIS, None),
        P(BASIS),
        P(STATE),
    )
    return jax.shard_map(
        on_device,
        mesh=fine,
        in_specs=placed,
        out_specs=(P(BASIS, STATE), P(BASIS, STATE)),
        check_vma=False,
    )
```

time: 138 us -> 132 us (0.957)
  blocking collectives: 35.9 us -> 30 us
  waiting for transfers between devices: 34.4 us -> 39.2 us
  matrix products: 1.19 us -> 5.65 us
  local copies, waits for them, and re-layouts: 4.84 us -> 1.26 us
  other arithmetic: 4.32 us -> 1.64 us
    all_gather x2 -> x0, blocking collectives: 35.9 us -> none  [the longest x1 22.6 us: on_device(): a = lax.all_gather(a, 'z', axis=0, tiled=True)]
    all_to_all x0 -> x1, blocking collectives: none -> 30 us  [on_device(): lax.all_to_all(half, CHIPS, 0, 0, tiled=True)]
    ppermute x1, starting transfers between devices: 8.79 us -> 1.97 us  [chip_half(): other = lax.ppermute(store, 'core', SWAP)]
    ppermute x1 -> x2, starting transfers between devices: 1.92 us -> 7.96 us  [on_device(): lax.ppermute(share(1 - core, m).astype(BF16), 'core', SWAP)]
    dot_general x2 -> x4, matrix products: 1.19 us -> 5.65 us  [share(): lax.dot_general(gathered, rhs, (((0,), (0,)), ((), ())), preferred_elemen...]
    all_to_all x4 -> x3, waiting for transfers between devices: 31.5 us -> 35.2 us  [the longest x1 21.3 us: on_device(): lax.all_to_all(copies.reshape(-1, lowers), GATHER, 0, 0, tiled=True)]
    unnamed x15 -> x17, local copies, waits for them, and re-layouts: 3.59 us -> 1.26 us
    select_n x1 -> x0, other arithmetic: 1.68 us -> none  [on_device(): jnp.where(first, kept, got)]
  transfers between devices with their start and end apart: 8 -> 8, of which waited for: 4 -> 6; matrix products, arithmetic and copies ran while one was open for 3% -> 2% of each run, Pallas kernels for 1% -> 4%
where the time goes in v4:
time: 132 us
  starting transfers between devices  45.9 us (35%)
  waiting for transfers between devices  39.2 us (30%)
  blocking collectives  30 us (23%)
  Pallas kernels  7.11 us (5%)
  matrix products  5.65 us (4%)
  other arithmetic  1.64 us (1%)
    all_to_all x1, blocking collectives, on_device(): lax.all_to_all(half, CHIPS, 0, 0, tiled=True)  30 us
    all_to_all x1, waiting for transfers between devices, on_device(): lax.all_to_all(copies.reshape(-1, lowers), GATHER, 0, 0, tiled=True)  21.3 us
    all_to_all x1, starting transfers between devices, on_device(): upper = lax.all_to_all(upper_coef, SHARED, 0, 0, tiled=True)  11.5 us
    all_to_all x1, starting transfers between devices, on_device(): lax.all_to_all(jnp.concatenate(added, 0), ('zlo',) + BASIS, 0, 0, tiled=T...  11.5 us
    all_to_all x1, waiting for transfers between devices, on_device(): lax.all_to_all(jnp.concatenate(added, 0), ('zlo',) + BASIS, 0, 0, tiled=T...  10.5 us
    all_to_all x1, starting transfers between devices, on_device(): lax.all_to_all(copies.reshape(-1, lowers), GATHER, 0, 0, tiled=True)  9.86 us
    ppermute x2, starting transfers between devices, on_device(): lax.ppermute(share(1 - core, m).astype(BF16), 'core', SWAP)  7.96 us
    dot_general x4, matrix products, share(): lax.dot_general(gathered, rhs, (((0,), (0,)), ((), ())), preferred_elemen...  5.65 us
  transfers between devices with their start and end apart: 8, of which 6 were waited for; matrix products, arithmetic and copies ran while one was open for 2% of the time, Pallas kernels for 4%

profile of v4, /device:TPU:1, one launch (start us, length us, event | category | flops | bytes accessed | tf_op | source)
XLA Modules:
  0.0 131.6 jit_solution(2659730801169843827)
XLA Ops:
  0.6 0.0 copy-start.1
  0.6 0.0 copy-start.5
  0.7 0.0 copy-start
  0.7 11.5 %all-to-all-start = ((bf16[4,768,256]{2,1,0:T(8,128)(2,1)}), bf16[4,768,256]{2,1,0:T(8,128)(2,1)}, u32[]{:S(2)}, u32[]{:S(2)}) async-start(bf16[4,768,256]{2,1,0:T(8,128)(2,1)} %bitcast.27), calls=%async_computation | async-start | bytes 3145728 | tf_op jit(solution)/shard_map/all_to_all | solution.py:128
  12.1 0.0 copy-done.1
  12.1 2.0 %collective-permute-start = (bf16[3072,128]{1,0:T(8,128)(2,1)S(1)}, bf16[3072,128]{1,0:T(8,128)(2,1)}, u32[]{:S(2)}, u32[]{:S(2)}) collective-permute-start(bf16[3072,128]{1,0:T(8,128)(2,1)S(1)} %copy-done.1), channel_id=1, source_target_pairs={{0,8},{8,0},{1,9},{9,1},{2,10},{10,2},{3,11},{11,3},{4,12},{12,4},... | collective-permute-start | bytes 2359304 | tf_op jit(solution)/shard_map/ppermute | solution.py:92
  14.1 1.3 collective-permute-start.1
  15.4 1.9 %collective-permute-start.2 = (bf16[256,128]{1,0:T(8,128)(2,1)S(1)}, bf16[256,128]{1,0:T(8,128)(2,1)S(1)}, u32[]{:S(2)}, u32[]{:S(2)}) collective-permute-start(bf16[256,128]{1,0:T(8,128)(2,1)S(1)} %get-tuple-element.6), channel_id=1, source_target_pairs={{8,1},{9,2},{10,3},{11,4},{12,5},{13,6},{14,7},{1,8},{2,9},{3,10},... | collective-permute-start | bytes 196616 | tf_op jit(solution)/shard_map/ppermute | solution.py:91
  17.4 0.0 copy-done.5
  17.4 0.1 copy.9.offsets_ref
  17.5 2.1 %collective-permute-done.1.own_edge = bf16[256,128]{1,0:T(8,128)(2,1)S(1)} collective-permute-done((bf16[256,128]{1,0:T(8,128)(2,1)S(1)}, bf16[256,128]{1,0:T(8,128)(2,1)S(1)}, u32[]{:S(2)}, u32[]{:S(2)}) %collective-permute-start.1) | collective-permute-done | bytes 65568 | tf_op jit(solution)/shard_map/ppermute | solution.py:90
  19.5 1.9 %collective-permute-done.2.other_edge = bf16[256,128]{1,0:T(8,128)(2,1)S(1)} collective-permute-done((bf16[256,128]{1,0:T(8,128)(2,1)S(1)}, bf16[256,128]{1,0:T(8,128)(2,1)S(1)}, u32[]{:S(2)}, u32[]{:S(2)}) %collective-permute-start.2) | collective-permute-done | bytes 65568 | tf_op jit(solution)/shard_map/ppermute | solution.py:91
  21.4 0.0 collective-permute-done.other
  21.4 0.0 copy-done
  21.4 0.0 copy-start.2
  21.4 1.1 copy-done.2
  22.6 5.5 %shard_map.86 = bf16[1536,256]{1,0:T(8,128)(2,1)S(1)} custom-call(s32[1]{0:T(128)} %bitcast.core_ref, s32[24,3]{1,0:T(8,128)S(1)} %copy.9.offsets_ref, bf16[3072,128]{1,0:T(8,128)(2,1)S(1)} %copy-done.2, bf16[3072,128]{1,0:T(8,128)(2,1)} %collective-permute-done.other, bf16[256,128]{1,0:T(8,128)(2,1)S(1)} %collective-permute-done.1.own_edge, ...), custom_call_target="tpu_custom_call" | custom-call | flops 301989888 | bytes 6291456 | tf_op jit(solution)/shard_map/pallas_call | solution.py:94
  28.1 0.0 copy-start.3
  28.1 3.3 %all-to-all-done = bf16[4,768,256]{2,1,0:T(8,128)(2,1)} async-done(((bf16[4,768,256]{2,1,0:T(8,128)(2,1)}), bf16[4,768,256]{2,1,0:T(8,128)(2,1)}, u32[]{:S(2)}, u32[]{:S(2)}) %all-to-all-start) | async-done | bytes 1572896 | tf_op jit(solution)/shard_map/all_to_all | solution.py:128
  31.4 30.0 %all_to_all.36.pieces = bf16[32,48,256]{2,1,0:T(8,128)(2,1)S(1)} all-to-all(bf16[32,48,256]{2,1,0:T(8,128)(2,1)S(1)} %bitcast.26), channel_id=1, replica_groups=mesh['yhi'=4,'zhi'=4,'zlo'=2,'core'=2,'ylo'=2,'x'=4] {'zlo','zhi','yhi'}, dimensions={0} | all-to-all | bytes 1572864 | tf_op jit(solution)/shard_map/all_to_all | solution.py:136
  61.4 0.0 copy-done.3
  61.4 1.6 %shard_map.87 = bf16[16,48,512]{2,1,0:T(8,128)(2,1)} custom-call(s32[1]{0:T(128)} %bitcast.core_ref, s32[4]{0:T(128)S(1)} %copy-done.3, bf16[32,48,256]{2,1,0:T(8,128)(2,1)S(1)} %all_to_all.36.pieces), custom_call_target="tpu_custom_call" | custom-call | bytes 1048576 | tf_op jit(solution)/shard_map/pallas_call | solution.py:138
  63.0 9.9 %all-to-all-start.2 = ((bf16[16,48,512]{2,1,0:T(8,128)(2,1)}), bf16[16,48,512]{2,1,0:T(8,128)(2,1)S(1)}, u32[]{:S(2)}, u32[]{:S(2)}) async-start(bf16[16,48,512]{2,1,0:T(8,128)(2,1)} %shard_map.87), calls=%async_computation.2 | async-start | bytes 1572864 | tf_op jit(solution)/shard_map/all_to_all | solution.py:147
  72.8 21.3 %all-to-all-done.2 = bf16[16,48,512]{2,1,0:T(8,128)(2,1)S(1)} async-done(((bf16[16,48,512]{2,1,0:T(8,128)(2,1)}), bf16[16,48,512]{2,1,0:T(8,128)(2,1)S(1)}, u32[]{:S(2)}, u32[]{:S(2)}) %all-to-all-start.2) | async-done | bytes 786464 | tf_op jit(solution)/shard_map/all_to_all | solution.py:147
  94.2 1.4 %convolution_convert_fusion = bf16[512,256]{1,0:T(8,128)(2,1)S(1)} fusion(bf16[768,512]{1,0:T(8,128)(2,1)S(1)} %bitcast.28, bf16[2,2,768,256]{3,2,1,0:T(8,128)(2,1)} %bitcast.2, s32[]{:T(128)S(6)} %select_n.25, s32[]{:T(128)S(6)} %add.20), kind=kOutput, calls=%fused_computation | convolution fusion | flops 201457664 | bytes 1441800 | tf_op jit(solution)/shard_map/dot_general | solution.py:151
  95.6 6.0 %collective-permute-start.4 = (bf16[512,256]{1,0:T(8,128)(2,1)S(1)}, bf16[512,256]{1,0:T(8,128)(2,1)S(1)}, u32[]{:S(2)}, u32[]{:S(2)}) collective-permute-start(bf16[512,256]{1,0:T(8,128)(2,1)S(1)} %convolution_convert_fusion), channel_id=1, source_target_pairs={{0,8},{8,0},{1,9},{9,1},{2,10},{10,2},{3,11},{11,3},{4,12},{12,4},... | collective-permute-start | bytes 786440 | tf_op jit(solution)/shard_map/ppermute | solution.py:156
  101.6 1.4 %convolution_convert_fusion.1 = bf16[512,256]{1,0:T(8,128)(2,1)S(1)} fusion(bf16[768,512]{1,0:T(8,128)(2,1)S(1)} %bitcast.29, bf16[2,2,768,256]{3,2,1,0:T(8,128)(2,1)} %bitcast.2, s32[]{:T(128)S(6)} %select_n.25), kind=kOutput, calls=%fused_computation.1 | convolution fusion | flops 201457664 | bytes 1441796 | tf_op jit(solution)/shard_map/dot_general | solution.py:151
  103.0 1.9 %collective-permute-start.3 = (bf16[512,256]{1,0:T(8,128)(2,1)S(1)}, bf16[512,256]{1,0:T(8,128)(2,1)S(1)}, u32[]{:S(2)}, u32[]{:S(2)}) collective-permute-start(bf16[512,256]{1,0:T(8,128)(2,1)S(1)} %convolution_convert_fusion.1), channel_id=1, source_target_pairs={{0,8},{8,0},{1,9},{9,1},{2,10},{10,2},{3,11},{11,3},{4,12},{12,4},... | collective-permute-start | bytes 786440 | tf_op jit(solution)/shard_map/ppermute | solution.py:156
  105.0 0.0 collective-permute-done.4
  105.0 1.4 %add_convert_fusion = bf16[512,256]{1,0:T(8,128)(2,1)S(1)} fusion(bf16[512,256]{1,0:T(8,128)(2,1)S(1)} %collective-permute-done.4, bf16[768,512]{1,0:T(8,128)(2,1)S(1)} %bitcast.30, bf16[2,2,768,256]{3,2,1,0:T(8,128)(2,1)} %bitcast.2, s32[]{:T(128)S(6)} %select_n.24, s32[]{:T(128)S(6)} %add.20), kind=kOutput, calls=%fused_computation.4 | convolution fusion | flops 201719808 | bytes 1703944 | tf_op jit(solution)/shard_map/dot_general | solution.py:151
  106.4 0.0 copy-start.7
  106.4 0.1 collective-permute-done.3
  106.5 1.4 %add_convert_fusion.1 = bf16[512,256]{1,0:T(8,128)(2,1)S(1)} fusion(bf16[512,256]{1,0:T(8,128)(2,1)S(1)} %collective-permute-done.3, bf16[768,512]{1,0:T(8,128)(2,1)S(1)} %bitcast.31, bf16[2,2,768,256]{3,2,1,0:T(8,128)(2,1)} %bitcast.2, s32[]{:T(128)S(6)} %select_n.24), kind=kOutput, calls=%fused_computation.5 | convolution fusion | flops 201719808 | bytes 1703940 | tf_op jit(solution)/shard_map/dot_general | solution.py:151
  107.9 0.0 copy-start.6
  107.9 0.8 pad_maximum_fusion
  108.7 11.5 %all-to-all-start.3 = ((bf16[16,64,256]{2,1,0:T(8,128)(2,1)}), bf16[16,64,256]{2,1,0:T(8,128)(2,1)S(1)}, u32[]{:S(2)}, u32[]{:S(2)}) async-start(bf16[16,64,256]{2,1,0:T(8,128)(2,1)} %bitcast.9), calls=%async_computation.3 | async-start | bytes 1048576 | tf_op jit(solution)/shard_map/all_to_all | solution.py:159
  120.2 0.0 copy-done.7
  120.2 10.5 %all-to-all-done.3 = bf16[16,64,256]{2,1,0:T(8,128)(2,1)S(1)} async-done(((bf16[16,64,256]{2,1,0:T(8,128)(2,1)}), bf16[16,64,256]{2,1,0:T(8,128)(2,1)S(1)}, u32[]{:S(2)}, u32[]{:S(2)}) %all-to-all-start.3) | async-done | bytes 524320 | tf_op jit(solution)/shard_map/all_to_all | solution.py:159
  130.7 0.1 convert_reduce_fusion
  130.8 0.0 copy-done.6
  130.8 0.0 copy-start.4
  130.8 0.7 fusion.3
  131.6 0.0 copy-done.4
  (2 shorter events, 0.0 us)
Async XLA Ops:
  0.6 11.5 %copy-start.1 = (bf16[3072,128]{1,0:T(8,128)(2,1)S(1)}, bf16[3072,128]{1,0:T(8,128)(2,1)}, u32[]{:S(2)}) copy-start(bf16[3072,128]{1,0:T(8,128)(2,1)} %store.1) | copy-start | bytes 2359300
  0.6 16.7 %copy-start.5 = (s32[24,3]{0,1:T(4,128)S(1)}, s32[24,3]{0,1:T(4,128)}, u32[]{:S(2)}) copy-start(s32[24,3]{0,1:T(4,128)} %param.11) | copy-start | bytes 868
  0.7 20.8 %copy-start = (bf16[24,3,128,128]{3,2,1,0:T(8,128)(2,1)S(1)}, bf16[24,3,128,128]{3,2,1,0:T(8,128)(2,1)}, u32[]{:S(2)}) copy-start(bf16[24,3,128,128]{3,2,1,0:T(8,128)(2,1)} %dipole.1) | copy-start | bytes 7077892
  0.7 30.8 %all-to-all-start = ((bf16[4,768,256]{2,1,0:T(8,128)(2,1)}), bf16[4,768,256]{2,1,0:T(8,128)(2,1)}, u32[]{:S(2)}, u32[]{:S(2)}) async-start(bf16[4,768,256]{2,1,0:T(8,128)(2,1)} %bitcast.27), calls=%async_computation | async-start | bytes 3145728 | tf_op jit(solution)/shard_map/all_to_all | solution.py:128
  12.1 9.3 %collective-permute-start = (bf16[3072,128]{1,0:T(8,128)(2,1)S(1)}, bf16[3072,128]{1,0:T(8,128)(2,1)}, u32[]{:S(2)}, u32[]{:S(2)}) collective-permute-start(bf16[3072,128]{1,0:T(8,128)(2,1)S(1)} %copy-done.1), channel_id=1, source_target_pairs={{0,8},{8,0},{1,9},{9,1},{2,10},{10,2},{3,11},{11,3},{4,12},{12,4},... | collective-permute-start | bytes 2359304 | tf_op jit(solution)/shard_map/ppermute | solution.py:92
  14.1 5.4 %collective-permute-start.1 = (bf16[256,128]{1,0:T(8,128)(2,1)S(1)}, bf16[256,128]{1,0:T(8,128)(2,1)S(1)}, u32[]{:S(2)}, u32[]{:S(2)}) collective-permute-start(bf16[256,128]{1,0:T(8,128)(2,1)S(1)} %get-tuple-element.7), channel_id=1, source_target_pairs={{0,1},{1,2},{2,3},{3,4},{4,5},{5,6},{6,7},{9,8},{10,9},{11,10},{12... | collective-permute-start | bytes 196616 | tf_op jit(solution)/shard_map/ppermute | solution.py:90
  15.4 6.0 %collective-permute-start.2 = (bf16[256,128]{1,0:T(8,128)(2,1)S(1)}, bf16[256,128]{1,0:T(8,128)(2,1)S(1)}, u32[]{:S(2)}, u32[]{:S(2)}) collective-permute-start(bf16[256,128]{1,0:T(8,128)(2,1)S(1)} %get-tuple-element.6), channel_id=1, source_target_pairs={{8,1},{9,2},{10,3},{11,4},{12,5},{13,6},{14,7},{1,8},{2,9},{3,10},... | collective-permute-start | bytes 196616 | tf_op jit(solution)/shard_map/ppermute | solution.py:91
  21.4 1.1 copy-start.2
  28.1 33.3 %copy-start.3 = (s32[4]{0:T(128)S(1)}, s32[4]{0:T(128)}, u32[]{:S(2)}) copy-start(s32[4]{0:T(128)} %owners_ref.1) | copy-start | bytes 52
  63.0 31.2 %all-to-all-start.2 = ((bf16[16,48,512]{2,1,0:T(8,128)(2,1)}), bf16[16,48,512]{2,1,0:T(8,128)(2,1)S(1)}, u32[]{:S(2)}, u32[]{:S(2)}) async-start(bf16[16,48,512]{2,1,0:T(8,128)(2,1)} %shard_map.87), calls=%async_computation.2 | async-start | bytes 1572864 | tf_op jit(solution)/shard_map/all_to_all | solution.py:147
  95.6 9.4 %collective-permute-start.4 = (bf16[512,256]{1,0:T(8,128)(2,1)S(1)}, bf16[512,256]{1,0:T(8,128)(2,1)S(1)}, u32[]{:S(2)}, u32[]{:S(2)}) collective-permute-start(bf16[512,256]{1,0:T(8,128)(2,1)S(1)} %convolution_convert_fusion), channel_id=1, source_target_pairs={{0,8},{8,0},{1,9},{9,1},{2,10},{10,2},{3,11},{11,3},{4,12},{12,4},... | collective-permute-start | bytes 786440 | tf_op jit(solution)/shard_map/ppermute | solution.py:156
  103.0 3.4 %collective-permute-start.3 = (bf16[512,256]{1,0:T(8,128)(2,1)S(1)}, bf16[512,256]{1,0:T(8,128)(2,1)S(1)}, u32[]{:S(2)}, u32[]{:S(2)}) collective-permute-start(bf16[512,256]{1,0:T(8,128)(2,1)S(1)} %convolution_convert_fusion.1), channel_id=1, source_target_pairs={{0,8},{8,0},{1,9},{9,1},{2,10},{10,2},{3,11},{11,3},{4,12},{12,4},... | collective-permute-start | bytes 786440 | tf_op jit(solution)/shard_map/ppermute | solution.py:156
  106.4 13.8 %copy-start.7 = (f32[64]{0:T(128)S(1)}, f32[64]{0:T(128)}, u32[]{:S(2)}) copy-start(f32[64]{0:T(128)} %param.12) | copy-start | bytes 772
  107.9 22.9 %copy-start.6 = (f32[256]{0:T(256)S(1)}, f32[256]{0:T(256)}, u32[]{:S(2)}) copy-start(f32[256]{0:T(256)} %param.13) | copy-start | bytes 3076
  108.7 22.0 %all-to-all-start.3 = ((bf16[16,64,256]{2,1,0:T(8,128)(2,1)}), bf16[16,64,256]{2,1,0:T(8,128)(2,1)S(1)}, u32[]{:S(2)}, u32[]{:S(2)}) async-start(bf16[16,64,256]{2,1,0:T(8,128)(2,1)} %bitcast.9), calls=%async_computation.3 | async-start | bytes 1048576 | tf_op jit(solution)/shard_map/all_to_all | solution.py:159
  130.8 0.7 copy-start.4

commit v5 on v4

--- a/solution.py
+++ b/solution.py
@@ -16,7 +16,7 @@
 STATE = ("yhi", "zhi", "zlo", "core")
 BASIS = ("ylo", "x")
 SHARED = ("core", "zlo")
-GATHER = ("zhi", "yhi")
+GATHER = ("yhi", "zhi")
 CHIPS = ("zlo",) + GATHER
 SWAP = [(0, 1), (1, 0)]
 
@@ -114,7 +114,7 @@
     for p in range(PANELS):
         owner = owners_ref[p]
         zlo, zhi, yhi = owner // 2 % 2, owner // 4 % SIZES["zhi"], owner // 16
-        piece = pieces[(zlo * SIZES["zhi"] + zhi) * SIZES["yhi"] + yhi]
+        piece = pieces[(zlo * SIZES["yhi"] + yhi) * SIZES["zhi"] + zhi]
         mine = owner % 2 == core_ref[0]
         chunk[:, pl.ds(p * width, width)] = jnp.where(mine, piece[:, :width], piece[:, width:])
     for i in range(copies.shape[0]):
@@ -146,18 +146,24 @@
     )(core.reshape(1), owners, pieces)
     gathered = lax.all_to_all(copies.reshape(-1, lowers), GATHER, 0, 0, tiled=True)
 
-    def share(kind, member):
-        rhs = lax.dynamic_index_in_dim(upper, kind, 0, keepdims=False)[member]
+    def beside(kind):
+        blocks = lax.dynamic_index_in_dim(upper, kind, 0, keepdims=False)
+        return jnp.concatenate([blocks[0], blocks[1]], 1)
+
+    def share(rhs):
         return lax.dot_general(
             gathered, rhs, (((0,), (0,)), ((), ())), preferred_element_type=F32
         )
 
-    received = [
-        lax.ppermute(share(1 - core, m).astype(BF16), "core", SWAP) for m in range(2)
-    ]
-    added = [(share(core, m) + received[m].astype(F32)).astype(BF16) for m in range(2)]
-    shares = lax.all_to_all(jnp.concatenate(added, 0), ("zlo",) + BASIS, 0, 0, tiled=True)
-    shares = shares.reshape(2 * lax.axis_size(BASIS), -1, uppers)
+    received = lax.ppermute(share(beside(1 - core)).astype(BF16), "core", SWAP)
+    kept, received = lax.optimization_barrier((share(beside(core)), received))
+    added = (kept + received.astype(F32)).astype(BF16)
+    ranges = lax.axis_size(BASIS)
+    sides = [added[:, :uppers], added[:, uppers:]]
+    added = jnp.stack([side.reshape(ranges, -1, uppers) for side in sides], 1)
+    added = added.reshape(2 * lowers, uppers)
+    shares = lax.all_to_all(added, BASIS + ("zlo",), 0, 0, tiled=True)
+    shares = shares.reshape(2 * ranges, -1, uppers)
     moments = jnp.sum(shares.astype(F32), axis=0)
     nu = upper_energy[None, :] - lower_energy[:, None]
     intensity = moments * moments * nu * jnp.exp(-lower_energy)[:, None] * (1.0 - jnp.exp(-nu))

time: 132 us -> 124 us (0.939)
  starting transfers between devices: 45.9 us -> 40.3 us
  matrix products: 5.65 us -> 1.19 us
  local copies, waits for them, and re-layouts: 1.26 us -> 2.76 us
    dot_general x4 -> x2, matrix products: 5.65 us -> 1.19 us  [share(): lax.dot_general(gathered, rhs, (((0,), (0,)), ((), ())), preferred_elemen...]
    all_to_all x1, starting transfers between devices: 11.5 us -> 8.16 us  [on_device(): shares = lax.all_to_all(added, BASIS + ('zlo',), 0, 0, tiled=True)]
    ppermute x2 -> x1, starting transfers between devices: 7.96 us -> 4.84 us  [on_device(): received = lax.ppermute(share(beside(1 - core)).astype(BF16), 'core', SWAP)]
    squeeze x0 -> x1, local copies, waits for them, and re-layouts: none -> 1.46 us  [beside(): return jnp.concatenate([blocks[0], blocks[1]], 1)]
  transfers between devices with their start and end apart: 8 -> 7, of which waited for: 6 -> 6; matrix products, arithmetic and copies ran while one was open for 2% -> 2% of each run, Pallas kernels for 4% -> 5%
where the time goes in v5:
time: 124 us; the launch traced here: 123 us
  starting transfers between devices  40.3 us (32%)
  waiting for transfers between devices  39.1 us (32%)
  blocking collectives  29.9 us (24%)
  Pallas kernels  7.1 us (6%)
  local copies, waits for them, and re-layouts  2.76 us (2%)
  other arithmetic  1.83 us (1%)
    all_to_all x1, blocking collectives, on_device(): lax.all_to_all(half, CHIPS, 0, 0, tiled=True)  29.9 us
    all_to_all x1, waiting for transfers between devices, on_device(): lax.all_to_all(copies.reshape(-1, lowers), GATHER, 0, 0, tiled=True)  21.5 us
    all_to_all x1, starting transfers between devices, on_device(): upper = lax.all_to_all(upper_coef, SHARED, 0, 0, tiled=True)  11.5 us
    all_to_all x1, starting transfers between devices, on_device(): lax.all_to_all(copies.reshape(-1, lowers), GATHER, 0, 0, tiled=True)  10.6 us
    all_to_all x1, waiting for transfers between devices, on_device(): shares = lax.all_to_all(added, BASIS + ('zlo',), 0, 0, tiled=True)  9.39 us
    all_to_all x1, starting transfers between devices, on_device(): shares = lax.all_to_all(added, BASIS + ('zlo',), 0, 0, tiled=True)  8.16 us
    pallas_call x1, Pallas kernels, chip_half(): pl.pallas_call(half_kernel, out_shape=jax.ShapeDtypeStruct((nblk // 2 * B...  5.55 us
    ppermute x1, starting transfers between devices, on_device(): received = lax.ppermute(share(beside(1 - core)).astype(BF16), 'core', SWAP)  4.84 us
  transfers between devices with their start and end apart: 7, of which 6 were waited for; matrix products, arithmetic and copies ran while one was open for 2% of the time, Pallas kernels for 5%

profile of v5, /device:TPU:1, one launch (start us, length us, event | category | flops | bytes accessed | tf_op | source)
XLA Modules:
  0.0 123.0 jit_solution(2986653937133209815)
XLA Ops:
  0.6 0.0 copy-start.1
  0.6 0.0 copy-start.5
  0.7 0.0 copy-start
  0.7 11.5 %all-to-all-start = ((bf16[4,768,256]{2,1,0:T(8,128)(2,1)}), bf16[4,768,256]{2,1,0:T(8,128)(2,1)}, u32[]{:S(2)}, u32[]{:S(2)}) async-start(bf16[4,768,256]{2,1,0:T(8,128)(2,1)} %bitcast.23), calls=%async_computation | async-start | bytes 3145728 | tf_op jit(solution)/shard_map/all_to_all | solution.py:128
  12.1 0.0 copy-done.1
  12.1 2.0 %collective-permute-start = (bf16[3072,128]{1,0:T(8,128)(2,1)S(1)}, bf16[3072,128]{1,0:T(8,128)(2,1)}, u32[]{:S(2)}, u32[]{:S(2)}) collective-permute-start(bf16[3072,128]{1,0:T(8,128)(2,1)S(1)} %copy-done.1), channel_id=1, source_target_pairs={{0,8},{8,0},{1,9},{9,1},{2,10},{10,2},{3,11},{11,3},{4,12},{12,4},... | collective-permute-start | bytes 2359304 | tf_op jit(solution)/shard_map/ppermute | solution.py:92
  14.1 1.3 %collective-permute-start.1 = (bf16[256,128]{1,0:T(8,128)(2,1)S(1)}, bf16[256,128]{1,0:T(8,128)(2,1)S(1)}, u32[]{:S(2)}, u32[]{:S(2)}) collective-permute-start(bf16[256,128]{1,0:T(8,128)(2,1)S(1)} %get-tuple-element.15), channel_id=1, source_target_pairs={{0,1},{1,2},{2,3},{3,4},{4,5},{5,6},{6,7},{9,8},{10,9},{11,10},{12... | collective-permute-start | bytes 196616 | tf_op jit(solution)/shard_map/ppermute | solution.py:90
  15.4 1.9 %collective-permute-start.2 = (bf16[256,128]{1,0:T(8,128)(2,1)S(1)}, bf16[256,128]{1,0:T(8,128)(2,1)S(1)}, u32[]{:S(2)}, u32[]{:S(2)}) collective-permute-start(bf16[256,128]{1,0:T(8,128)(2,1)S(1)} %get-tuple-element.14), channel_id=1, source_target_pairs={{8,1},{9,2},{10,3},{11,4},{12,5},{13,6},{14,7},{1,8},{2,9},{3,10},... | collective-permute-start | bytes 196616 | tf_op jit(solution)/shard_map/ppermute | solution.py:91
  17.4 0.0 copy-done.5
  17.4 0.1 copy.10.offsets_ref
  17.5 2.1 %collective-permute-done.1.own_edge = bf16[256,128]{1,0:T(8,128)(2,1)S(1)} collective-permute-done((bf16[256,128]{1,0:T(8,128)(2,1)S(1)}, bf16[256,128]{1,0:T(8,128)(2,1)S(1)}, u32[]{:S(2)}, u32[]{:S(2)}) %collective-permute-start.1) | collective-permute-done | bytes 65568 | tf_op jit(solution)/shard_map/ppermute | solution.py:90
  19.5 1.9 %collective-permute-done.2.other_edge = bf16[256,128]{1,0:T(8,128)(2,1)S(1)} collective-permute-done((bf16[256,128]{1,0:T(8,128)(2,1)S(1)}, bf16[256,128]{1,0:T(8,128)(2,1)S(1)}, u32[]{:S(2)}, u32[]{:S(2)}) %collective-permute-start.2) | collective-permute-done | bytes 65568 | tf_op jit(solution)/shard_map/ppermute | solution.py:91
  21.4 0.0 collective-permute-done.other
  21.4 0.0 copy-done
  21.4 0.0 copy-start.2
  21.4 1.1 copy-done.2
  22.6 5.5 %shard_map.86 = bf16[1536,256]{1,0:T(8,128)(2,1)S(1)} custom-call(s32[1]{0:T(128)} %bitcast.core_ref, s32[24,3]{1,0:T(8,128)S(1)} %copy.10.offsets_ref, bf16[3072,128]{1,0:T(8,128)(2,1)S(1)} %copy-done.2, bf16[3072,128]{1,0:T(8,128)(2,1)} %collective-permute-done.other, bf16[256,128]{1,0:T(8,128)(2,1)S(1)} %collective-permute-done.1.own_edge, ...), custom_call_target="tpu_custom_call" | custom-call | flops 301989888 | bytes 6291456 | tf_op jit(solution)/shard_map/pallas_call | solution.py:94
  28.1 0.0 copy-start.3
  28.1 3.3 %all-to-all-done = bf16[4,768,256]{2,1,0:T(8,128)(2,1)} async-done(((bf16[4,768,256]{2,1,0:T(8,128)(2,1)}), bf16[4,768,256]{2,1,0:T(8,128)(2,1)}, u32[]{:S(2)}, u32[]{:S(2)}) %all-to-all-start) | async-done | bytes 1572896 | tf_op jit(solution)/shard_map/all_to_all | solution.py:128
  31.4 29.9 %all_to_all.36.pieces = bf16[32,48,256]{2,1,0:T(8,128)(2,1)S(1)} all-to-all(bf16[32,48,256]{2,1,0:T(8,128)(2,1)S(1)} %bitcast.22), channel_id=1, replica_groups=mesh['yhi'=4,'zhi'=4,'zlo'=2,'core'=2,'ylo'=2,'x'=4] {'zlo','yhi','zhi'}, dimensions={0} | all-to-all | bytes 1572864 | tf_op jit(solution)/shard_map/all_to_all | solution.py:136
  61.4 0.0 copy-done.3
  61.4 1.6 %shard_map.87 = bf16[16,48,512]{2,1,0:T(8,128)(2,1)} custom-call(s32[1]{0:T(128)} %bitcast.core_ref, s32[4]{0:T(128)S(1)} %copy-done.3, bf16[32,48,256]{2,1,0:T(8,128)(2,1)S(1)} %all_to_all.36.pieces), custom_call_target="tpu_custom_call" | custom-call | bytes 1048576 | tf_op jit(solution)/shard_map/pallas_call | solution.py:138
  62.9 10.6 %all-to-all-start.2 = ((bf16[16,48,512]{2,1,0:T(8,128)(2,1)}), bf16[16,48,512]{2,1,0:T(8,128)(2,1)S(1)}, u32[]{:S(2)}, u32[]{:S(2)}) async-start(bf16[16,48,512]{2,1,0:T(8,128)(2,1)} %shard_map.87), calls=%async_computation.2 | async-start | bytes 1572864 | tf_op jit(solution)/shard_map/all_to_all | solution.py:147
  73.5 1.5 %dynamic-slice_bitcast_fusion.1 = (bf16[768,256]{1,0:T(8,128)(2,1)S(1)}, bf16[768,256]{1,0:T(8,128)(2,1)S(1)}, bf16[768,256]{1,0:T(8,128)(2,1)S(1)}, bf16[768,256]{1,0:T(8,128)(2,1)S(1)}) fusion(bf16[2,2,768,256]{3,2,1,0:T(8,128)(2,1)} %bitcast.2, s32[]{:T(128)S(6)} %select_n.23, s32[]{:T(128)S(6)} %select_n.22, s32[]{:T(128)S(6)} %add.14), kind=kLoop, calls=%fused_computation.12 | loop fusion | bytes 3145740 | tf_op jit(solution)/shard_map/squeeze | solution.py:151
  75.0 21.5 %all-to-all-done.2 = bf16[16,48,512]{2,1,0:T(8,128)(2,1)S(1)} async-done(((bf16[16,48,512]{2,1,0:T(8,128)(2,1)}), bf16[16,48,512]{2,1,0:T(8,128)(2,1)S(1)}, u32[]{:S(2)}, u32[]{:S(2)}) %all-to-all-start.2) | async-done | bytes 786464 | tf_op jit(solution)/shard_map/all_to_all | solution.py:147
  96.6 0.6 convolution_convert_fusion
  97.2 4.8 %collective-permute-start.3 = (bf16[512,512]{1,0:T(8,128)(2,1)S(1)}, bf16[512,512]{1,0:T(8,128)(2,1)S(1)}, u32[]{:S(2)}, u32[]{:S(2)}) collective-permute-start(bf16[512,512]{1,0:T(8,128)(2,1)S(1)} %convolution_convert_fusion), channel_id=1, source_target_pairs={{0,8},{8,0},{1,9},{9,1},{2,10},{10,2},{3,11},{11,3},{4,12},{12,4},... | collective-permute-start | bytes 1572872 | tf_op jit(solution)/shard_map/ppermute | solution.py:158
  102.0 0.6 fusion
  102.6 0.9 collective-permute-done.3
  103.5 0.2 add_convert_fusion
  103.7 0.0 copy-start.7
  103.7 0.0 copy-start.6
  103.8 0.9 pad_maximum_fusion
  104.6 8.2 %all-to-all-start.3 = ((bf16[16,64,256]{2,1,0:T(8,128)(2,1)}), bf16[16,64,256]{2,1,0:T(8,128)(2,1)S(1)}, u32[]{:S(2)}, u32[]{:S(2)}) async-start(bf16[16,64,256]{2,1,0:T(8,128)(2,1)} %bitcast.13), calls=%async_computation.3 | async-start | bytes 1048576 | tf_op jit(solution)/shard_map/all_to_all | solution.py:165
  112.8 0.0 copy-done.7
  112.8 9.4 %all-to-all-done.3 = bf16[16,64,256]{2,1,0:T(8,128)(2,1)S(1)} async-done(((bf16[16,64,256]{2,1,0:T(8,128)(2,1)}), bf16[16,64,256]{2,1,0:T(8,128)(2,1)S(1)}, u32[]{:S(2)}, u32[]{:S(2)}) %all-to-all-start.3) | async-done | bytes 524320 | tf_op jit(solution)/shard_map/all_to_all | solution.py:165
  122.2 0.1 convert_reduce_fusion
  122.3 0.0 copy-done.6
  122.3 0.0 copy-start.4
  122.3 0.7 fusion.8
  123.0 0.0 copy-done.4
  (3 shorter events, 0.1 us)
Async XLA Ops:
  0.6 11.5 %copy-start.1 = (bf16[3072,128]{1,0:T(8,128)(2,1)S(1)}, bf16[3072,128]{1,0:T(8,128)(2,1)}, u32[]{:S(2)}) copy-start(bf16[3072,128]{1,0:T(8,128)(2,1)} %store.1) | copy-start | bytes 2359300
  0.6 16.7 %copy-start.5 = (s32[24,3]{0,1:T(4,128)S(1)}, s32[24,3]{0,1:T(4,128)}, u32[]{:S(2)}) copy-start(s32[24,3]{0,1:T(4,128)} %param.11) | copy-start | bytes 868
  0.7 20.8 %copy-start = (bf16[24,3,128,128]{3,2,1,0:T(8,128)(2,1)S(1)}, bf16[24,3,128,128]{3,2,1,0:T(8,128)(2,1)}, u32[]{:S(2)}) copy-start(bf16[24,3,128,128]{3,2,1,0:T(8,128)(2,1)} %dipole.1) | copy-start | bytes 7077892
  0.7 30.8 %all-to-all-start = ((bf16[4,768,256]{2,1,0:T(8,128)(2,1)}), bf16[4,768,256]{2,1,0:T(8,128)(2,1)}, u32[]{:S(2)}, u32[]{:S(2)}) async-start(bf16[4,768,256]{2,1,0:T(8,128)(2,1)} %bitcast.23), calls=%async_computation | async-start | bytes 3145728 | tf_op jit(solution)/shard_map/all_to_all | solution.py:128
  12.1 9.3 %collective-permute-start = (bf16[3072,128]{1,0:T(8,128)(2,1)S(1)}, bf16[3072,128]{1,0:T(8,128)(2,1)}, u32[]{:S(2)}, u32[]{:S(2)}) collective-permute-start(bf16[3072,128]{1,0:T(8,128)(2,1)S(1)} %copy-done.1), channel_id=1, source_target_pairs={{0,8},{8,0},{1,9},{9,1},{2,10},{10,2},{3,11},{11,3},{4,12},{12,4},... | collective-permute-start | bytes 2359304 | tf_op jit(solution)/shard_map/ppermute | solution.py:92
  14.1 5.4 %collective-permute-start.1 = (bf16[256,128]{1,0:T(8,128)(2,1)S(1)}, bf16[256,128]{1,0:T(8,128)(2,1)S(1)}, u32[]{:S(2)}, u32[]{:S(2)}) collective-permute-start(bf16[256,128]{1,0:T(8,128)(2,1)S(1)} %get-tuple-element.15), channel_id=1, source_target_pairs={{0,1},{1,2},{2,3},{3,4},{4,5},{5,6},{6,7},{9,8},{10,9},{11,10},{12... | collective-permute-start | bytes 196616 | tf_op jit(solution)/shard_map/ppermute | solution.py:90
  15.4 6.0 %collective-permute-start.2 = (bf16[256,128]{1,0:T(8,128)(2,1)S(1)}, bf16[256,128]{1,0:T(8,128)(2,1)S(1)}, u32[]{:S(2)}, u32[]{:S(2)}) collective-permute-start(bf16[256,128]{1,0:T(8,128)(2,1)S(1)} %get-tuple-element.14), channel_id=1, source_target_pairs={{8,1},{9,2},{10,3},{11,4},{12,5},{13,6},{14,7},{1,8},{2,9},{3,10},... | collective-permute-start | bytes 196616 | tf_op jit(solution)/shard_map/ppermute | solution.py:91
  21.4 1.1 copy-start.2
  28.1 33.2 %copy-start.3 = (s32[4]{0:T(128)S(1)}, s32[4]{0:T(128)}, u32[]{:S(2)}) copy-start(s32[4]{0:T(128)} %owners_ref.1) | copy-start | bytes 52
  62.9 33.6 %all-to-all-start.2 = ((bf16[16,48,512]{2,1,0:T(8,128)(2,1)}), bf16[16,48,512]{2,1,0:T(8,128)(2,1)S(1)}, u32[]{:S(2)}, u32[]{:S(2)}) async-start(bf16[16,48,512]{2,1,0:T(8,128)(2,1)} %shard_map.87), calls=%async_computation.2 | async-start | bytes 1572864 | tf_op jit(solution)/shard_map/all_to_all | solution.py:147
  97.2 6.4 %collective-permute-start.3 = (bf16[512,512]{1,0:T(8,128)(2,1)S(1)}, bf16[512,512]{1,0:T(8,128)(2,1)S(1)}, u32[]{:S(2)}, u32[]{:S(2)}) collective-permute-start(bf16[512,512]{1,0:T(8,128)(2,1)S(1)} %convolution_convert_fusion), channel_id=1, source_target_pairs={{0,8},{8,0},{1,9},{9,1},{2,10},{10,2},{3,11},{11,3},{4,12},{12,4},... | collective-permute-start | bytes 1572872 | tf_op jit(solution)/shard_map/ppermute | solution.py:158
  103.7 9.1 %copy-start.7 = (f32[64]{0:T(128)S(1)}, f32[64]{0:T(128)}, u32[]{:S(2)}) copy-start(f32[64]{0:T(128)} %param.12) | copy-start | bytes 772
  103.7 18.5 %copy-start.6 = (f32[256]{0:T(256)S(1)}, f32[256]{0:T(256)}, u32[]{:S(2)}) copy-start(f32[256]{0:T(256)} %param.13) | copy-start | bytes 3076
  104.6 17.6 %all-to-all-start.3 = ((bf16[16,64,256]{2,1,0:T(8,128)(2,1)}), bf16[16,64,256]{2,1,0:T(8,128)(2,1)S(1)}, u32[]{:S(2)}, u32[]{:S(2)}) async-start(bf16[16,64,256]{2,1,0:T(8,128)(2,1)} %bitcast.13), calls=%async_computation.3 | async-start | bytes 1048576 | tf_op jit(solution)/shard_map/all_to_all | solution.py:165
  122.3 0.7 copy-start.4

commit v6 on v5

v6 whole, which is shorter than its diff:
```python
import functools

import jax
import jax.numpy as jnp
from jax import lax
from jax.experimental import pallas as pl
from jax.experimental.pallas import tpu as pltpu
from jax.sharding import Mesh
from jax.sharding import PartitionSpec as P

BS = 128
REACH = 2
PANELS = 4
BF16 = jnp.bfloat16
F32 = jnp.float32

SIZES = {"yhi": 4, "zhi": 4, "zlo": 2, "core": 2, "ylo": 2, "x": 4}
STATE = ("yhi", "zhi", "zlo", "core")
BASIS = ("ylo", "x")
SHARED = ("core", "zlo")
GATHER = ("yhi", "zhi")
CHIPS = ("zlo",) + GATHER
SWAP = [(0, 1), (1, 0)]

VMEM = pl.BlockSpec(memory_space=pltpu.VMEM)
SMEM = pl.BlockSpec(memory_space=pltpu.SMEM)


def owned(owners_ref, state):
    found = owners_ref[0] == state
    for p in range(1, PANELS):
        found = found | (owners_ref[p] == state)
    return found


def half_kernel(
    second, state_ref, owners_ref, offsets_ref, own, other, own_edge, other_edge, dipole, half
):
    nblk, terms = dipole.shape[0], dipole.shape[1]
    ncol = nblk // 2
    core = lax.rem(state_ref[0], 2)
    first = core * ncol
    if second:
        mine = core == 1
    else:
        mine = (core == 0) == owned(owners_ref, state_ref[0] - core)

    for j in range(ncol):
        column = first + j
        blocks = []
        for k in range(terms):
            block = column + offsets_ref[column, k]
            inside = (block >= 0) & (block < nblk)
            block_in = jnp.clip(block, 0, nblk - 1)
            source = pl.ds(pl.multiple_of(block_in * BS, BS), BS)
            rows = jnp.where(mine, own[source, :], other[source, :])
            if j < REACH or j >= ncol - REACH:
                place = jnp.where(block < 0, block + REACH, block - nblk)
                beyond = pl.ds(pl.multiple_of(jnp.clip(place, 0, REACH - 1) * BS, BS), BS)
                edge = jnp.where(mine, own_edge[beyond, :], other_edge[beyond, :])
                rows = jnp.where(inside, rows, edge)
            blocks.append(rows)
        half[pl.ds(j * BS, BS), :] = lax.dot_general(
            dipole[column].reshape(terms * BS, BS),
            jnp.concatenate(blocks, axis=0),
            (((0,), (0,)), ((), ())),
            preferred_element_type=F32,
        ).astype(BF16)


def chip_panels(store, core):
    rows = store.shape[0]
    reach = REACH * BS
    count = lax.axis_size(BASIS)

    def member(basis, kind):
        return basis + count * kind

    own_pairs = [(member(b, 0), member(b + 1, 0)) for b in range(count - 1)]
    own_pairs += [(member(b + 1, 1), member(b, 1)) for b in range(count - 1)]
    other_pairs = [(member(b, 1), member(b + 1, 0)) for b in range(count - 1)]
    other_pairs += [(member(b + 1, 0), member(b, 1)) for b in range(count - 1)]
    axes = ("core",) + BASIS
    low, high = store[:reach], store[rows - reach :]
    first = core == 0
    own_edge = lax.ppermute(jnp.where(first, high, low), axes, own_pairs)
    other_edge = lax.ppermute(jnp.where(first, low, high), axes, other_pairs)
    other = lax.ppermute(store, "core", SWAP)
    return store, other, own_edge, other_edge


def chip_half(second, state, owners, offsets, panels, dipole):
    nblk, terms = offsets.shape
    rows, width = panels[0].shape
    return pl.pallas_call(
        functools.partial(half_kernel, second),
        out_shape=jax.ShapeDtypeStruct((rows // 2, width), BF16),
        in_specs=[SMEM, SMEM, SMEM] + [VMEM] * 5,
        out_specs=VMEM,
        compiler_params=pltpu.CompilerParams(vmem_limit_bytes=12 << 20),
        cost_estimate=pl.CostEstimate(
            flops=nblk * terms * BS * BS * width, bytes_accessed=6 << 20, transcendentals=0
        ),
    )(state.reshape(1), owners, offsets, *panels, dipole)


def pick_kernel(owners_ref, pieces, seconds, copies, chunk):
    width = pieces.shape[2]
    for p in range(PANELS):
        owner = owners_ref[p]
        core, zlo, zhi, yhi = owner % 2, owner // 2 % 2, owner // 4 % SIZES["zhi"], owner // 16
        chip = (zlo * SIZES["yhi"] + yhi) * SIZES["zhi"] + zhi
        late = (core == 1) & owned(owners_ref, owner - 1)
        chunk[:, pl.ds(p * width, width)] = jnp.where(late, seconds[chip], pieces[chip])
    for i in range(copies.shape[0]):
        copies[i] = chunk[...]


def pick(owners, pieces, seconds):
    peers = lax.axis_size(GATHER)
    rows, width = pieces.shape[1:]
    return pl.pallas_call(
        pick_kernel,
        out_shape=jax.ShapeDtypeStruct((peers, rows, PANELS * width), BF16),
        in_specs=[SMEM, VMEM, VMEM],
        out_specs=VMEM,
        scratch_shapes=[pltpu.VMEM((rows, PANELS * width), BF16)],
        compiler_params=pltpu.CompilerParams(vmem_limit_bytes=8 << 20),
        cost_estimate=pl.CostEstimate(flops=0, bytes_accessed=1 << 20, transcendentals=0),
    )(owners, pieces, seconds)


def on_device(upper_coef, store, owners, dipole, offsets, lower_energy, upper_energy):
    core = lax.axis_index("core")
    state = lax.axis_index(STATE)
    width = store.shape[1]
    lowers = PANELS * width
    uppers = upper_coef.shape[1]
    upper = lax.all_to_all(upper_coef, SHARED, 0, 0, tiled=True)
    upper = upper.reshape(2, 2, -1, uppers)

    panels = chip_panels(store, core)
    half = chip_half(False, state, owners, offsets, panels, dipole)
    half, upper = lax.optimization_barrier((half, upper))

    def scatter(half):
        chips = lax.axis_size(CHIPS)
        return lax.all_to_all(half, CHIPS, 0, 0, tiled=True).reshape(chips, -1, width)

    pieces = scatter(half)
    chips_of = owners // 2
    shared = jnp.sum((chips_of[:, None] == chips_of[None, :]).astype(jnp.int32)) > PANELS
    copies = lax.cond(
        shared,
        lambda: pick(
            owners, pieces, scatter(chip_half(True, state, owners, offsets, panels, dipole))
        ),
        lambda: pick(owners, pieces, pieces),
    )
    gathered = lax.all_to_all(copies.reshape(-1, lowers), GATHER, 0, 0, tiled=True)

    def beside(kind):
        blocks = lax.dynamic_index_in_dim(upper, kind, 0, keepdims=False)
        return jnp.concatenate([blocks[0], blocks[1]], 1)

    def share(rhs):
        return lax.dot_general(
            gathered, rhs, (((0,), (0,)), ((), ())), preferred_element_type=F32
        )

    received = lax.ppermute(share(beside(1 - core)).astype(BF16), "core", SWAP)
    kept, received = lax.optimization_barrier((share(beside(core)), received))
    added = (kept + received.astype(F32)).astype(BF16)
    ranges = lax.axis_size(BASIS)
    sides = [added[:, :uppers], added[:, uppers:]]
    added = jnp.stack([side.reshape(ranges, -1, uppers) for side in sides], 1)
    added = added.reshape(2 * lowers, uppers)
    shares = lax.all_to_all(added, BASIS + ("zlo",), 0, 0, tiled=True)
    shares = shares.reshape(2 * ranges, -1, uppers)
    moments = jnp.sum(shares.astype(F32), axis=0)
    nu = upper_energy[None, :] - lower_energy[:, None]
    intensity = moments * moments * nu * jnp.exp(-lower_energy)[:, None] * (1.0 - jnp.exp(-nu))
    return moments, intensity


def solution(mesh):
    fine = Mesh(mesh.devices.reshape(tuple(SIZES.values())), tuple(SIZES))
    placed = (
        P(BASIS, STATE),
        P(BASIS, STATE),
        P(),
        P(BASIS, None, None, None),
        P(BASIS, None),
        P(BASIS),
        P(STATE),
    )
    return jax.shard_map(
        on_device,
        mesh=fine,
        in_specs=placed,
        out_specs=(P(BASIS, STATE), P(BASIS, STATE)),
        check_vma=False,
    )
```

time: 124 us -> 114 us (0.919)
  blocking collectives: 29.9 us -> 0 us
  waiting for transfers between devices: 39.1 us -> 60.1 us
  Pallas kernels: 7.1 us -> 4.12 us
  starting transfers between devices: 40.3 us -> 42 us
    all_to_all x1 -> x0, blocking collectives: 29.9 us -> none  [on_device(): lax.all_to_all(half, CHIPS, 0, 0, tiled=True)]
    all_to_all x0 -> x1, waiting for transfers between devices: none -> 14.2 us  [scatter(): lax.all_to_all(half, CHIPS, 0, 0, tiled=True).reshape(chips, -1, width)]
    all_to_all x0 -> x1, starting transfers between devices: none -> 10.3 us  [scatter(): lax.all_to_all(half, CHIPS, 0, 0, tiled=True).reshape(chips, -1, width)]
    all_to_all x1, starting transfers between devices: 10.6 us -> 5.56 us  [on_device(): lax.all_to_all(copies.reshape(-1, lowers), GATHER, 0, 0, tiled=True)]
    all_to_all x1, waiting for transfers between devices: 3.31 us -> 7.44 us  [on_device(): upper = lax.all_to_all(upper_coef, SHARED, 0, 0, tiled=True)]
    all_to_all x1, starting transfers between devices: 8.16 us -> 4.83 us  [on_device(): shares = lax.all_to_all(added, BASIS + ('zlo',), 0, 0, tiled=True)]
    pallas_call x2, Pallas kernels: 7.1 us -> 4.12 us  [the longest x1 2.56 us: chip_half(): pl.pallas_call(functools.partial(half_kernel, second), out_shape=jax.Shap...]
    all_to_all x1, waiting for transfers between devices: 21.5 us -> 24.3 us  [on_device(): lax.all_to_all(copies.reshape(-1, lowers), GATHER, 0, 0, tiled=True)]
  transfers between devices with their start and end apart: 7 -> 8, of which waited for: 6 -> 7; matrix products, arithmetic and copies ran while one was open for 2% -> 3% of each run, Pallas kernels for 5% -> 2%
where the time goes in v6:
time: 114 us; the launch traced here: 113 us
  waiting for transfers between devices  60.1 us (53%)
  starting transfers between devices  42 us (37%)
  Pallas kernels  4.12 us (4%)
  other arithmetic  2.61 us (2%)
  local copies, waits for them, and re-layouts  1.63 us (1%)
  between operations  1.55 us (1%)
  matrix products  1.19 us (1%)
    all_to_all x1, waiting for transfers between devices, on_device(): lax.all_to_all(copies.reshape(-1, lowers), GATHER, 0, 0, tiled=True)  24.3 us
    all_to_all x1, waiting for transfers between devices, scatter(): lax.all_to_all(half, CHIPS, 0, 0, tiled=True).reshape(chips, -1, width)  14.2 us
    all_to_all x1, starting transfers between devices, on_device(): upper = lax.all_to_all(upper_coef, SHARED, 0, 0, tiled=True)  11.5 us
    all_to_all x1, starting transfers between devices, scatter(): lax.all_to_all(half, CHIPS, 0, 0, tiled=True).reshape(chips, -1, width)  10.3 us
    all_to_all x1, waiting for transfers between devices, on_device(): shares = lax.all_to_all(added, BASIS + ('zlo',), 0, 0, tiled=True)  9.39 us
    all_to_all x1, waiting for transfers between devices, on_device(): upper = lax.all_to_all(upper_coef, SHARED, 0, 0, tiled=True)  7.44 us
    all_to_all x1, starting transfers between devices, on_device(): lax.all_to_all(copies.reshape(-1, lowers), GATHER, 0, 0, tiled=True)  5.56 us
    all_to_all x1, starting transfers between devices, on_device(): shares = lax.all_to_all(added, BASIS + ('zlo',), 0, 0, tiled=True)  4.83 us
  transfers between devices with their start and end apart: 8, of which 7 were waited for; matrix products, arithmetic and copies ran while one was open for 3% of the time, Pallas kernels for 2%

profile of v6, /device:TPU:1, one launch (start us, length us, event | category | flops | bytes accessed | tf_op | source)
XLA Modules:
  0.0 113.3 jit_solution(10620002890068785053)
XLA Ops:
  0.6 0.0 copy-start.1
  0.6 0.0 copy-start.6
  0.7 0.0 copy-start
  0.7 0.0 copy-start.5
  0.7 11.5 %all-to-all-start.1 = ((bf16[4,768,256]{2,1,0:T(8,128)(2,1)}), bf16[4,768,256]{2,1,0:T(8,128)(2,1)}, u32[]{:S(2)}, u32[]{:S(2)}) async-start(bf16[4,768,256]{2,1,0:T(8,128)(2,1)} %bitcast.25), calls=%async_computation.1 | async-start | bytes 3145728 | tf_op jit(solution)/shard_map/all_to_all | solution.py:139
  12.1 0.0 copy-done.1
  12.1 2.0 %collective-permute-start = (bf16[3072,128]{1,0:T(8,128)(2,1)S(1)}, bf16[3072,128]{1,0:T(8,128)(2,1)}, u32[]{:S(2)}, u32[]{:S(2)}) collective-permute-start(bf16[3072,128]{1,0:T(8,128)(2,1)S(1)} %copy-done.1), channel_id=1, source_target_pairs={{0,8},{8,0},{1,9},{9,1},{2,10},{10,2},{3,11},{11,3},{4,12},{12,4},... | collective-permute-start | bytes 2359304 | tf_op jit(solution)/shard_map/ppermute | solution.py:88
  14.1 1.3 %collective-permute-start.1 = (bf16[256,128]{1,0:T(8,128)(2,1)S(1)}, bf16[256,128]{1,0:T(8,128)(2,1)S(1)}, u32[]{:S(2)}, u32[]{:S(2)}) collective-permute-start(bf16[256,128]{1,0:T(8,128)(2,1)S(1)} %get-tuple-element.78), channel_id=1, source_target_pairs={{0,1},{1,2},{2,3},{3,4},{4,5},{5,6},{6,7},{9,8},{10,9},{11,10},{12... | collective-permute-start | bytes 196616 | tf_op jit(solution)/shard_map/ppermute | solution.py:86
  15.4 1.9 %collective-permute-start.2 = (bf16[256,128]{1,0:T(8,128)(2,1)S(1)}, bf16[256,128]{1,0:T(8,128)(2,1)S(1)}, u32[]{:S(2)}, u32[]{:S(2)}) collective-permute-start(bf16[256,128]{1,0:T(8,128)(2,1)S(1)} %get-tuple-element.77), channel_id=1, source_target_pairs={{8,1},{9,2},{10,3},{11,4},{12,5},{13,6},{14,7},{1,8},{2,9},{3,10},... | collective-permute-start | bytes 196616 | tf_op jit(solution)/shard_map/ppermute | solution.py:87
  17.4 0.0 copy-done.6
  17.4 0.1 copy.15.offsets_ref
  17.5 2.1 %collective-permute-done.1.own_edge = bf16[256,128]{1,0:T(8,128)(2,1)S(1)} collective-permute-done((bf16[256,128]{1,0:T(8,128)(2,1)S(1)}, bf16[256,128]{1,0:T(8,128)(2,1)S(1)}, u32[]{:S(2)}, u32[]{:S(2)}) %collective-permute-start.1) | collective-permute-done | bytes 65568 | tf_op jit(solution)/shard_map/ppermute | solution.py:86
  19.5 0.0 copy-start.2
  19.6 1.9 %collective-permute-done.2.other_edge = bf16[256,128]{1,0:T(8,128)(2,1)S(1)} collective-permute-done((bf16[256,128]{1,0:T(8,128)(2,1)S(1)}, bf16[256,128]{1,0:T(8,128)(2,1)S(1)}, u32[]{:S(2)}, u32[]{:S(2)}) %collective-permute-start.2) | collective-permute-done | bytes 65568 | tf_op jit(solution)/shard_map/ppermute | solution.py:87
  21.4 0.0 copy-start.3
  21.4 0.0 collective-permute-done.other
  21.4 0.0 copy-done
  21.4 0.0 copy-done.5
  21.4 2.6 %shard_map.86 = bf16[1536,128]{1,0:T(8,128)(2,1)} custom-call(s32[1]{0:T(128)} %bitcast.2.state_ref, s32[4]{0:T(128)S(1)} %copy-done.5, s32[24,3]{1,0:T(8,128)S(1)} %copy.15.offsets_ref, bf16[3072,128]{1,0:T(8,128)(2,1)S(1)} %copy-done.1, bf16[3072,128]{1,0:T(8,128)(2,1)} %collective-permute-done.other, ...), custom_call_target="tpu_custom_call" | custom-call | flops 150994944 | bytes 6291456 | tf_op jit(solution)/shard_map/pallas_call | solution.py:95
  24.0 0.0 copy-done.2
  24.0 0.0 copy-done.3
  24.0 7.4 %all-to-all-done.1 = bf16[4,768,256]{2,1,0:T(8,128)(2,1)} async-done(((bf16[4,768,256]{2,1,0:T(8,128)(2,1)}), bf16[4,768,256]{2,1,0:T(8,128)(2,1)}, u32[]{:S(2)}, u32[]{:S(2)}) %all-to-all-start.1) | async-done | bytes 1572896 | tf_op jit(solution)/shard_map/all_to_all | solution.py:139
  31.4 10.3 %all-to-all-start.2 = ((bf16[32,48,128]{2,1,0:T(8,128)(2,1)}), bf16[32,48,128]{2,1,0:T(8,128)(2,1)S(1)}, u32[]{:S(2)}, u32[]{:S(2)}) async-start(bf16[32,48,128]{2,1,0:T(8,128)(2,1)} %bitcast.5), calls=%async_computation.2 | async-start | bytes 786432 | tf_op jit(solution)/shard_map/all_to_all | solution.py:148
  41.8 0.8 convert_reduce_fusion.1
  43.2 14.2 %all-to-all-done.2 = bf16[32,48,128]{2,1,0:T(8,128)(2,1)S(1)} async-done(((bf16[32,48,128]{2,1,0:T(8,128)(2,1)}), bf16[32,48,128]{2,1,0:T(8,128)(2,1)S(1)}, u32[]{:S(2)}, u32[]{:S(2)}) %all-to-all-start.2) | async-done | bytes 393248 | tf_op jit(solution)/shard_map/all_to_all | solution.py:148
  57.4 1.6 %conditional.1 = (bf16[16,48,512]{2,1,0:T(8,128)(2,1)}) conditional(s32[]{:T(128)} %convert_element_type.19, (s32[4]{0:T(128)S(1)}, bf16[32,48,128]{2,1,0:T(8,128)(2,1)S(1)}) %tuple.35, (s32[]{:T(128)}, s32[4]{0:T(128)S(1)}, s32[24,3]{0,1:T(4,128)}, bf16[3072,128]{1,0:T(8,128)(2,1)S(1)}, bf16[3072,128]{1,0:T(8,128)(2,1)}, ...), branch_computations={%region_1.2_spmd, %region_2.3_spmd} | conditional | flops 150994944 | bytes 8127048 | solution.py:153
  57.4 1.6 %branch_0_fun.1 = bf16[16,48,512]{2,1,0:T(8,128)(2,1)} custom-call(s32[4]{0:T(128)S(1)} %get-tuple-element.12.owners_ref, bf16[32,48,128]{2,1,0:T(8,128)(2,1)S(1)} %get-tuple-element.26.pieces.seconds, bf16[32,48,128]{2,1,0:T(8,128)(2,1)S(1)} %get-tuple-element.26.pieces.seconds), custom_call_target="tpu_custom_call" | custom-call | bytes 1048576 | tf_op jit(solution)/shard_map/cond/branch_0_fun/pallas_call | solution.py:122
  59.0 5.6 %all-to-all-start.3 = ((bf16[16,48,512]{2,1,0:T(8,128)(2,1)}), bf16[16,48,512]{2,1,0:T(8,128)(2,1)S(1)}, u32[]{:S(2)}, u32[]{:S(2)}) async-start(bf16[16,48,512]{2,1,0:T(8,128)(2,1)} %get-tuple-element.81), calls=%async_computation.3 | async-start | bytes 1572864 | tf_op jit(solution)/shard_map/all_to_all | solution.py:160
  64.6 1.5 %dynamic-slice_bitcast_fusion.1 = (bf16[768,256]{1,0:T(8,128)(2,1)S(1)}, bf16[768,256]{1,0:T(8,128)(2,1)S(1)}, bf16[768,256]{1,0:T(8,128)(2,1)S(1)}, bf16[768,256]{1,0:T(8,128)(2,1)S(1)}) fusion(bf16[2,2,768,256]{3,2,1,0:T(8,128)(2,1)} %bitcast.4, s32[]{:T(128)S(6)} %select_n.29, s32[]{:T(128)S(6)} %select_n.28, s32[]{:T(128)S(6)} %add.27), kind=kLoop, calls=%fused_computation.12 | loop fusion | bytes 3145740 | tf_op jit(solution)/shard_map/squeeze | solution.py:164
  66.0 24.3 %all-to-all-done.3 = bf16[16,48,512]{2,1,0:T(8,128)(2,1)S(1)} async-done(((bf16[16,48,512]{2,1,0:T(8,128)(2,1)}), bf16[16,48,512]{2,1,0:T(8,128)(2,1)S(1)}, u32[]{:S(2)}, u32[]{:S(2)}) %all-to-all-start.3) | async-done | bytes 786464 | tf_op jit(solution)/shard_map/all_to_all | solution.py:160
  90.3 0.6 convolution_convert_fusion
  90.9 4.7 %collective-permute-start.3 = (bf16[512,512]{1,0:T(8,128)(2,1)S(1)}, bf16[512,512]{1,0:T(8,128)(2,1)S(1)}, u32[]{:S(2)}, u32[]{:S(2)}) collective-permute-start(bf16[512,512]{1,0:T(8,128)(2,1)S(1)} %convolution_convert_fusion), channel_id=1, source_target_pairs={{0,8},{8,0},{1,9},{9,1},{2,10},{10,2},{3,11},{11,3},{4,12},{12,4},... | collective-permute-start | bytes 1572872 | tf_op jit(solution)/shard_map/ppermute | solution.py:171
  95.6 0.6 fusion
  96.2 0.9 collective-permute-done.3
  97.1 0.2 add_convert_fusion
  97.3 0.0 copy-start.8
  97.3 0.0 copy-start.7
  97.4 0.9 pad_maximum_fusion
  98.2 4.8 %all-to-all-start.4 = ((bf16[16,64,256]{2,1,0:T(8,128)(2,1)}), bf16[16,64,256]{2,1,0:T(8,128)(2,1)S(1)}, u32[]{:S(2)}, u32[]{:S(2)}) async-start(bf16[16,64,256]{2,1,0:T(8,128)(2,1)} %bitcast.15), calls=%async_computation.4 | async-start | bytes 1048576 | tf_op jit(solution)/shard_map/all_to_all | solution.py:178
  103.0 0.0 copy-done.8
  103.1 9.4 %all-to-all-done.4 = bf16[16,64,256]{2,1,0:T(8,128)(2,1)S(1)} async-done(((bf16[16,64,256]{2,1,0:T(8,128)(2,1)}), bf16[16,64,256]{2,1,0:T(8,128)(2,1)S(1)}, u32[]{:S(2)}, u32[]{:S(2)}) %all-to-all-start.4) | async-done | bytes 524320 | tf_op jit(solution)/shard_map/all_to_all | solution.py:178
  112.5 0.1 convert_reduce_fusion
  112.5 0.0 copy-done.7
  112.6 0.0 copy-start.4
  112.6 0.7 fusion.8
  113.3 0.0 copy-done.4
  (4 shorter events, 0.1 us)
Async XLA Ops:
  0.6 11.5 %copy-start.1 = (bf16[3072,128]{1,0:T(8,128)(2,1)S(1)}, bf16[3072,128]{1,0:T(8,128)(2,1)}, u32[]{:S(2)}) copy-start(bf16[3072,128]{1,0:T(8,128)(2,1)} %own.1) | copy-start | bytes 2359300
  0.6 16.7 %copy-start.6 = (s32[24,3]{0,1:T(4,128)S(1)}, s32[24,3]{0,1:T(4,128)}, u32[]{:S(2)}) copy-start(s32[24,3]{0,1:T(4,128)} %param.13) | copy-start | bytes 868
  0.7 20.8 %copy-start = (bf16[24,3,128,128]{3,2,1,0:T(8,128)(2,1)S(1)}, bf16[24,3,128,128]{3,2,1,0:T(8,128)(2,1)}, u32[]{:S(2)}) copy-start(bf16[24,3,128,128]{3,2,1,0:T(8,128)(2,1)} %dipole.1) | copy-start | bytes 7077892
  0.7 20.8 %copy-start.5 = (s32[4]{0:T(128)S(1)}, s32[4]{0:T(128)}, u32[]{:S(2)}) copy-start(s32[4]{0:T(128)} %owners_ref.1) | copy-start | bytes 52
  0.7 30.8 %all-to-all-start.1 = ((bf16[4,768,256]{2,1,0:T(8,128)(2,1)}), bf16[4,768,256]{2,1,0:T(8,128)(2,1)}, u32[]{:S(2)}, u32[]{:S(2)}) async-start(bf16[4,768,256]{2,1,0:T(8,128)(2,1)} %bitcast.25), calls=%async_computation.1 | async-start | bytes 3145728 | tf_op jit(solution)/shard_map/all_to_all | solution.py:139
  12.1 9.3 %collective-permute-start = (bf16[3072,128]{1,0:T(8,128)(2,1)S(1)}, bf16[3072,128]{1,0:T(8,128)(2,1)}, u32[]{:S(2)}, u32[]{:S(2)}) collective-permute-start(bf16[3072,128]{1,0:T(8,128)(2,1)S(1)} %copy-done.1), channel_id=1, source_target_pairs={{0,8},{8,0},{1,9},{9,1},{2,10},{10,2},{3,11},{11,3},{4,12},{12,4},... | collective-permute-start | bytes 2359304 | tf_op jit(solution)/shard_map/ppermute | solution.py:88
  14.1 5.4 %collective-permute-start.1 = (bf16[256,128]{1,0:T(8,128)(2,1)S(1)}, bf16[256,128]{1,0:T(8,128)(2,1)S(1)}, u32[]{:S(2)}, u32[]{:S(2)}) collective-permute-start(bf16[256,128]{1,0:T(8,128)(2,1)S(1)} %get-tuple-element.78), channel_id=1, source_target_pairs={{0,1},{1,2},{2,3},{3,4},{4,5},{5,6},{6,7},{9,8},{10,9},{11,10},{12... | collective-permute-start | bytes 196616 | tf_op jit(solution)/shard_map/ppermute | solution.py:86
  15.4 6.0 %collective-permute-start.2 = (bf16[256,128]{1,0:T(8,128)(2,1)S(1)}, bf16[256,128]{1,0:T(8,128)(2,1)S(1)}, u32[]{:S(2)}, u32[]{:S(2)}) collective-permute-start(bf16[256,128]{1,0:T(8,128)(2,1)S(1)} %get-tuple-element.77), channel_id=1, source_target_pairs={{8,1},{9,2},{10,3},{11,4},{12,5},{13,6},{14,7},{1,8},{2,9},{3,10},... | collective-permute-start | bytes 196616 | tf_op jit(solution)/shard_map/ppermute | solution.py:87
  19.5 4.5 %copy-start.2 = (bf16[256,128]{1,0:T(8,128)(2,1)}, bf16[256,128]{1,0:T(8,128)(2,1)S(1)}, u32[]{:S(2)}) copy-start(bf16[256,128]{1,0:T(8,128)(2,1)S(1)} %collective-permute-done.1.own_edge) | copy-start | bytes 196612
  21.4 2.6 %copy-start.3 = (bf16[256,128]{1,0:T(8,128)(2,1)}, bf16[256,128]{1,0:T(8,128)(2,1)S(1)}, u32[]{:S(2)}) copy-start(bf16[256,128]{1,0:T(8,128)(2,1)S(1)} %collective-permute-done.2.other_edge) | copy-start | bytes 196612
  31.4 26.0 %all-to-all-start.2 = ((bf16[32,48,128]{2,1,0:T(8,128)(2,1)}), bf16[32,48,128]{2,1,0:T(8,128)(2,1)S(1)}, u32[]{:S(2)}, u32[]{:S(2)}) async-start(bf16[32,48,128]{2,1,0:T(8,128)(2,1)} %bitcast.5), calls=%async_computation.2 | async-start | bytes 786432 | tf_op jit(solution)/shard_map/all_to_all | solution.py:148
  59.0 31.3 %all-to-all-start.3 = ((bf16[16,48,512]{2,1,0:T(8,128)(2,1)}), bf16[16,48,512]{2,1,0:T(8,128)(2,1)S(1)}, u32[]{:S(2)}, u32[]{:S(2)}) async-start(bf16[16,48,512]{2,1,0:T(8,128)(2,1)} %get-tuple-element.81), calls=%async_computation.3 | async-start | bytes 1572864 | tf_op jit(solution)/shard_map/all_to_all | solution.py:160
  90.9 6.2 %collective-permute-start.3 = (bf16[512,512]{1,0:T(8,128)(2,1)S(1)}, bf16[512,512]{1,0:T(8,128)(2,1)S(1)}, u32[]{:S(2)}, u32[]{:S(2)}) collective-permute-start(bf16[512,512]{1,0:T(8,128)(2,1)S(1)} %convolution_convert_fusion), channel_id=1, source_target_pairs={{0,8},{8,0},{1,9},{9,1},{2,10},{10,2},{3,11},{11,3},{4,12},{12,4},... | collective-permute-start | bytes 1572872 | tf_op jit(solution)/shard_map/ppermute | solution.py:171
  97.3 5.8 %copy-start.8 = (f32[64]{0:T(128)S(1)}, f32[64]{0:T(128)}, u32[]{:S(2)}) copy-start(f32[64]{0:T(128)} %param.14) | copy-start | bytes 772
  97.3 15.2 %copy-start.7 = (f32[256]{0:T(256)S(1)}, f32[256]{0:T(256)}, u32[]{:S(2)}) copy-start(f32[256]{0:T(256)} %param.15) | copy-start | bytes 3076
  98.2 14.3 %all-to-all-start.4 = ((bf16[16,64,256]{2,1,0:T(8,128)(2,1)}), bf16[16,64,256]{2,1,0:T(8,128)(2,1)S(1)}, u32[]{:S(2)}, u32[]{:S(2)}) async-start(bf16[16,64,256]{2,1,0:T(8,128)(2,1)} %bitcast.15), calls=%async_computation.4 | async-start | bytes 1048576 | tf_op jit(solution)/shard_map/all_to_all | solution.py:178
  112.6 0.7 copy-start.4

commit v7 on v6

--- a/solution.py
+++ b/solution.py
@@ -17,7 +17,7 @@
 SIZES = {"yhi": 4, "zhi": 4, "zlo": 2, "core": 2, "ylo": 2, "x": 4}
 STATE = ("yhi", "zhi", "zlo", "core")
 BASIS = ("ylo", "x")
-SHARED = ("core", "zlo")
+SHARED = ("zlo", "core")
 GATHER = ("yhi", "zhi")
 CHIPS = ("zlo",) + GATHER
 SWAP = [(0, 1), (1, 0)]
@@ -136,18 +136,33 @@
     width = store.shape[1]
     lowers = PANELS * width
     uppers = upper_coef.shape[1]
-    upper = lax.all_to_all(upper_coef, SHARED, 0, 0, tiled=True)
-    upper = upper.reshape(2, 2, -1, uppers)
-
+    zlo = lax.axis_index("zlo")
+    quarter = upper_coef.shape[0] // 4
+
+    def mine(flip_zlo, flip_core):
+        start = ((core ^ flip_core) * 2 + (zlo ^ flip_zlo)) * quarter
+        return lax.dynamic_slice_in_dim(upper_coef, start, quarter, 0)
+
+    def from_peer(flip_zlo, flip_core):
+        flip = 2 * flip_zlo + flip_core
+        return lax.ppermute(mine(flip_zlo, flip_core), SHARED, [(i, i ^ flip) for i in range(4)])
+
+    def beside(near, far):
+        low = zlo == 0
+        return jnp.concatenate([jnp.where(low, near, far), jnp.where(low, far, near)], 1)
+
+    kinds = [from_peer(1, 1), from_peer(1, 0), from_peer(0, 1)]
     panels = chip_panels(store, core)
     half = chip_half(False, state, owners, offsets, panels, dipole)
-    half, upper = lax.optimization_barrier((half, upper))
+
+    half, kinds[1] = lax.optimization_barrier((half, kinds[1]))
 
     def scatter(half):
         chips = lax.axis_size(CHIPS)
         return lax.all_to_all(half, CHIPS, 0, 0, tiled=True).reshape(chips, -1, width)
 
     pieces = scatter(half)
+    pieces, kinds[0], kinds[2] = lax.optimization_barrier((pieces, kinds[0], kinds[2]))
     chips_of = owners // 2
     shared = jnp.sum((chips_of[:, None] == chips_of[None, :]).astype(jnp.int32)) > PANELS
     copies = lax.cond(
@@ -159,17 +174,16 @@
     )
     gathered = lax.all_to_all(copies.reshape(-1, lowers), GATHER, 0, 0, tiled=True)
 
-    def beside(kind):
-        blocks = lax.dynamic_index_in_dim(upper, kind, 0, keepdims=False)
-        return jnp.concatenate([blocks[0], blocks[1]], 1)
+    upper_other = beside(kinds[2], kinds[0])
+    upper_own = beside(mine(0, 0), kinds[1])
 
     def share(rhs):
         return lax.dot_general(
             gathered, rhs, (((0,), (0,)), ((), ())), preferred_element_type=F32
         )
 
-    received = lax.ppermute(share(beside(1 - core)).astype(BF16), "core", SWAP)
-    kept, received = lax.optimization_barrier((share(beside(core)), received))
+    received = lax.ppermute(share(upper_other).astype(BF16), "core", SWAP)
+    kept, received = lax.optimization_barrier((share(upper_own), received))
     added = (kept + received.astype(F32)).astype(BF16)
     ranges = lax.axis_size(BASIS)
     sides = [added[:, :uppers], added[:, uppers:]]

time: 114 us -> 118 us (1.035)
  waiting for transfers between devices: 60.1 us -> 44.7 us
  starting transfers between devices: 42 us -> 55.6 us
  other arithmetic: 2.61 us -> 7.46 us
    all_to_all x1, waiting for transfers between devices: 14.2 us -> 0.01 us  [scatter(): lax.all_to_all(half, CHIPS, 0, 0, tiled=True).reshape(chips, -1, width)]
    all_to_all x1 -> x0, starting transfers between devices: 11.5 us -> none  [on_device(): upper = lax.all_to_all(upper_coef, SHARED, 0, 0, tiled=True)]
    ppermute x1 -> x4, waiting for transfers between devices: 0.91 us -> 9.69 us  [the longest x3 8.8 us: from_peer(): lax.ppermute(mine(flip_zlo, flip_core), SHARED, [(i, i ^ flip) for i in r...]
    all_to_all x1 -> x0, waiting for transfers between devices: 7.44 us -> none  [on_device(): upper = lax.all_to_all(upper_coef, SHARED, 0, 0, tiled=True)]
    ppermute x1, starting transfers between devices: 1.97 us -> 8.92 us  [chip_panels(): other = lax.ppermute(store, 'core', SWAP)]
    ppermute x1 -> x4, starting transfers between devices: 4.71 us -> 11.7 us  [the longest x3 7.36 us: from_peer(): lax.ppermute(mine(flip_zlo, flip_core), SHARED, [(i, i ^ flip) for i in r...]
    all_to_all x1, starting transfers between devices: 4.83 us -> 9.44 us  [on_device(): shares = lax.all_to_all(added, BASIS + ('zlo',), 0, 0, tiled=True)]
    select_n x0 -> x2, other arithmetic: none -> 4.06 us  [beside(): jnp.where(low, near, far)]
  transfers between devices with their start and end apart: 8 -> 10, of which waited for: 7 -> 6; matrix products, arithmetic and copies ran while one was open for 3% -> 7% of each run, Pallas kernels for 2% -> 3%
where the time goes in v7:
time: 118 us; the launch traced here: 117 us
  starting transfers between devices  55.6 us (47%)
  waiting for transfers between devices  44.7 us (38%)
  other arithmetic  7.46 us (6%)
  Pallas kernels  5.01 us (4%)
  local copies, waits for them, and re-layouts  1.89 us (2%)
  between operations  1.51 us (1%)
  matrix products  1.19 us (1%)
    all_to_all x1, waiting for transfers between devices, on_device(): lax.all_to_all(copies.reshape(-1, lowers), GATHER, 0, 0, tiled=True)  22.7 us
    all_to_all x1, starting transfers between devices, scatter(): lax.all_to_all(half, CHIPS, 0, 0, tiled=True).reshape(chips, -1, width)  13.3 us
    all_to_all x1, starting transfers between devices, on_device(): shares = lax.all_to_all(added, BASIS + ('zlo',), 0, 0, tiled=True)  9.44 us
    all_to_all x1, waiting for transfers between devices, on_device(): shares = lax.all_to_all(added, BASIS + ('zlo',), 0, 0, tiled=True)  9.39 us
    all_to_all x1, starting transfers between devices, on_device(): lax.all_to_all(copies.reshape(-1, lowers), GATHER, 0, 0, tiled=True)  8.92 us
    ppermute x1, starting transfers between devices, chip_panels(): other = lax.ppermute(store, 'core', SWAP)  8.92 us
    ppermute x3, waiting for transfers between devices, from_peer(): lax.ppermute(mine(flip_zlo, flip_core), SHARED, [(i, i ^ flip) for i in r...  8.8 us
    ppermute x3, starting transfers between devices, from_peer(): lax.ppermute(mine(flip_zlo, flip_core), SHARED, [(i, i ^ flip) for i in r...  7.36 us
  transfers between devices with their start and end apart: 10, of which 6 were waited for; matrix products, arithmetic and copies ran while one was open for 7% of the time, Pallas kernels for 3%

profile of v7, /device:TPU:1, one launch (start us, length us, event | category | flops | bytes accessed | tf_op | source)
XLA Modules:
  0.0 117.4 jit_solution(15945656995601176454)
XLA Ops:
  0.6 0.0 copy-start.1
  0.6 8.9 %collective-permute-start = (bf16[3072,128]{1,0:T(8,128)(2,1)}, bf16[3072,128]{1,0:T(8,128)(2,1)S(1)}, u32[]{:S(2)}, u32[]{:S(2)}) collective-permute-start(bf16[3072,128]{1,0:T(8,128)(2,1)} %own.1), channel_id=1, source_target_pairs={{0,8},{8,0},{1,9},{9,1},{2,10},{10,2},{3,11},{11,3},{4,12},{12,4},... | collective-permute-start | bytes 2359304 | tf_op jit(solution)/shard_map/ppermute | solution.py:88
  9.6 1.0 constant_dynamic-slice_fusion.2
  10.6 1.9 %collective-permute-start.3 = (bf16[768,256]{1,0:T(8,128)(2,1)S(1)}, bf16[768,256]{1,0:T(8,128)(2,1)S(1)}, u32[]{:S(2)}, u32[]{:S(2)}) collective-permute-start(bf16[768,256]{1,0:T(8,128)(2,1)S(1)} %constant_dynamic-slice_fusion.2), channel_id=1, source_target_pairs={{0,16},{8,24},{16,0},{24,8},{1,17},{9,25},{17,1},{25,9},{2,18},{10... | collective-permute-start | bytes 1179656 | tf_op jit(solution)/shard_map/ppermute | solution.py:148
  12.5 0.9 broadcast_select_fusion.4
  13.4 1.3 %collective-permute-start.1 = (bf16[256,128]{1,0:T(8,128)(2,1)S(1)}, bf16[256,128]{1,0:T(8,128)(2,1)S(1)}, u32[]{:S(2)}, u32[]{:S(2)}) collective-permute-start(bf16[256,128]{1,0:T(8,128)(2,1)S(1)} %get-tuple-element.86), channel_id=1, source_target_pairs={{0,1},{1,2},{2,3},{3,4},{4,5},{5,6},{6,7},{9,8},{10,9},{11,10},{12... | collective-permute-start | bytes 196616 | tf_op jit(solution)/shard_map/ppermute | solution.py:86
  14.7 2.1 %collective-permute-start.2 = (bf16[256,128]{1,0:T(8,128)(2,1)S(1)}, bf16[256,128]{1,0:T(8,128)(2,1)S(1)}, u32[]{:S(2)}, u32[]{:S(2)}) collective-permute-start(bf16[256,128]{1,0:T(8,128)(2,1)S(1)} %get-tuple-element.85), channel_id=1, source_target_pairs={{8,1},{9,2},{10,3},{11,4},{12,5},{13,6},{14,7},{1,8},{2,9},{3,10},... | collective-permute-start | bytes 196616 | tf_op jit(solution)/shard_map/ppermute | solution.py:87
  16.9 0.8 copy.15.offsets_ref
  17.6 1.1 collective-permute-done.1.own_edge
  18.7 1.9 %collective-permute-done.2.other_edge = bf16[256,128]{1,0:T(8,128)(2,1)S(1)} collective-permute-done((bf16[256,128]{1,0:T(8,128)(2,1)S(1)}, bf16[256,128]{1,0:T(8,128)(2,1)S(1)}, u32[]{:S(2)}, u32[]{:S(2)}) %collective-permute-start.2) | collective-permute-done | bytes 65568 | tf_op jit(solution)/shard_map/ppermute | solution.py:87
  20.6 0.0 collective-permute-done.other
  20.6 0.0 copy-done.1
  20.6 3.4 %shard_map.86 = bf16[1536,128]{1,0:T(8,128)(2,1)} custom-call(s32[1]{0:T(128)} %bitcast.2.state_ref, s32[4]{0:T(128)} %owners_ref.1, s32[24,3]{1,0:T(8,128)S(1)} %copy.15.offsets_ref, bf16[3072,128]{1,0:T(8,128)(2,1)S(1)} %copy-done.1, bf16[3072,128]{1,0:T(8,128)(2,1)S(1)} %collective-permute-done.other, ...), custom_call_target="tpu_custom_call" | custom-call | flops 150994944 | bytes 6291456 | tf_op jit(solution)/shard_map/pallas_call | solution.py:95
  24.0 0.0 copy-done.6
  24.0 0.0 copy-done.7
  24.0 0.0 copy-done.2
  24.0 0.0 collective-permute-done.3
  24.0 0.0 copy-start.3
  24.0 13.3 %all-to-all-start.1 = ((bf16[32,48,128]{2,1,0:T(8,128)(2,1)}), bf16[32,48,128]{2,1,0:T(8,128)(2,1)S(1)}, u32[]{:S(2)}, u32[]{:S(2)}) async-start(bf16[32,48,128]{2,1,0:T(8,128)(2,1)} %bitcast.3), calls=%async_computation.1 | async-start | bytes 786432 | tf_op jit(solution)/shard_map/all_to_all | solution.py:162
  37.3 0.0 copy-start.9
  37.4 0.0 copy-start
  37.4 2.9 %broadcast_select_fusion.3 = (bf16[768,256]{1,0:T(8,128)(2,1)}, bf16[768,256]{1,0:T(8,128)(2,1)}, bf16[768,256]{1,0:T(8,128)(2,1)}, bf16[768,256]{1,0:T(8,128)(2,1)}) fusion(bf16[768,256]{1,0:T(8,128)(2,1)} %copy-done.3, pred[]{:T(512)S(6)} %eq.24, bf16[3072,256]{1,0:T(8,128)(2,1)} %param.9, s32[]{:T(128)S(6)} %select_n.57, s32[]{:T(128)S(6)} %select_n.54, ...), kind=kLoop, calls=%fused_computation.14 | loop fusion | flops 393216 | bytes 3145741 | tf_op jit(solution)/shard_map/jit(_where)/select_n | solution.py:152
  40.3 1.9 %collective-permute-start.4 = (bf16[768,256]{1,0:T(8,128)(2,1)}, bf16[768,256]{1,0:T(8,128)(2,1)}, u32[]{:S(2)}, u32[]{:S(2)}) collective-permute-start(bf16[768,256]{1,0:T(8,128)(2,1)} %get-tuple-element.81), channel_id=1, source_target_pairs={{0,24},{8,16},{16,8},{24,0},{1,25},{9,17},{17,9},{25,1},{2,26},{10... | collective-permute-start | bytes 1179656 | tf_op jit(solution)/shard_map/ppermute | solution.py:148
  42.2 3.5 %collective-permute-start.5 = (bf16[768,256]{1,0:T(8,128)(2,1)}, bf16[768,256]{1,0:T(8,128)(2,1)}, u32[]{:S(2)}, u32[]{:S(2)}) collective-permute-start(bf16[768,256]{1,0:T(8,128)(2,1)} %get-tuple-element.82), channel_id=1, source_target_pairs={{0,8},{8,0},{16,24},{24,16},{1,9},{9,1},{17,25},{25,17},{2,10},{10... | collective-permute-start | bytes 1179656 | tf_op jit(solution)/shard_map/ppermute | solution.py:148
  45.7 0.7 convert_reduce_fusion.1
  47.0 8.8 %collective-permute-done.4 = bf16[768,256]{1,0:T(8,128)(2,1)} collective-permute-done((bf16[768,256]{1,0:T(8,128)(2,1)}, bf16[768,256]{1,0:T(8,128)(2,1)}, u32[]{:S(2)}, u32[]{:S(2)}) %collective-permute-start.4) | collective-permute-done | bytes 393248 | tf_op jit(solution)/shard_map/ppermute | solution.py:148
  55.8 0.0 collective-permute-done.5
  55.8 0.0 all-to-all-done.1
  55.8 1.6 %conditional.1 = (bf16[16,48,512]{2,1,0:T(8,128)(2,1)}) conditional(s32[]{:T(128)} %convert_element_type.19, (s32[4]{0:T(128)S(1)}, bf16[32,48,128]{2,1,0:T(8,128)(2,1)S(1)}) %tuple.39, (s32[]{:T(128)}, s32[4]{0:T(128)S(1)}, s32[24,3]{0,1:T(4,128)}, bf16[3072,128]{1,0:T(8,128)(2,1)S(1)}, bf16[3072,128]{1,0:T(8,128)(2,1)}, ...), branch_computations={%region_1.2_spmd, %region_2.3_spmd} | conditional | flops 150994944 | bytes 8127048 | solution.py:168
  55.8 1.6 %branch_0_fun.1 = bf16[16,48,512]{2,1,0:T(8,128)(2,1)} custom-call(s32[4]{0:T(128)S(1)} %get-tuple-element.12.owners_ref, bf16[32,48,128]{2,1,0:T(8,128)(2,1)S(1)} %get-tuple-element.26.pieces.seconds, bf16[32,48,128]{2,1,0:T(8,128)(2,1)S(1)} %get-tuple-element.26.pieces.seconds), custom_call_target="tpu_custom_call" | custom-call | bytes 1048576 | tf_op jit(solution)/shard_map/cond/branch_0_fun/pallas_call | solution.py:122
  57.5 8.9 %all-to-all-start.2 = ((bf16[16,48,512]{2,1,0:T(8,128)(2,1)}), bf16[16,48,512]{2,1,0:T(8,128)(2,1)S(1)}, u32[]{:S(2)}, u32[]{:S(2)}) async-start(bf16[16,48,512]{2,1,0:T(8,128)(2,1)} %get-tuple-element.89), calls=%async_computation.2 | async-start | bytes 1572864 | tf_op jit(solution)/shard_map/all_to_all | solution.py:175
  66.4 1.2 broadcast_select_fusion.1
  67.6 22.7 %all-to-all-done.2 = bf16[16,48,512]{2,1,0:T(8,128)(2,1)S(1)} async-done(((bf16[16,48,512]{2,1,0:T(8,128)(2,1)}), bf16[16,48,512]{2,1,0:T(8,128)(2,1)S(1)}, u32[]{:S(2)}, u32[]{:S(2)}) %all-to-all-start.2) | async-done | bytes 786464 | tf_op jit(solution)/shard_map/all_to_all | solution.py:175
  90.2 0.6 convolution_convert_fusion
  90.8 4.3 %collective-permute-start.6 = (bf16[512,512]{1,0:T(8,128)(2,1)S(1)}, bf16[512,512]{1,0:T(8,128)(2,1)S(1)}, u32[]{:S(2)}, u32[]{:S(2)}) collective-permute-start(bf16[512,512]{1,0:T(8,128)(2,1)S(1)} %convolution_convert_fusion), channel_id=1, source_target_pairs={{0,8},{8,0},{1,9},{9,1},{2,10},{10,2},{3,11},{11,3},{4,12},{12,4},... | collective-permute-start | bytes 1572872 | tf_op jit(solution)/shard_map/ppermute | solution.py:185
  95.1 0.0 copy-done.4
  95.1 0.0 copy-done.5
  95.1 0.6 fusion
  95.7 0.9 collective-permute-done.6
  96.6 0.2 add_convert_fusion
  96.8 0.0 copy-start.11
  96.8 0.0 copy-start.10
  96.9 0.8 pad_maximum_fusion
  97.7 9.4 %all-to-all-start.3 = ((bf16[16,64,256]{2,1,0:T(8,128)(2,1)}), bf16[16,64,256]{2,1,0:T(8,128)(2,1)S(1)}, u32[]{:S(2)}, u32[]{:S(2)}) async-start(bf16[16,64,256]{2,1,0:T(8,128)(2,1)} %bitcast.9), calls=%async_computation.3 | async-start | bytes 1048576 | tf_op jit(solution)/shard_map/all_to_all | solution.py:192
  107.2 9.4 %all-to-all-done.3 = bf16[16,64,256]{2,1,0:T(8,128)(2,1)S(1)} async-done(((bf16[16,64,256]{2,1,0:T(8,128)(2,1)}), bf16[16,64,256]{2,1,0:T(8,128)(2,1)S(1)}, u32[]{:S(2)}, u32[]{:S(2)}) %all-to-all-start.3) | async-done | bytes 524320 | tf_op jit(solution)/shard_map/all_to_all | solution.py:192
  116.6 0.1 convert_reduce_fusion
  116.7 0.0 copy-start.8
  116.7 0.7 fusion.8
  (14 shorter events, 0.1 us)
Async XLA Ops:
  0.6 20.0 %copy-start.1 = (bf16[3072,128]{1,0:T(8,128)(2,1)S(1)}, bf16[3072,128]{1,0:T(8,128)(2,1)}, u32[]{:S(2)}) copy-start(bf16[3072,128]{1,0:T(8,128)(2,1)} %own.1) | copy-start | bytes 2359300
  0.6 20.0 %collective-permute-start = (bf16[3072,128]{1,0:T(8,128)(2,1)}, bf16[3072,128]{1,0:T(8,128)(2,1)S(1)}, u32[]{:S(2)}, u32[]{:S(2)}) collective-permute-start(bf16[3072,128]{1,0:T(8,128)(2,1)} %own.1), channel_id=1, source_target_pairs={{0,8},{8,0},{1,9},{9,1},{2,10},{10,2},{3,11},{11,3},{4,12},{12,4},... | collective-permute-start | bytes 2359304 | tf_op jit(solution)/shard_map/ppermute | solution.py:88
  10.6 13.4 %collective-permute-start.3 = (bf16[768,256]{1,0:T(8,128)(2,1)S(1)}, bf16[768,256]{1,0:T(8,128)(2,1)S(1)}, u32[]{:S(2)}, u32[]{:S(2)}) collective-permute-start(bf16[768,256]{1,0:T(8,128)(2,1)S(1)} %constant_dynamic-slice_fusion.2), channel_id=1, source_target_pairs={{0,16},{8,24},{16,0},{24,8},{1,17},{9,25},{17,1},{25,9},{2,18},{10... | collective-permute-start | bytes 1179656 | tf_op jit(solution)/shard_map/ppermute | solution.py:148
  13.4 5.3 %collective-permute-start.1 = (bf16[256,128]{1,0:T(8,128)(2,1)S(1)}, bf16[256,128]{1,0:T(8,128)(2,1)S(1)}, u32[]{:S(2)}, u32[]{:S(2)}) collective-permute-start(bf16[256,128]{1,0:T(8,128)(2,1)S(1)} %get-tuple-element.86), channel_id=1, source_target_pairs={{0,1},{1,2},{2,3},{3,4},{4,5},{5,6},{6,7},{9,8},{10,9},{11,10},{12... | collective-permute-start | bytes 196616 | tf_op jit(solution)/shard_map/ppermute | solution.py:86
  14.7 5.9 %collective-permute-start.2 = (bf16[256,128]{1,0:T(8,128)(2,1)S(1)}, bf16[256,128]{1,0:T(8,128)(2,1)S(1)}, u32[]{:S(2)}, u32[]{:S(2)}) collective-permute-start(bf16[256,128]{1,0:T(8,128)(2,1)S(1)} %get-tuple-element.85), channel_id=1, source_target_pairs={{8,1},{9,2},{10,3},{11,4},{12,5},{13,6},{14,7},{1,8},{2,9},{3,10},... | collective-permute-start | bytes 196616 | tf_op jit(solution)/shard_map/ppermute | solution.py:87
  18.7 5.3 %copy-start.6 = (bf16[256,128]{1,0:T(8,128)(2,1)}, bf16[256,128]{1,0:T(8,128)(2,1)S(1)}, u32[]{:S(2)}) copy-start(bf16[256,128]{1,0:T(8,128)(2,1)S(1)} %collective-permute-done.1.own_edge) | copy-start | bytes 196612
  20.6 3.4 %copy-start.7 = (bf16[256,128]{1,0:T(8,128)(2,1)}, bf16[256,128]{1,0:T(8,128)(2,1)S(1)}, u32[]{:S(2)}) copy-start(bf16[256,128]{1,0:T(8,128)(2,1)S(1)} %collective-permute-done.2.other_edge) | copy-start | bytes 196612
  20.6 3.4 %copy-start.2 = (bf16[3072,128]{1,0:T(8,128)(2,1)}, bf16[3072,128]{1,0:T(8,128)(2,1)S(1)}, u32[]{:S(2)}) copy-start(bf16[3072,128]{1,0:T(8,128)(2,1)S(1)} %collective-permute-done.other) | copy-start | bytes 2359300
  24.0 13.3 %copy-start.3 = (bf16[768,256]{1,0:T(8,128)(2,1)}, bf16[768,256]{1,0:T(8,128)(2,1)S(1)}, u32[]{:S(2)}) copy-start(bf16[768,256]{1,0:T(8,128)(2,1)S(1)} %collective-permute-done.3) | copy-start | bytes 1179652
  24.0 31.8 %all-to-all-start.1 = ((bf16[32,48,128]{2,1,0:T(8,128)(2,1)}), bf16[32,48,128]{2,1,0:T(8,128)(2,1)S(1)}, u32[]{:S(2)}, u32[]{:S(2)}) async-start(bf16[32,48,128]{2,1,0:T(8,128)(2,1)} %bitcast.3), calls=%async_computation.1 | async-start | bytes 786432 | tf_op jit(solution)/shard_map/all_to_all | solution.py:162
  37.3 8.4 %copy-start.9 = (s32[4]{0:T(128)S(1)}, s32[4]{0:T(128)}, u32[]{:S(2)}) copy-start(s32[4]{0:T(128)} %owners_ref.1) | copy-start | bytes 52
  37.4 18.5 %copy-start = (bf16[24,3,128,128]{3,2,1,0:T(8,128)(2,1)S(1)}, bf16[24,3,128,128]{3,2,1,0:T(8,128)(2,1)}, u32[]{:S(2)}) copy-start(bf16[24,3,128,128]{3,2,1,0:T(8,128)(2,1)} %dipole.1) | copy-start | bytes 7077892
  40.3 15.5 %collective-permute-start.4 = (bf16[768,256]{1,0:T(8,128)(2,1)}, bf16[768,256]{1,0:T(8,128)(2,1)}, u32[]{:S(2)}, u32[]{:S(2)}) collective-permute-start(bf16[768,256]{1,0:T(8,128)(2,1)} %get-tuple-element.81), channel_id=1, source_target_pairs={{0,24},{8,16},{16,8},{24,0},{1,25},{9,17},{17,9},{25,1},{2,26},{10... | collective-permute-start | bytes 1179656 | tf_op jit(solution)/shard_map/ppermute | solution.py:148
  42.2 13.6 %collective-permute-start.5 = (bf16[768,256]{1,0:T(8,128)(2,1)}, bf16[768,256]{1,0:T(8,128)(2,1)}, u32[]{:S(2)}, u32[]{:S(2)}) collective-permute-start(bf16[768,256]{1,0:T(8,128)(2,1)} %get-tuple-element.82), channel_id=1, source_target_pairs={{0,8},{8,0},{16,24},{24,16},{1,9},{9,1},{17,25},{25,17},{2,10},{10... | collective-permute-start | bytes 1179656 | tf_op jit(solution)/shard_map/ppermute | solution.py:148
  57.5 32.8 %all-to-all-start.2 = ((bf16[16,48,512]{2,1,0:T(8,128)(2,1)}), bf16[16,48,512]{2,1,0:T(8,128)(2,1)S(1)}, u32[]{:S(2)}, u32[]{:S(2)}) async-start(bf16[16,48,512]{2,1,0:T(8,128)(2,1)} %get-tuple-element.89), calls=%async_computation.2 | async-start | bytes 1572864 | tf_op jit(solution)/shard_map/all_to_all | solution.py:175
  90.2 4.9 %copy-start.4 = (bf16[768,256]{1,0:T(8,128)(2,1)S(1)}, bf16[768,256]{1,0:T(8,128)(2,1)}, u32[]{:S(2)}) copy-start(bf16[768,256]{1,0:T(8,128)(2,1)} %get-tuple-element.79) | copy-start | bytes 1179652
  90.2 4.9 %copy-start.5 = (bf16[768,256]{1,0:T(8,128)(2,1)S(1)}, bf16[768,256]{1,0:T(8,128)(2,1)}, u32[]{:S(2)}) copy-start(bf16[768,256]{1,0:T(8,128)(2,1)} %get-tuple-element.80) | copy-start | bytes 1179652
  90.8 5.8 %collective-permute-start.6 = (bf16[512,512]{1,0:T(8,128)(2,1)S(1)}, bf16[512,512]{1,0:T(8,128)(2,1)S(1)}, u32[]{:S(2)}, u32[]{:S(2)}) collective-permute-start(bf16[512,512]{1,0:T(8,128)(2,1)S(1)} %convolution_convert_fusion), channel_id=1, source_target_pairs={{0,8},{8,0},{1,9},{9,1},{2,10},{10,2},{3,11},{11,3},{4,12},{12,4},... | collective-permute-start | bytes 1572872 | tf_op jit(solution)/shard_map/ppermute | solution.py:185
  96.8 10.4 %copy-start.11 = (f32[64]{0:T(128)S(1)}, f32[64]{0:T(128)}, u32[]{:S(2)}) copy-start(f32[64]{0:T(128)} %param.14) | copy-start | bytes 772
  96.8 19.8 %copy-start.10 = (f32[256]{0:T(256)S(1)}, f32[256]{0:T(256)}, u32[]{:S(2)}) copy-start(f32[256]{0:T(256)} %param.15) | copy-start | bytes 3076
  97.7 18.9 %all-to-all-start.3 = ((bf16[16,64,256]{2,1,0:T(8,128)(2,1)}), bf16[16,64,256]{2,1,0:T(8,128)(2,1)S(1)}, u32[]{:S(2)}, u32[]{:S(2)}) async-start(bf16[16,64,256]{2,1,0:T(8,128)(2,1)} %bitcast.9), calls=%async_computation.3 | async-start | bytes 1048576 | tf_op jit(solution)/shard_map/all_to_all | solution.py:192
  116.7 0.7 copy-start.8

commit v8 on v7

--- a/solution.py
+++ b/solution.py
@@ -162,7 +162,7 @@
         return lax.all_to_all(half, CHIPS, 0, 0, tiled=True).reshape(chips, -1, width)
 
     pieces = scatter(half)
-    pieces, kinds[0], kinds[2] = lax.optimization_barrier((pieces, kinds[0], kinds[2]))
+    pieces, kinds[2] = lax.optimization_barrier((pieces, kinds[2]))
     chips_of = owners // 2
     shared = jnp.sum((chips_of[:, None] == chips_of[None, :]).astype(jnp.int32)) > PANELS
     copies = lax.cond(

time: 118 us -> 114 us (0.966)
  starting transfers between devices: 55.6 us -> 45.9 us
  waiting for transfers between devices: 44.7 us -> 49.6 us
  local copies, waits for them, and re-layouts: 1.89 us -> 3.96 us
    all_to_all x1, waiting for transfers between devices: 22.7 us -> 0.01 us  [on_device(): lax.all_to_all(copies.reshape(-1, lowers), GATHER, 0, 0, tiled=True)]
    ppermute x3, waiting for transfers between devices: 8.8 us -> 25.3 us  [from_peer(): lax.ppermute(mine(flip_zlo, flip_core), SHARED, [(i, i ^ flip) for i in r...]
    all_to_all x1, waiting for transfers between devices: 0.01 us -> 11.3 us  [scatter(): lax.all_to_all(half, CHIPS, 0, 0, tiled=True).reshape(chips, -1, width)]
    all_to_all x1, starting transfers between devices: 8.92 us -> 4.31 us  [on_device(): lax.all_to_all(copies.reshape(-1, lowers), GATHER, 0, 0, tiled=True)]
    all_to_all x1, starting transfers between devices: 9.44 us -> 7.06 us  [on_device(): shares = lax.all_to_all(added, BASIS + ('zlo',), 0, 0, tiled=True)]
    ppermute x1, starting transfers between devices: 4.3 us -> 2.31 us  [on_device(): received = lax.ppermute(share(upper_other).astype(BF16), 'core', SWAP)]
    select_n x2, other arithmetic: 4.06 us -> 2.32 us  [beside(): jnp.where(low, near, far)]
    dynamic_slice x1, local copies, waits for them, and re-layouts: 1.03 us -> 2.24 us  [mine(): return lax.dynamic_slice_in_dim(upper_coef, start, quarter, 0)]
where the time goes in v8:
time: 114 us; the launch traced here: 113 us
  waiting for transfers between devices  49.6 us (44%)
  starting transfers between devices  45.9 us (40%)
  other arithmetic  6.41 us (6%)
  Pallas kernels  4.43 us (4%)
  local copies, waits for them, and re-layouts  3.96 us (3%)
  between operations  1.55 us (1%)
  matrix products  1.19 us (1%)
    ppermute x3, waiting for transfers between devices, from_peer(): lax.ppermute(mine(flip_zlo, flip_core), SHARED, [(i, i ^ flip) for i in r...  25.3 us
    all_to_all x1, starting transfers between devices, scatter(): lax.all_to_all(half, CHIPS, 0, 0, tiled=True).reshape(chips, -1, width)  13 us
    all_to_all x1, waiting for transfers between devices, scatter(): lax.all_to_all(half, CHIPS, 0, 0, tiled=True).reshape(chips, -1, width)  11.3 us
    all_to_all x1, waiting for transfers between devices, on_device(): shares = lax.all_to_all(added, BASIS + ('zlo',), 0, 0, tiled=True)  9.65 us
    ppermute x1, starting transfers between devices, chip_panels(): other = lax.ppermute(store, 'core', SWAP)  8.92 us
    all_to_all x1, starting transfers between devices, on_device(): shares = lax.all_to_all(added, BASIS + ('zlo',), 0, 0, tiled=True)  7.06 us
    ppermute x3, starting transfers between devices, from_peer(): lax.ppermute(mine(flip_zlo, flip_core), SHARED, [(i, i ^ flip) for i in r...  6.92 us
    all_to_all x1, starting transfers between devices, on_device(): lax.all_to_all(copies.reshape(-1, lowers), GATHER, 0, 0, tiled=True)  4.31 us
  transfers between devices with their start and end apart: 10, of which 6 were waited for; matrix products, arithmetic and copies ran while one was open for 7% of the time, Pallas kernels for 3%

profile of v8, /device:TPU:1, one launch (start us, length us, event | category | flops | bytes accessed | tf_op | source)
XLA Modules:
  0.0 113.0 jit_solution(17974282443633227382)
XLA Ops:
  0.6 0.0 copy-start.5
  0.6 0.0 copy-start
  0.6 8.9 %collective-permute-start = (bf16[3072,128]{1,0:T(8,128)(2,1)}, bf16[3072,128]{1,0:T(8,128)(2,1)S(1)}, u32[]{:S(2)}, u32[]{:S(2)}) collective-permute-start(bf16[3072,128]{1,0:T(8,128)(2,1)} %own.1), channel_id=1, source_target_pairs={{0,8},{8,0},{1,9},{9,1},{2,10},{10,2},{3,11},{11,3},{4,12},{12,4},... | collective-permute-start | bytes 2359304 | tf_op jit(solution)/shard_map/ppermute | solution.py:88
  9.6 2.2 %constant_dynamic-slice_fusion = (bf16[768,256]{1,0:T(8,128)(2,1)}, bf16[768,256]{1,0:T(8,128)(2,1)}, bf16[768,256]{1,0:T(8,128)(2,1)S(1)}) fusion(bf16[3072,256]{1,0:T(8,128)(2,1)} %param.9, s32[]{:T(128)S(6)} %select_n.59, s32[]{:T(128)S(6)} %select_n.54, s32[]{:T(128)S(6)} %select_n.53), kind=kLoop, calls=%fused_computation.28 | loop fusion | bytes 2359308 | tf_op jit(solution)/shard_map/dynamic_slice | solution.py:144
  11.8 1.9 %collective-permute-start.3 = (bf16[768,256]{1,0:T(8,128)(2,1)S(1)}, bf16[768,256]{1,0:T(8,128)(2,1)}, u32[]{:S(2)}, u32[]{:S(2)}) collective-permute-start(bf16[768,256]{1,0:T(8,128)(2,1)S(1)} %get-tuple-element.81), channel_id=1, source_target_pairs={{0,16},{8,24},{16,0},{24,8},{1,17},{9,25},{17,1},{25,9},{2,18},{10... | collective-permute-start | bytes 1179656 | tf_op jit(solution)/shard_map/ppermute | solution.py:148
  13.8 1.5 %broadcast_select_fusion.4 = (bf16[256,128]{1,0:T(8,128)(2,1)}, bf16[256,128]{1,0:T(8,128)(2,1)}) fusion(pred[]{:T(512)S(6)} %eq.23, bf16[3072,128]{1,0:T(8,128)(2,1)} %own.1), kind=kLoop, calls=%fused_computation.21 | loop fusion | flops 65536 | bytes 262145 | tf_op jit(solution)/shard_map/jit(_where)/select_n | solution.py:87
  15.3 1.3 %collective-permute-start.1 = (bf16[256,128]{1,0:T(8,128)(2,1)}, bf16[256,128]{1,0:T(8,128)(2,1)}, u32[]{:S(2)}, u32[]{:S(2)}) collective-permute-start(bf16[256,128]{1,0:T(8,128)(2,1)} %get-tuple-element.85), channel_id=1, source_target_pairs={{0,1},{1,2},{2,3},{3,4},{4,5},{5,6},{6,7},{9,8},{10,9},{11,10},{12... | collective-permute-start | bytes 196616 | tf_op jit(solution)/shard_map/ppermute | solution.py:86
  16.6 2.1 %collective-permute-start.2 = (bf16[256,128]{1,0:T(8,128)(2,1)}, bf16[256,128]{1,0:T(8,128)(2,1)}, u32[]{:S(2)}, u32[]{:S(2)}) collective-permute-start(bf16[256,128]{1,0:T(8,128)(2,1)} %get-tuple-element.84), channel_id=1, source_target_pairs={{8,1},{9,2},{10,3},{11,4},{12,5},{13,6},{14,7},{1,8},{2,9},{3,10},... | collective-permute-start | bytes 196616 | tf_op jit(solution)/shard_map/ppermute | solution.py:87
  18.7 0.8 copy.15.offsets_ref
  19.5 1.4 %collective-permute-done.1.own_edge = bf16[256,128]{1,0:T(8,128)(2,1)} collective-permute-done((bf16[256,128]{1,0:T(8,128)(2,1)}, bf16[256,128]{1,0:T(8,128)(2,1)}, u32[]{:S(2)}, u32[]{:S(2)}) %collective-permute-start.1) | collective-permute-done | bytes 65568 | tf_op jit(solution)/shard_map/ppermute | solution.py:86
  20.9 1.9 %collective-permute-done.2.other_edge = bf16[256,128]{1,0:T(8,128)(2,1)} collective-permute-done((bf16[256,128]{1,0:T(8,128)(2,1)}, bf16[256,128]{1,0:T(8,128)(2,1)}, u32[]{:S(2)}, u32[]{:S(2)}) %collective-permute-start.2) | collective-permute-done | bytes 65568 | tf_op jit(solution)/shard_map/ppermute | solution.py:87
  22.8 0.0 collective-permute-done.other
  22.8 0.9 copy-done.2
  23.7 0.0 copy-done.5
  23.7 0.0 copy-done
  23.7 2.8 %shard_map.86 = bf16[1536,128]{1,0:T(8,128)(2,1)} custom-call(s32[1]{0:T(128)} %bitcast.2.state_ref, s32[4]{0:T(128)S(1)} %copy-done.5, s32[24,3]{1,0:T(8,128)S(1)} %copy.15.offsets_ref, bf16[3072,128]{1,0:T(8,128)(2,1)} %own.1, bf16[3072,128]{1,0:T(8,128)(2,1)} %copy-done.2, bf16[256,128]{1,0:T(8,128)(2,1)} %collective-permute-done.1.own_edge, ...), custom_call_target="tpu_custom_call" | custom-call | flops 150994944 | bytes 6291456 | tf_op jit(solution)/shard_map/pallas_call | solution.py:95
  26.5 0.0 collective-permute-done.3
  26.5 13.0 %all-to-all-start.1 = ((bf16[32,48,128]{2,1,0:T(8,128)(2,1)}), bf16[32,48,128]{2,1,0:T(8,128)(2,1)S(1)}, u32[]{:S(2)}, u32[]{:S(2)}) async-start(bf16[32,48,128]{2,1,0:T(8,128)(2,1)} %bitcast.3), calls=%async_computation.1 | async-start | bytes 786432 | tf_op jit(solution)/shard_map/all_to_all | solution.py:162
  39.5 1.9 %collective-permute-start.4 = (bf16[768,256]{1,0:T(8,128)(2,1)}, bf16[768,256]{1,0:T(8,128)(2,1)}, u32[]{:S(2)}, u32[]{:S(2)}) collective-permute-start(bf16[768,256]{1,0:T(8,128)(2,1)} %get-tuple-element.80), channel_id=1, source_target_pairs={{0,8},{8,0},{16,24},{24,16},{1,9},{9,1},{17,25},{25,17},{2,10},{10... | collective-permute-start | bytes 1179656 | tf_op jit(solution)/shard_map/ppermute | solution.py:148
  41.4 0.7 convert_reduce_fusion.1
  42.8 0.7 collective-permute-done.4
  43.5 11.3 %all-to-all-done.1 = bf16[32,48,128]{2,1,0:T(8,128)(2,1)S(1)} async-done(((bf16[32,48,128]{2,1,0:T(8,128)(2,1)}), bf16[32,48,128]{2,1,0:T(8,128)(2,1)S(1)}, u32[]{:S(2)}, u32[]{:S(2)}) %all-to-all-start.1) | async-done | bytes 393248 | tf_op jit(solution)/shard_map/all_to_all | solution.py:162
  54.7 0.0 copy-done.1
  54.7 1.6 %conditional.1 = (bf16[16,48,512]{2,1,0:T(8,128)(2,1)}) conditional(s32[]{:T(128)} %convert_element_type.19, (s32[4]{0:T(128)S(1)}, bf16[32,48,128]{2,1,0:T(8,128)(2,1)S(1)}) %tuple.37, (s32[]{:T(128)}, s32[4]{0:T(128)S(1)}, s32[24,3]{0,1:T(4,128)}, bf16[3072,128]{1,0:T(8,128)(2,1)S(1)}, bf16[3072,128]{1,0:T(8,128)(2,1)}, ...), branch_computations={%region_1.2_spmd, %region_2.3_spmd} | conditional | flops 150994944 | bytes 8127048 | solution.py:168
  54.7 1.6 %branch_0_fun.1 = bf16[16,48,512]{2,1,0:T(8,128)(2,1)} custom-call(s32[4]{0:T(128)S(1)} %get-tuple-element.12.owners_ref, bf16[32,48,128]{2,1,0:T(8,128)(2,1)S(1)} %get-tuple-element.26.pieces.seconds, bf16[32,48,128]{2,1,0:T(8,128)(2,1)S(1)} %get-tuple-element.26.pieces.seconds), custom_call_target="tpu_custom_call" | custom-call | bytes 1048576 | tf_op jit(solution)/shard_map/cond/branch_0_fun/pallas_call | solution.py:122
  56.3 4.3 %all-to-all-start.2 = ((bf16[16,48,512]{2,1,0:T(8,128)(2,1)}), bf16[16,48,512]{2,1,0:T(8,128)(2,1)S(1)}, u32[]{:S(2)}, u32[]{:S(2)}) async-start(bf16[16,48,512]{2,1,0:T(8,128)(2,1)} %get-tuple-element.88), calls=%async_computation.2 | async-start | bytes 1572864 | tf_op jit(solution)/shard_map/all_to_all | solution.py:175
  60.7 0.0 copy-done.3
  60.7 3.1 %collective-permute-start.5 = (bf16[768,256]{1,0:T(8,128)(2,1)S(1)}, bf16[768,256]{1,0:T(8,128)(2,1)S(1)}, u32[]{:S(2)}, u32[]{:S(2)}) collective-permute-start(bf16[768,256]{1,0:T(8,128)(2,1)S(1)} %copy-done.3), channel_id=1, source_target_pairs={{0,24},{8,16},{16,8},{24,0},{1,25},{9,17},{17,9},{25,1},{2,26},{10... | collective-permute-start | bytes 1179656 | tf_op jit(solution)/shard_map/ppermute | solution.py:148
  63.8 24.7 %collective-permute-done.5 = bf16[768,256]{1,0:T(8,128)(2,1)S(1)} collective-permute-done((bf16[768,256]{1,0:T(8,128)(2,1)S(1)}, bf16[768,256]{1,0:T(8,128)(2,1)S(1)}, u32[]{:S(2)}, u32[]{:S(2)}) %collective-permute-start.5) | collective-permute-done | bytes 393248 | tf_op jit(solution)/shard_map/ppermute | solution.py:148
  88.4 1.1 broadcast_select_fusion.1
  89.5 0.0 all-to-all-done.2
  89.5 0.6 convolution_convert_fusion
  90.1 2.3 %collective-permute-start.6 = (bf16[512,512]{1,0:T(8,128)(2,1)S(1)}, bf16[512,512]{1,0:T(8,128)(2,1)S(1)}, u32[]{:S(2)}, u32[]{:S(2)}) collective-permute-start(bf16[512,512]{1,0:T(8,128)(2,1)S(1)} %convolution_convert_fusion), channel_id=1, source_target_pairs={{0,8},{8,0},{1,9},{9,1},{2,10},{10,2},{3,11},{11,3},{4,12},{12,4},... | collective-permute-start | bytes 1572872 | tf_op jit(solution)/shard_map/ppermute | solution.py:185
  92.4 1.3 %broadcast_select_fusion.3 = (bf16[768,256]{1,0:T(8,128)(2,1)S(1)}, bf16[768,256]{1,0:T(8,128)(2,1)S(1)}) fusion(bf16[768,256]{1,0:T(8,128)(2,1)} %collective-permute-done.3, pred[]{:T(512)S(6)} %eq.24, bf16[3072,256]{1,0:T(8,128)(2,1)} %param.9, s32[]{:T(128)S(6)} %select_n.56), kind=kLoop, calls=%fused_computation.14 | loop fusion | flops 393216 | bytes 1572869 | tf_op jit(solution)/shard_map/jit(_where)/select_n | solution.py:152
  93.7 0.6 fusion
  94.3 0.0 collective-permute-done.6
  94.3 0.2 add_convert_fusion
  94.5 0.0 copy-start.7
  94.6 0.0 copy-start.6
  94.6 0.9 pad_maximum_fusion
  95.4 7.1 %all-to-all-start.3 = ((bf16[16,64,256]{2,1,0:T(8,128)(2,1)}), bf16[16,64,256]{2,1,0:T(8,128)(2,1)S(1)}, u32[]{:S(2)}, u32[]{:S(2)}) async-start(bf16[16,64,256]{2,1,0:T(8,128)(2,1)} %bitcast.9), calls=%async_computation.3 | async-start | bytes 1048576 | tf_op jit(solution)/shard_map/all_to_all | solution.py:192
  102.5 0.0 copy-done.7
  102.5 9.7 %all-to-all-done.3 = bf16[16,64,256]{2,1,0:T(8,128)(2,1)S(1)} async-done(((bf16[16,64,256]{2,1,0:T(8,128)(2,1)}), bf16[16,64,256]{2,1,0:T(8,128)(2,1)S(1)}, u32[]{:S(2)}, u32[]{:S(2)}) %all-to-all-start.3) | async-done | bytes 524320 | tf_op jit(solution)/shard_map/all_to_all | solution.py:192
  112.2 0.1 convert_reduce_fusion
  112.2 0.0 copy-done.6
  112.3 0.0 copy-start.4
  112.3 0.7 fusion.8
  113.0 0.0 copy-done.4
  (6 shorter events, 0.1 us)
Async XLA Ops:
  0.6 23.1 %copy-start.5 = (s32[4]{0:T(128)S(1)}, s32[4]{0:T(128)}, u32[]{:S(2)}) copy-start(s32[4]{0:T(128)} %owners_ref.1) | copy-start | bytes 52
  0.6 23.1 %copy-start = (bf16[24,3,128,128]{3,2,1,0:T(8,128)(2,1)S(1)}, bf16[24,3,128,128]{3,2,1,0:T(8,128)(2,1)}, u32[]{:S(2)}) copy-start(bf16[24,3,128,128]{3,2,1,0:T(8,128)(2,1)} %dipole.1) | copy-start | bytes 7077892
  0.6 22.1 %collective-permute-start = (bf16[3072,128]{1,0:T(8,128)(2,1)}, bf16[3072,128]{1,0:T(8,128)(2,1)S(1)}, u32[]{:S(2)}, u32[]{:S(2)}) collective-permute-start(bf16[3072,128]{1,0:T(8,128)(2,1)} %own.1), channel_id=1, source_target_pairs={{0,8},{8,0},{1,9},{9,1},{2,10},{10,2},{3,11},{11,3},{4,12},{12,4},... | collective-permute-start | bytes 2359304 | tf_op jit(solution)/shard_map/ppermute | solution.py:88
  11.8 14.7 %collective-permute-start.3 = (bf16[768,256]{1,0:T(8,128)(2,1)S(1)}, bf16[768,256]{1,0:T(8,128)(2,1)}, u32[]{:S(2)}, u32[]{:S(2)}) collective-permute-start(bf16[768,256]{1,0:T(8,128)(2,1)S(1)} %get-tuple-element.81), channel_id=1, source_target_pairs={{0,16},{8,24},{16,0},{24,8},{1,17},{9,25},{17,1},{25,9},{2,18},{10... | collective-permute-start | bytes 1179656 | tf_op jit(solution)/shard_map/ppermute | solution.py:148
  15.3 5.6 %collective-permute-start.1 = (bf16[256,128]{1,0:T(8,128)(2,1)}, bf16[256,128]{1,0:T(8,128)(2,1)}, u32[]{:S(2)}, u32[]{:S(2)}) collective-permute-start(bf16[256,128]{1,0:T(8,128)(2,1)} %get-tuple-element.85), channel_id=1, source_target_pairs={{0,1},{1,2},{2,3},{3,4},{4,5},{5,6},{6,7},{9,8},{10,9},{11,10},{12... | collective-permute-start | bytes 196616 | tf_op jit(solution)/shard_map/ppermute | solution.py:86
  16.6 6.2 %collective-permute-start.2 = (bf16[256,128]{1,0:T(8,128)(2,1)}, bf16[256,128]{1,0:T(8,128)(2,1)}, u32[]{:S(2)}, u32[]{:S(2)}) collective-permute-start(bf16[256,128]{1,0:T(8,128)(2,1)} %get-tuple-element.84), channel_id=1, source_target_pairs={{8,1},{9,2},{10,3},{11,4},{12,5},{13,6},{14,7},{1,8},{2,9},{3,10},... | collective-permute-start | bytes 196616 | tf_op jit(solution)/shard_map/ppermute | solution.py:87
  22.8 0.9 copy-start.2
  23.7 31.1 %copy-start.1 = (bf16[3072,128]{1,0:T(8,128)(2,1)S(1)}, bf16[3072,128]{1,0:T(8,128)(2,1)}, u32[]{:S(2)}) copy-start(bf16[3072,128]{1,0:T(8,128)(2,1)} %own.1) | copy-start | bytes 2359300
  26.5 28.2 %all-to-all-start.1 = ((bf16[32,48,128]{2,1,0:T(8,128)(2,1)}), bf16[32,48,128]{2,1,0:T(8,128)(2,1)S(1)}, u32[]{:S(2)}, u32[]{:S(2)}) async-start(bf16[32,48,128]{2,1,0:T(8,128)(2,1)} %bitcast.3), calls=%async_computation.1 | async-start | bytes 786432 | tf_op jit(solution)/shard_map/all_to_all | solution.py:162
  39.5 4.0 %collective-permute-start.4 = (bf16[768,256]{1,0:T(8,128)(2,1)}, bf16[768,256]{1,0:T(8,128)(2,1)}, u32[]{:S(2)}, u32[]{:S(2)}) collective-permute-start(bf16[768,256]{1,0:T(8,128)(2,1)} %get-tuple-element.80), channel_id=1, source_target_pairs={{0,8},{8,0},{16,24},{24,16},{1,9},{9,1},{17,25},{25,17},{2,10},{10... | collective-permute-start | bytes 1179656 | tf_op jit(solution)/shard_map/ppermute | solution.py:148
  56.3 4.3 %copy-start.3 = (bf16[768,256]{1,0:T(8,128)(2,1)S(1)}, bf16[768,256]{1,0:T(8,128)(2,1)}, u32[]{:S(2)}) copy-start(bf16[768,256]{1,0:T(8,128)(2,1)} %get-tuple-element.79) | copy-start | bytes 1179652
  56.3 33.1 %all-to-all-start.2 = ((bf16[16,48,512]{2,1,0:T(8,128)(2,1)}), bf16[16,48,512]{2,1,0:T(8,128)(2,1)S(1)}, u32[]{:S(2)}, u32[]{:S(2)}) async-start(bf16[16,48,512]{2,1,0:T(8,128)(2,1)} %get-tuple-element.88), calls=%async_computation.2 | async-start | bytes 1572864 | tf_op jit(solution)/shard_map/all_to_all | solution.py:175
  60.7 27.8 %collective-permute-start.5 = (bf16[768,256]{1,0:T(8,128)(2,1)S(1)}, bf16[768,256]{1,0:T(8,128)(2,1)S(1)}, u32[]{:S(2)}, u32[]{:S(2)}) collective-permute-start(bf16[768,256]{1,0:T(8,128)(2,1)S(1)} %copy-done.3), channel_id=1, source_target_pairs={{0,24},{8,16},{16,8},{24,0},{1,25},{9,17},{17,9},{25,1},{2,26},{10... | collective-permute-start | bytes 1179656 | tf_op jit(solution)/shard_map/ppermute | solution.py:148
  90.1 4.2 %collective-permute-start.6 = (bf16[512,512]{1,0:T(8,128)(2,1)S(1)}, bf16[512,512]{1,0:T(8,128)(2,1)S(1)}, u32[]{:S(2)}, u32[]{:S(2)}) collective-permute-start(bf16[512,512]{1,0:T(8,128)(2,1)S(1)} %convolution_convert_fusion), channel_id=1, source_target_pairs={{0,8},{8,0},{1,9},{9,1},{2,10},{10,2},{3,11},{11,3},{4,12},{12,4},... | collective-permute-start | bytes 1572872 | tf_op jit(solution)/shard_map/ppermute | solution.py:185
  94.5 8.0 %copy-start.7 = (f32[64]{0:T(128)S(1)}, f32[64]{0:T(128)}, u32[]{:S(2)}) copy-start(f32[64]{0:T(128)} %param.14) | copy-start | bytes 772
  94.6 17.7 %copy-start.6 = (f32[256]{0:T(256)S(1)}, f32[256]{0:T(256)}, u32[]{:S(2)}) copy-start(f32[256]{0:T(256)} %param.15) | copy-start | bytes 3076
  95.4 16.7 %all-to-all-start.3 = ((bf16[16,64,256]{2,1,0:T(8,128)(2,1)}), bf16[16,64,256]{2,1,0:T(8,128)(2,1)S(1)}, u32[]{:S(2)}, u32[]{:S(2)}) async-start(bf16[16,64,256]{2,1,0:T(8,128)(2,1)} %bitcast.9), calls=%async_computation.3 | async-start | bytes 1048576 | tf_op jit(solution)/shard_map/all_to_all | solution.py:192
  112.3 0.7 copy-start.4

commit v9 on v8

--- a/solution.py
+++ b/solution.py
@@ -130,6 +130,16 @@
     )(owners, pieces, seconds)
 
 
+def add_kernel(kept, received, added):
+    ranges, sides, rows, width = added.shape
+    for r in range(ranges):
+        here = pl.ds(r * rows, rows)
+        for side in range(sides):
+            lanes = pl.ds(side * width, width)
+            total = kept[here, lanes] + received[here, lanes].astype(F32)
+            added[r, side] = total.astype(BF16)
+
+
 def on_device(upper_coef, store, owners, dipole, offsets, lower_energy, upper_energy):
     core = lax.axis_index("core")
     state = lax.axis_index(STATE)
@@ -139,30 +149,33 @@
     zlo = lax.axis_index("zlo")
     quarter = upper_coef.shape[0] // 4
 
-    def mine(flip_zlo, flip_core):
+    def mine(rows, flip_zlo, flip_core):
         start = ((core ^ flip_core) * 2 + (zlo ^ flip_zlo)) * quarter
-        return lax.dynamic_slice_in_dim(upper_coef, start, quarter, 0)
-
-    def from_peer(flip_zlo, flip_core):
+        return lax.dynamic_slice_in_dim(rows, start, quarter, 0)
+
+    def from_peer(rows, flip_zlo, flip_core):
         flip = 2 * flip_zlo + flip_core
-        return lax.ppermute(mine(flip_zlo, flip_core), SHARED, [(i, i ^ flip) for i in range(4)])
+        piece = mine(rows, flip_zlo, flip_core)
+        return lax.ppermute(piece, SHARED, [(i, i ^ flip) for i in range(4)])
 
     def beside(near, far):
         low = zlo == 0
         return jnp.concatenate([jnp.where(low, near, far), jnp.where(low, far, near)], 1)
 
-    kinds = [from_peer(1, 1), from_peer(1, 0), from_peer(0, 1)]
+    across_z = from_peer(upper_coef, 1, 0)
     panels = chip_panels(store, core)
     half = chip_half(False, state, owners, offsets, panels, dipole)
 
-    half, kinds[1] = lax.optimization_barrier((half, kinds[1]))
+    half, across_z, later = lax.optimization_barrier((half, across_z, upper_coef))
+    across_cores = from_peer(later, 0, 1)
+    across_both = from_peer(later, 1, 1)
 
     def scatter(half):
         chips = lax.axis_size(CHIPS)
         return lax.all_to_all(half, CHIPS, 0, 0, tiled=True).reshape(chips, -1, width)
 
     pieces = scatter(half)
-    pieces, kinds[2] = lax.optimization_barrier((pieces, kinds[2]))
+    pieces, across_cores = lax.optimization_barrier((pieces, across_cores))
     chips_of = owners // 2
     shared = jnp.sum((chips_of[:, None] == chips_of[None, :]).astype(jnp.int32)) > PANELS
     copies = lax.cond(
@@ -174,8 +187,8 @@
     )
     gathered = lax.all_to_all(copies.reshape(-1, lowers), GATHER, 0, 0, tiled=True)
 
-    upper_other = beside(kinds[2], kinds[0])
-    upper_own = beside(mine(0, 0), kinds[1])
+    upper_other = beside(across_cores, across_both)
+    upper_own = beside(mine(later, 0, 0), across_z)
 
     def share(rhs):
         return lax.dot_general(
@@ -183,12 +196,15 @@
         )
 
     received = lax.ppermute(share(upper_other).astype(BF16), "core", SWAP)
-    kept, received = lax.optimization_barrier((share(upper_own), received))
-    added = (kept + received.astype(F32)).astype(BF16)
+    kept = share(upper_own)
     ranges = lax.axis_size(BASIS)
-    sides = [added[:, :uppers], added[:, uppers:]]
-    added = jnp.stack([side.reshape(ranges, -1, uppers) for side in sides], 1)
-    added = added.reshape(2 * lowers, uppers)
+    added = pl.pallas_call(
+        add_kernel,
+        out_shape=jax.ShapeDtypeStruct((ranges, 2, lowers // ranges, uppers), BF16),
+        in_specs=[VMEM, VMEM],
+        out_specs=VMEM,
+        compiler_params=pltpu.CompilerParams(vmem_limit_bytes=8 << 20),
+    )(kept, received).reshape(2 * lowers, uppers)
     shares = lax.all_to_all(added, BASIS + ("zlo",), 0, 0, tiled=True)
     shares = shares.reshape(2 * ranges, -1, uppers)
     moments = jnp.sum(shares.astype(F32), axis=0)

time: 114 us -> 111 us (0.974)
  waiting for transfers between devices: 49.6 us -> 46.1 us
  local copies, waits for them, and re-layouts: 3.96 us -> 1.85 us
  Pallas kernels: 4.43 us -> 5.89 us
    all_to_all x1, waiting for transfers between devices: 11.3 us -> 8.03 us  [scatter(): lax.all_to_all(half, CHIPS, 0, 0, tiled=True).reshape(chips, -1, width)]
    select_n x2, other arithmetic: 2.32 us -> 3.96 us  [beside(): jnp.where(low, near, far)]
    dynamic_slice x1, local copies, waits for them, and re-layouts: 2.24 us -> 1.03 us  [mine(): return lax.dynamic_slice_in_dim(rows, start, quarter, 0)]
  transfers between devices with their start and end apart: 10 -> 10, of which waited for: 6 -> 7; matrix products, arithmetic and copies ran while one was open for 7% -> 7% of each run, Pallas kernels for 3% -> 3%
where the time goes in v9:
time: 111 us; the launch traced here: 110 us
  starting transfers between devices  46.7 us (42%)
  waiting for transfers between devices  46.1 us (42%)
  other arithmetic  6.37 us (6%)
  Pallas kernels  5.89 us (5%)
  local copies, waits for them, and re-layouts  1.85 us (2%)
  between operations  1.59 us (1%)
  matrix products  1.19 us (1%)
    ppermute x3, waiting for transfers between devices, from_peer(): return lax.ppermute(piece, SHARED, [(i, i ^ flip) for i in range(4)])  24.8 us
    all_to_all x1, starting transfers between devices, scatter(): lax.all_to_all(half, CHIPS, 0, 0, tiled=True).reshape(chips, -1, width)  13.3 us
    all_to_all x1, waiting for transfers between devices, on_device(): shares = lax.all_to_all(added, BASIS + ('zlo',), 0, 0, tiled=True)  9.39 us
    ppermute x1, starting transfers between devices, chip_panels(): other = lax.ppermute(store, 'core', SWAP)  8.92 us
    all_to_all x1, waiting for transfers between devices, scatter(): lax.all_to_all(half, CHIPS, 0, 0, tiled=True).reshape(chips, -1, width)  8.03 us
    all_to_all x1, starting transfers between devices, on_device(): shares = lax.all_to_all(added, BASIS + ('zlo',), 0, 0, tiled=True)  7.38 us
    ppermute x3, starting transfers between devices, from_peer(): return lax.ppermute(piece, SHARED, [(i, i ^ flip) for i in range(4)])  7.14 us
    all_to_all x1, starting transfers between devices, on_device(): lax.all_to_all(copies.reshape(-1, lowers), GATHER, 0, 0, tiled=True)  4.26 us
  transfers between devices with their start and end apart: 10, of which 7 were waited for; matrix products, arithmetic and copies ran while one was open for 7% of the time, Pallas kernels for 3%

profile of v9, /device:TPU:1, one launch (start us, length us, event | category | flops | bytes accessed | tf_op | source)
XLA Modules:
  0.0 109.7 jit_solution(179886738303169455)
XLA Ops:
  0.6 0.0 copy-start.1
  0.6 8.9 %collective-permute-start = (bf16[3072,128]{1,0:T(8,128)(2,1)}, bf16[3072,128]{1,0:T(8,128)(2,1)S(1)}, u32[]{:S(2)}, u32[]{:S(2)}) collective-permute-start(bf16[3072,128]{1,0:T(8,128)(2,1)} %own.1), channel_id=1, source_target_pairs={{0,8},{8,0},{1,9},{9,1},{2,10},{10,2},{3,11},{11,3},{4,12},{12,4},... | collective-permute-start | bytes 2359304 | tf_op jit(solution)/shard_map/ppermute | solution.py:88
  9.6 1.0 constant_dynamic-slice_fusion.2
  10.6 1.9 %collective-permute-start.3 = (bf16[768,256]{1,0:T(8,128)(2,1)S(1)}, bf16[768,256]{1,0:T(8,128)(2,1)S(1)}, u32[]{:S(2)}, u32[]{:S(2)}) collective-permute-start(bf16[768,256]{1,0:T(8,128)(2,1)S(1)} %constant_dynamic-slice_fusion.2), channel_id=1, source_target_pairs={{0,16},{8,24},{16,0},{24,8},{1,17},{9,25},{17,1},{25,9},{2,18},{10... | collective-permute-start | bytes 1179656 | tf_op jit(solution)/shard_map/ppermute | solution.py:159
  12.5 0.9 broadcast_select_fusion.4
  13.4 1.3 %collective-permute-start.1 = (bf16[256,128]{1,0:T(8,128)(2,1)S(1)}, bf16[256,128]{1,0:T(8,128)(2,1)S(1)}, u32[]{:S(2)}, u32[]{:S(2)}) collective-permute-start(bf16[256,128]{1,0:T(8,128)(2,1)S(1)} %get-tuple-element.73), channel_id=1, source_target_pairs={{0,1},{1,2},{2,3},{3,4},{4,5},{5,6},{6,7},{9,8},{10,9},{11,10},{12... | collective-permute-start | bytes 196616 | tf_op jit(solution)/shard_map/ppermute | solution.py:86
  14.7 2.1 %collective-permute-start.2 = (bf16[256,128]{1,0:T(8,128)(2,1)S(1)}, bf16[256,128]{1,0:T(8,128)(2,1)S(1)}, u32[]{:S(2)}, u32[]{:S(2)}) collective-permute-start(bf16[256,128]{1,0:T(8,128)(2,1)S(1)} %get-tuple-element.72), channel_id=1, source_target_pairs={{8,1},{9,2},{10,3},{11,4},{12,5},{13,6},{14,7},{1,8},{2,9},{3,10},... | collective-permute-start | bytes 196616 | tf_op jit(solution)/shard_map/ppermute | solution.py:87
  16.9 0.8 copy.11.offsets_ref
  17.6 1.1 %collective-permute-done.1.own_edge = bf16[256,128]{1,0:T(8,128)(2,1)S(1)} collective-permute-done((bf16[256,128]{1,0:T(8,128)(2,1)S(1)}, bf16[256,128]{1,0:T(8,128)(2,1)S(1)}, u32[]{:S(2)}, u32[]{:S(2)}) %collective-permute-start.1) | collective-permute-done | bytes 65568 | tf_op jit(solution)/shard_map/ppermute | solution.py:86
  18.7 1.9 %collective-permute-done.2.other_edge = bf16[256,128]{1,0:T(8,128)(2,1)S(1)} collective-permute-done((bf16[256,128]{1,0:T(8,128)(2,1)S(1)}, bf16[256,128]{1,0:T(8,128)(2,1)S(1)}, u32[]{:S(2)}, u32[]{:S(2)}) %collective-permute-start.2) | collective-permute-done | bytes 65568 | tf_op jit(solution)/shard_map/ppermute | solution.py:87
  20.6 0.0 collective-permute-done.other
  20.6 0.0 copy-done.1
  20.6 3.4 %shard_map.86 = bf16[1536,128]{1,0:T(8,128)(2,1)} custom-call(s32[1]{0:T(128)} %bitcast.2.state_ref, s32[4]{0:T(128)} %owners_ref.1, s32[24,3]{1,0:T(8,128)S(1)} %copy.11.offsets_ref, bf16[3072,128]{1,0:T(8,128)(2,1)S(1)} %copy-done.1, bf16[3072,128]{1,0:T(8,128)(2,1)S(1)} %collective-permute-done.other, ...), custom_call_target="tpu_custom_call" | custom-call | flops 150994944 | bytes 6291456 | tf_op jit(solution)/shard_map/pallas_call | solution.py:95
  24.0 0.0 copy-done.8
  24.0 0.0 collective-permute-done.3
  24.0 0.0 copy-start.3
  24.0 13.3 %all-to-all-start.1 = ((bf16[32,48,128]{2,1,0:T(8,128)(2,1)}), bf16[32,48,128]{2,1,0:T(8,128)(2,1)S(1)}, u32[]{:S(2)}, u32[]{:S(2)}) async-start(bf16[32,48,128]{2,1,0:T(8,128)(2,1)} %bitcast.3), calls=%async_computation.1 | async-start | bytes 786432 | tf_op jit(solution)/shard_map/all_to_all | solution.py:175
  37.3 0.0 copy-start.10
  37.4 0.0 copy-start
  37.4 2.9 %broadcast_select_fusion.3 = (bf16[768,256]{1,0:T(8,128)(2,1)}, bf16[768,256]{1,0:T(8,128)(2,1)}, bf16[768,256]{1,0:T(8,128)(2,1)}, bf16[768,256]{1,0:T(8,128)(2,1)}) fusion(bf16[768,256]{1,0:T(8,128)(2,1)} %copy-done.3, pred[]{:T(512)S(6)} %eq.24, bf16[3072,256]{1,0:T(8,128)(2,1)} %param.9, s32[]{:T(128)S(6)} %select_n.56, s32[]{:T(128)S(6)} %select_n.59, ...), kind=kLoop, calls=%fused_computation.12 | loop fusion | flops 393216 | bytes 3145741 | tf_op jit(solution)/shard_map/jit(_where)/select_n | solution.py:163
  40.3 1.9 %collective-permute-start.4 = (bf16[768,256]{1,0:T(8,128)(2,1)}, bf16[768,256]{1,0:T(8,128)(2,1)}, u32[]{:S(2)}, u32[]{:S(2)}) collective-permute-start(bf16[768,256]{1,0:T(8,128)(2,1)} %get-tuple-element.69), channel_id=1, source_target_pairs={{0,8},{8,0},{16,24},{24,16},{1,9},{9,1},{17,25},{25,17},{2,10},{10... | collective-permute-start | bytes 1179656 | tf_op jit(solution)/shard_map/ppermute | solution.py:159
  42.2 0.7 convert_reduce_fusion.1
  43.6 0.7 collective-permute-done.4
  44.2 8.0 %all-to-all-done.1 = bf16[32,48,128]{2,1,0:T(8,128)(2,1)S(1)} async-done(((bf16[32,48,128]{2,1,0:T(8,128)(2,1)}), bf16[32,48,128]{2,1,0:T(8,128)(2,1)S(1)}, u32[]{:S(2)}, u32[]{:S(2)}) %all-to-all-start.1) | async-done | bytes 393248 | tf_op jit(solution)/shard_map/all_to_all | solution.py:175
  52.3 0.0 copy-done
  52.3 1.6 %conditional.1 = (bf16[16,48,512]{2,1,0:T(8,128)(2,1)}) conditional(s32[]{:T(128)} %convert_element_type.13, (s32[4]{0:T(128)S(1)}, bf16[32,48,128]{2,1,0:T(8,128)(2,1)S(1)}) %tuple.35, (s32[]{:T(128)}, s32[4]{0:T(128)S(1)}, s32[24,3]{0,1:T(4,128)}, bf16[3072,128]{1,0:T(8,128)(2,1)S(1)}, bf16[3072,128]{1,0:T(8,128)(2,1)}, ...), branch_computations={%region_1.2_spmd, %region_2.3_spmd} | conditional | flops 150994944 | bytes 8127048 | solution.py:181
  52.3 1.6 %branch_0_fun.1 = bf16[16,48,512]{2,1,0:T(8,128)(2,1)} custom-call(s32[4]{0:T(128)S(1)} %get-tuple-element.12.owners_ref, bf16[32,48,128]{2,1,0:T(8,128)(2,1)S(1)} %get-tuple-element.26.pieces.seconds, bf16[32,48,128]{2,1,0:T(8,128)(2,1)S(1)} %get-tuple-element.26.pieces.seconds), custom_call_target="tpu_custom_call" | custom-call | bytes 1048576 | tf_op jit(solution)/shard_map/cond/branch_0_fun/pallas_call | solution.py:122
  53.9 4.3 %all-to-all-start.2 = ((bf16[16,48,512]{2,1,0:T(8,128)(2,1)}), bf16[16,48,512]{2,1,0:T(8,128)(2,1)S(1)}, u32[]{:S(2)}, u32[]{:S(2)}) async-start(bf16[16,48,512]{2,1,0:T(8,128)(2,1)} %get-tuple-element.74), calls=%async_computation.2 | async-start | bytes 1572864 | tf_op jit(solution)/shard_map/all_to_all | solution.py:188
  58.2 3.3 %collective-permute-start.5 = (bf16[768,256]{1,0:T(8,128)(2,1)S(1)}, bf16[768,256]{1,0:T(8,128)(2,1)S(1)}, u32[]{:S(2)}, u32[]{:S(2)}) collective-permute-start(bf16[768,256]{1,0:T(8,128)(2,1)S(1)} %copy-done.6), channel_id=1, source_target_pairs={{0,24},{8,16},{16,8},{24,0},{1,25},{9,17},{17,9},{25,1},{2,26},{10... | collective-permute-start | bytes 1179656 | tf_op jit(solution)/shard_map/ppermute | solution.py:159
  61.5 24.2 %collective-permute-done.5 = bf16[768,256]{1,0:T(8,128)(2,1)S(1)} collective-permute-done((bf16[768,256]{1,0:T(8,128)(2,1)S(1)}, bf16[768,256]{1,0:T(8,128)(2,1)S(1)}, u32[]{:S(2)}, u32[]{:S(2)}) %collective-permute-start.5) | collective-permute-done | bytes 393248 | tf_op jit(solution)/shard_map/ppermute | solution.py:159
  85.7 1.1 broadcast_select_fusion.1
  86.7 0.0 all-to-all-done.2
  86.7 0.0 copy-start.4
  86.7 0.0 copy-start.5
  86.8 0.6 convolution_convert_fusion
  87.4 2.3 %collective-permute-start.6 = (bf16[512,512]{1,0:T(8,128)(2,1)S(1)}, bf16[512,512]{1,0:T(8,128)(2,1)S(1)}, u32[]{:S(2)}, u32[]{:S(2)}) collective-permute-start(bf16[512,512]{1,0:T(8,128)(2,1)S(1)} %convolution_convert_fusion), channel_id=1, source_target_pairs={{0,8},{8,0},{1,9},{9,1},{2,10},{10,2},{3,11},{11,3},{4,12},{12,4},... | collective-permute-start | bytes 1572872 | tf_op jit(solution)/shard_map/ppermute | solution.py:198
  89.7 0.0 copy-done.4
  89.7 0.0 copy-done.5
  89.7 0.6 fusion.kept
  90.3 0.0 copy-start.12
  90.3 0.0 copy-start.11
  90.3 0.9 collective-permute-done.6.received
  91.2 0.9 shard_map.87
  92.1 7.4 %all-to-all-start.3 = ((bf16[16,64,256]{2,1,0:T(8,128)(2,1)}), bf16[16,64,256]{2,1,0:T(8,128)(2,1)S(1)}, u32[]{:S(2)}, u32[]{:S(2)}) async-start(bf16[16,64,256]{2,1,0:T(8,128)(2,1)} %bitcast.5), calls=%async_computation.3 | async-start | bytes 1048576 | tf_op jit(solution)/shard_map/all_to_all | solution.py:208
  99.5 9.4 %all-to-all-done.3 = bf16[16,64,256]{2,1,0:T(8,128)(2,1)S(1)} async-done(((bf16[16,64,256]{2,1,0:T(8,128)(2,1)}), bf16[16,64,256]{2,1,0:T(8,128)(2,1)S(1)}, u32[]{:S(2)}, u32[]{:S(2)}) %all-to-all-start.3) | async-done | bytes 524320 | tf_op jit(solution)/shard_map/all_to_all | solution.py:208
  108.9 0.1 convert_reduce_fusion
  109.0 0.0 copy-start.9
  109.0 0.7 fusion.8
  (14 shorter events, 0.0 us)
Async XLA Ops:
  0.6 20.0 %copy-start.1 = (bf16[3072,128]{1,0:T(8,128)(2,1)S(1)}, bf16[3072,128]{1,0:T(8,128)(2,1)}, u32[]{:S(2)}) copy-start(bf16[3072,128]{1,0:T(8,128)(2,1)} %own.1) | copy-start | bytes 2359300
  0.6 20.0 %collective-permute-start = (bf16[3072,128]{1,0:T(8,128)(2,1)}, bf16[3072,128]{1,0:T(8,128)(2,1)S(1)}, u32[]{:S(2)}, u32[]{:S(2)}) collective-permute-start(bf16[3072,128]{1,0:T(8,128)(2,1)} %own.1), channel_id=1, source_target_pairs={{0,8},{8,0},{1,9},{9,1},{2,10},{10,2},{3,11},{11,3},{4,12},{12,4},... | collective-permute-start | bytes 2359304 | tf_op jit(solution)/shard_map/ppermute | solution.py:88
  10.6 13.4 %collective-permute-start.3 = (bf16[768,256]{1,0:T(8,128)(2,1)S(1)}, bf16[768,256]{1,0:T(8,128)(2,1)S(1)}, u32[]{:S(2)}, u32[]{:S(2)}) collective-permute-start(bf16[768,256]{1,0:T(8,128)(2,1)S(1)} %constant_dynamic-slice_fusion.2), channel_id=1, source_target_pairs={{0,16},{8,24},{16,0},{24,8},{1,17},{9,25},{17,1},{25,9},{2,18},{10... | collective-permute-start | bytes 1179656 | tf_op jit(solution)/shard_map/ppermute | solution.py:159
  13.4 5.3 %collective-permute-start.1 = (bf16[256,128]{1,0:T(8,128)(2,1)S(1)}, bf16[256,128]{1,0:T(8,128)(2,1)S(1)}, u32[]{:S(2)}, u32[]{:S(2)}) collective-permute-start(bf16[256,128]{1,0:T(8,128)(2,1)S(1)} %get-tuple-element.73), channel_id=1, source_target_pairs={{0,1},{1,2},{2,3},{3,4},{4,5},{5,6},{6,7},{9,8},{10,9},{11,10},{12... | collective-permute-start | bytes 196616 | tf_op jit(solution)/shard_map/ppermute | solution.py:86
  14.7 5.9 %collective-permute-start.2 = (bf16[256,128]{1,0:T(8,128)(2,1)S(1)}, bf16[256,128]{1,0:T(8,128)(2,1)S(1)}, u32[]{:S(2)}, u32[]{:S(2)}) collective-permute-start(bf16[256,128]{1,0:T(8,128)(2,1)S(1)} %get-tuple-element.72), channel_id=1, source_target_pairs={{8,1},{9,2},{10,3},{11,4},{12,5},{13,6},{14,7},{1,8},{2,9},{3,10},... | collective-permute-start | bytes 196616 | tf_op jit(solution)/shard_map/ppermute | solution.py:87
  18.7 5.3 %copy-start.7 = (bf16[256,128]{1,0:T(8,128)(2,1)}, bf16[256,128]{1,0:T(8,128)(2,1)S(1)}, u32[]{:S(2)}) copy-start(bf16[256,128]{1,0:T(8,128)(2,1)S(1)} %collective-permute-done.1.own_edge) | copy-start | bytes 196612
  20.6 3.4 %copy-start.8 = (bf16[256,128]{1,0:T(8,128)(2,1)}, bf16[256,128]{1,0:T(8,128)(2,1)S(1)}, u32[]{:S(2)}) copy-start(bf16[256,128]{1,0:T(8,128)(2,1)S(1)} %collective-permute-done.2.other_edge) | copy-start | bytes 196612
  20.6 3.4 %copy-start.2 = (bf16[3072,128]{1,0:T(8,128)(2,1)}, bf16[3072,128]{1,0:T(8,128)(2,1)S(1)}, u32[]{:S(2)}) copy-start(bf16[3072,128]{1,0:T(8,128)(2,1)S(1)} %collective-permute-done.other) | copy-start | bytes 2359300
  24.0 13.3 %copy-start.3 = (bf16[768,256]{1,0:T(8,128)(2,1)}, bf16[768,256]{1,0:T(8,128)(2,1)S(1)}, u32[]{:S(2)}) copy-start(bf16[768,256]{1,0:T(8,128)(2,1)S(1)} %collective-permute-done.3) | copy-start | bytes 1179652
  24.0 28.2 %all-to-all-start.1 = ((bf16[32,48,128]{2,1,0:T(8,128)(2,1)}), bf16[32,48,128]{2,1,0:T(8,128)(2,1)S(1)}, u32[]{:S(2)}, u32[]{:S(2)}) async-start(bf16[32,48,128]{2,1,0:T(8,128)(2,1)} %bitcast.3), calls=%async_computation.1 | async-start | bytes 786432 | tf_op jit(solution)/shard_map/all_to_all | solution.py:175
  37.3 4.9 %copy-start.10 = (s32[4]{0:T(128)S(1)}, s32[4]{0:T(128)}, u32[]{:S(2)}) copy-start(s32[4]{0:T(128)} %owners_ref.1) | copy-start | bytes 52
  37.4 14.9 %copy-start = (bf16[24,3,128,128]{3,2,1,0:T(8,128)(2,1)S(1)}, bf16[24,3,128,128]{3,2,1,0:T(8,128)(2,1)}, u32[]{:S(2)}) copy-start(bf16[24,3,128,128]{3,2,1,0:T(8,128)(2,1)} %dipole.1) | copy-start | bytes 7077892
  40.3 3.9 %collective-permute-start.4 = (bf16[768,256]{1,0:T(8,128)(2,1)}, bf16[768,256]{1,0:T(8,128)(2,1)}, u32[]{:S(2)}, u32[]{:S(2)}) collective-permute-start(bf16[768,256]{1,0:T(8,128)(2,1)} %get-tuple-element.69), channel_id=1, source_target_pairs={{0,8},{8,0},{16,24},{24,16},{1,9},{9,1},{17,25},{25,17},{2,10},{10... | collective-permute-start | bytes 1179656 | tf_op jit(solution)/shard_map/ppermute | solution.py:159
  53.9 4.3 %copy-start.6 = (bf16[768,256]{1,0:T(8,128)(2,1)S(1)}, bf16[768,256]{1,0:T(8,128)(2,1)}, u32[]{:S(2)}) copy-start(bf16[768,256]{1,0:T(8,128)(2,1)} %get-tuple-element.68) | copy-start | bytes 1179652
  53.9 32.8 %all-to-all-start.2 = ((bf16[16,48,512]{2,1,0:T(8,128)(2,1)}), bf16[16,48,512]{2,1,0:T(8,128)(2,1)S(1)}, u32[]{:S(2)}, u32[]{:S(2)}) async-start(bf16[16,48,512]{2,1,0:T(8,128)(2,1)} %get-tuple-element.74), calls=%async_computation.2 | async-start | bytes 1572864 | tf_op jit(solution)/shard_map/all_to_all | solution.py:188
  58.2 27.5 %collective-permute-start.5 = (bf16[768,256]{1,0:T(8,128)(2,1)S(1)}, bf16[768,256]{1,0:T(8,128)(2,1)S(1)}, u32[]{:S(2)}, u32[]{:S(2)}) collective-permute-start(bf16[768,256]{1,0:T(8,128)(2,1)S(1)} %copy-done.6), channel_id=1, source_target_pairs={{0,24},{8,16},{16,8},{24,0},{1,25},{9,17},{17,9},{25,1},{2,26},{10... | collective-permute-start | bytes 1179656 | tf_op jit(solution)/shard_map/ppermute | solution.py:159
  86.7 2.9 %copy-start.4 = (bf16[768,256]{1,0:T(8,128)(2,1)S(1)}, bf16[768,256]{1,0:T(8,128)(2,1)}, u32[]{:S(2)}) copy-start(bf16[768,256]{1,0:T(8,128)(2,1)} %get-tuple-element.66) | copy-start | bytes 1179652
  86.7 2.9 %copy-start.5 = (bf16[768,256]{1,0:T(8,128)(2,1)S(1)}, bf16[768,256]{1,0:T(8,128)(2,1)}, u32[]{:S(2)}) copy-start(bf16[768,256]{1,0:T(8,128)(2,1)} %get-tuple-element.67) | copy-start | bytes 1179652
  87.4 3.8 %collective-permute-start.6 = (bf16[512,512]{1,0:T(8,128)(2,1)S(1)}, bf16[512,512]{1,0:T(8,128)(2,1)S(1)}, u32[]{:S(2)}, u32[]{:S(2)}) collective-permute-start(bf16[512,512]{1,0:T(8,128)(2,1)S(1)} %convolution_convert_fusion), channel_id=1, source_target_pairs={{0,8},{8,0},{1,9},{9,1},{2,10},{10,2},{3,11},{11,3},{4,12},{12,4},... | collective-permute-start | bytes 1572872 | tf_op jit(solution)/shard_map/ppermute | solution.py:198
  90.3 9.2 %copy-start.12 = (f32[64]{0:T(128)S(1)}, f32[64]{0:T(128)}, u32[]{:S(2)}) copy-start(f32[64]{0:T(128)} %param.14) | copy-start | bytes 772
  90.3 18.7 %copy-start.11 = (f32[256]{0:T(256)S(1)}, f32[256]{0:T(256)}, u32[]{:S(2)}) copy-start(f32[256]{0:T(256)} %param.15) | copy-start | bytes 3076
  92.1 16.8 %all-to-all-start.3 = ((bf16[16,64,256]{2,1,0:T(8,128)(2,1)}), bf16[16,64,256]{2,1,0:T(8,128)(2,1)S(1)}, u32[]{:S(2)}, u32[]{:S(2)}) async-start(bf16[16,64,256]{2,1,0:T(8,128)(2,1)} %bitcast.5), calls=%async_computation.3 | async-start | bytes 1048576 | tf_op jit(solution)/shard_map/all_to_all | solution.py:208
  109.0 0.7 copy-start.9

commit v10 on v9

--- a/solution.py
+++ b/solution.py
@@ -167,7 +167,6 @@
     half = chip_half(False, state, owners, offsets, panels, dipole)
 
     half, across_z, later = lax.optimization_barrier((half, across_z, upper_coef))
-    across_cores = from_peer(later, 0, 1)
     across_both = from_peer(later, 1, 1)
 
     def scatter(half):
@@ -175,7 +174,10 @@
         return lax.all_to_all(half, CHIPS, 0, 0, tiled=True).reshape(chips, -1, width)
 
     pieces = scatter(half)
-    pieces, across_cores = lax.optimization_barrier((pieces, across_cores))
+    pieces, across_both, across_z, last = lax.optimization_barrier(
+        (pieces, across_both, across_z, later)
+    )
+    across_cores = from_peer(last, 0, 1)
     chips_of = owners // 2
     shared = jnp.sum((chips_of[:, None] == chips_of[None, :]).astype(jnp.int32)) > PANELS
     copies = lax.cond(
@@ -188,7 +190,7 @@
     gathered = lax.all_to_all(copies.reshape(-1, lowers), GATHER, 0, 0, tiled=True)
 
     upper_other = beside(across_cores, across_both)
-    upper_own = beside(mine(later, 0, 0), across_z)
+    upper_own = beside(mine(last, 0, 0), across_z)
 
     def share(rhs):
         return lax.dot_general(

time: 111 us -> 122 us (1.099)
  starting transfers between devices: 46.7 us -> 57.7 us
  local copies, waits for them, and re-layouts: 1.85 us -> 6.62 us
  waiting for transfers between devices: 46.1 us -> 43.7 us
  other arithmetic: 6.37 us -> 4.68 us
    all_to_all x1, waiting for transfers between devices: 0.01 us -> 16.2 us  [on_device(): lax.all_to_all(copies.reshape(-1, lowers), GATHER, 0, 0, tiled=True)]
    ppermute x3, waiting for transfers between devices: 24.8 us -> 14.2 us  [from_peer(): return lax.ppermute(piece, SHARED, [(i, i ^ flip) for i in range(4)])]
    all_to_all x1, waiting for transfers between devices: 8.03 us -> 0.01 us  [scatter(): lax.all_to_all(half, CHIPS, 0, 0, tiled=True).reshape(chips, -1, width)]
    all_to_all x1, starting transfers between devices: 4.26 us -> 9.33 us  [on_device(): lax.all_to_all(copies.reshape(-1, lowers), GATHER, 0, 0, tiled=True)]
    all_to_all x1, starting transfers between devices: 7.38 us -> 10.9 us  [on_device(): shares = lax.all_to_all(added, BASIS + ('zlo',), 0, 0, tiled=True)]
    ppermute x1, starting transfers between devices: 2.31 us -> 5.44 us  [on_device(): received = lax.ppermute(share(upper_other).astype(BF16), 'core', SWAP)]
    dynamic_slice x1 -> x2, local copies, waits for them, and re-layouts: 1.03 us -> 3.53 us  [mine(): return lax.dynamic_slice_in_dim(rows, start, quarter, 0)]
    unnamed x27 -> x23, local copies, waits for them, and re-layouts: 0.83 us -> 3.09 us
where the time goes in v10:
time: 122 us; the launch traced here: 121 us
  starting transfers between devices  57.7 us (47%)
  waiting for transfers between devices  43.7 us (36%)
  local copies, waits for them, and re-layouts  6.62 us (5%)
  Pallas kernels  6.01 us (5%)
  other arithmetic  4.68 us (4%)
  between operations  1.59 us (1%)
    all_to_all x1, waiting for transfers between devices, on_device(): lax.all_to_all(copies.reshape(-1, lowers), GATHER, 0, 0, tiled=True)  16.2 us
    ppermute x3, waiting for transfers between devices, from_peer(): return lax.ppermute(piece, SHARED, [(i, i ^ flip) for i in range(4)])  14.2 us
    all_to_all x1, starting transfers between devices, scatter(): lax.all_to_all(half, CHIPS, 0, 0, tiled=True).reshape(chips, -1, width)  13.2 us
    all_to_all x1, starting transfers between devices, on_device(): shares = lax.all_to_all(added, BASIS + ('zlo',), 0, 0, tiled=True)  10.9 us
    all_to_all x1, waiting for transfers between devices, on_device(): shares = lax.all_to_all(added, BASIS + ('zlo',), 0, 0, tiled=True)  9.39 us
    all_to_all x1, starting transfers between devices, on_device(): lax.all_to_all(copies.reshape(-1, lowers), GATHER, 0, 0, tiled=True)  9.33 us
    ppermute x1, starting transfers between devices, chip_panels(): other = lax.ppermute(store, 'core', SWAP)  8.92 us
    ppermute x3, starting transfers between devices, from_peer(): return lax.ppermute(piece, SHARED, [(i, i ^ flip) for i in range(4)])  6.42 us
  transfers between devices with their start and end apart: 10, of which 7 were waited for; matrix products, arithmetic and copies ran while one was open for 7% of the time, Pallas kernels for 3%

profile of v10, /device:TPU:1, one launch (start us, length us, event | category | flops | bytes accessed | tf_op | source)
XLA Modules:
  0.0 121.5 jit_solution(1650261184236621667)
XLA Ops:
  0.6 0.0 copy-start.1
  0.6 8.9 %collective-permute-start = (bf16[3072,128]{1,0:T(8,128)(2,1)}, bf16[3072,128]{1,0:T(8,128)(2,1)S(1)}, u32[]{:S(2)}, u32[]{:S(2)}) collective-permute-start(bf16[3072,128]{1,0:T(8,128)(2,1)} %own.1), channel_id=1, source_target_pairs={{0,8},{8,0},{1,9},{9,1},{2,10},{10,2},{3,11},{11,3},{4,12},{12,4},... | collective-permute-start | bytes 2359304 | tf_op jit(solution)/shard_map/ppermute | solution.py:88
  9.6 1.8 %constant_dynamic-slice_fusion.2 = bf16[768,256]{1,0:T(8,128)(2,1)} fusion(bf16[3072,256]{1,0:T(8,128)(2,1)} %param.9, s32[]{:T(128)S(6)} %select_n.53), kind=kLoop, calls=%fused_computation.28 | loop fusion | bytes 786436 | tf_op jit(solution)/shard_map/dynamic_slice | solution.py:154
  11.3 1.9 %collective-permute-start.3 = (bf16[768,256]{1,0:T(8,128)(2,1)}, bf16[768,256]{1,0:T(8,128)(2,1)S(1)}, u32[]{:S(2)}, u32[]{:S(2)}) collective-permute-start(bf16[768,256]{1,0:T(8,128)(2,1)} %constant_dynamic-slice_fusion.2), channel_id=1, source_target_pairs={{0,16},{8,24},{16,0},{24,8},{1,17},{9,25},{17,1},{25,9},{2,18},{10... | collective-permute-start | bytes 1179656 | tf_op jit(solution)/shard_map/ppermute | solution.py:159
  13.3 0.9 broadcast_select_fusion.4
  14.2 1.3 %collective-permute-start.1 = (bf16[256,128]{1,0:T(8,128)(2,1)S(1)}, bf16[256,128]{1,0:T(8,128)(2,1)S(1)}, u32[]{:S(2)}, u32[]{:S(2)}) collective-permute-start(bf16[256,128]{1,0:T(8,128)(2,1)S(1)} %get-tuple-element.76), channel_id=1, source_target_pairs={{0,1},{1,2},{2,3},{3,4},{4,5},{5,6},{6,7},{9,8},{10,9},{11,10},{12... | collective-permute-start | bytes 196616 | tf_op jit(solution)/shard_map/ppermute | solution.py:86
  15.5 2.1 %collective-permute-start.2 = (bf16[256,128]{1,0:T(8,128)(2,1)S(1)}, bf16[256,128]{1,0:T(8,128)(2,1)S(1)}, u32[]{:S(2)}, u32[]{:S(2)}) collective-permute-start(bf16[256,128]{1,0:T(8,128)(2,1)S(1)} %get-tuple-element.75), channel_id=1, source_target_pairs={{8,1},{9,2},{10,3},{11,4},{12,5},{13,6},{14,7},{1,8},{2,9},{3,10},... | collective-permute-start | bytes 196616 | tf_op jit(solution)/shard_map/ppermute | solution.py:87
  17.6 0.8 copy.11.offsets_ref
  18.4 1.1 collective-permute-done.1.own_edge
  19.5 1.9 %collective-permute-done.2.other_edge = bf16[256,128]{1,0:T(8,128)(2,1)S(1)} collective-permute-done((bf16[256,128]{1,0:T(8,128)(2,1)S(1)}, bf16[256,128]{1,0:T(8,128)(2,1)S(1)}, u32[]{:S(2)}, u32[]{:S(2)}) %collective-permute-start.2) | collective-permute-done | bytes 65568 | tf_op jit(solution)/shard_map/ppermute | solution.py:87
  21.3 0.0 collective-permute-done.other
  21.3 0.0 copy-done.5
  21.4 0.6 copy-done.6
  22.0 0.9 copy-done.2
  22.9 0.0 copy-done.1
  22.9 3.5 %shard_map.86 = bf16[1536,128]{1,0:T(8,128)(2,1)} custom-call(s32[1]{0:T(128)} %bitcast.2.state_ref, s32[4]{0:T(128)} %owners_ref.1, s32[24,3]{1,0:T(8,128)S(1)} %copy.11.offsets_ref, bf16[3072,128]{1,0:T(8,128)(2,1)S(1)} %copy-done.1, bf16[3072,128]{1,0:T(8,128)(2,1)} %copy-done.2, bf16[256,128]{1,0:T(8,128)(2,1)} %copy-done.5, bf16[256,128]{1,0:T(8,128)(2,1)} %copy-done.6, ...), custom_call_target="tpu_custom_call" | custom-call | flops 150994944 | bytes 6291456 | tf_op jit(solution)/shard_map/pallas_call | solution.py:95
  26.4 0.0 collective-permute-done.3
  26.4 0.8 copy-done.4
  27.2 13.2 %all-to-all-start.1 = ((bf16[32,48,128]{2,1,0:T(8,128)(2,1)}), bf16[32,48,128]{2,1,0:T(8,128)(2,1)S(1)}, u32[]{:S(2)}, u32[]{:S(2)}) async-start(bf16[32,48,128]{2,1,0:T(8,128)(2,1)} %bitcast.3), calls=%async_computation.1 | async-start | bytes 786432 | tf_op jit(solution)/shard_map/all_to_all | solution.py:174
  40.4 1.8 %constant_dynamic-slice_fusion.1 = bf16[768,256]{1,0:T(8,128)(2,1)} fusion(bf16[3072,256]{1,0:T(8,128)(2,1)} %param.9, s32[]{:T(128)S(6)} %select_n.54), kind=kLoop, calls=%fused_computation.27 | loop fusion | bytes 786436 | tf_op jit(solution)/shard_map/dynamic_slice | solution.py:154
  42.2 1.9 %collective-permute-start.4 = (bf16[768,256]{1,0:T(8,128)(2,1)}, bf16[768,256]{1,0:T(8,128)(2,1)}, u32[]{:S(2)}, u32[]{:S(2)}) collective-permute-start(bf16[768,256]{1,0:T(8,128)(2,1)} %constant_dynamic-slice_fusion.1), channel_id=1, source_target_pairs={{0,24},{8,16},{16,8},{24,0},{1,25},{9,17},{17,9},{25,1},{2,26},{10... | collective-permute-start | bytes 1179656 | tf_op jit(solution)/shard_map/ppermute | solution.py:159
  44.1 0.0 copy-done.8
  44.1 0.8 convert_reduce_fusion.1
  45.6 12.9 %collective-permute-done.4 = bf16[768,256]{1,0:T(8,128)(2,1)} collective-permute-done((bf16[768,256]{1,0:T(8,128)(2,1)}, bf16[768,256]{1,0:T(8,128)(2,1)}, u32[]{:S(2)}, u32[]{:S(2)}) %collective-permute-start.4) | collective-permute-done | bytes 393248 | tf_op jit(solution)/shard_map/ppermute | solution.py:159
  58.5 0.0 all-to-all-done.1
  58.5 0.0 copy-done
  58.5 1.6 %conditional.1 = (bf16[16,48,512]{2,1,0:T(8,128)(2,1)}) conditional(s32[]{:T(128)} %convert_element_type.13, (s32[4]{0:T(128)S(1)}, bf16[32,48,128]{2,1,0:T(8,128)(2,1)S(1)}) %tuple.34, (s32[]{:T(128)}, s32[4]{0:T(128)S(1)}, s32[24,3]{0,1:T(4,128)}, bf16[3072,128]{1,0:T(8,128)(2,1)S(1)}, bf16[3072,128]{1,0:T(8,128)(2,1)}, ...), branch_computations={%region_1.2_spmd, %region_2.3_spmd} | conditional | flops 150994944 | bytes 8127048 | solution.py:183
  58.5 1.6 %branch_0_fun.1 = bf16[16,48,512]{2,1,0:T(8,128)(2,1)} custom-call(s32[4]{0:T(128)S(1)} %get-tuple-element.12.owners_ref, bf16[32,48,128]{2,1,0:T(8,128)(2,1)S(1)} %get-tuple-element.26.pieces.seconds, bf16[32,48,128]{2,1,0:T(8,128)(2,1)S(1)} %get-tuple-element.26.pieces.seconds), custom_call_target="tpu_custom_call" | custom-call | bytes 1048576 | tf_op jit(solution)/shard_map/cond/branch_0_fun/pallas_call | solution.py:122
  60.1 9.3 %all-to-all-start.2 = ((bf16[16,48,512]{2,1,0:T(8,128)(2,1)}), bf16[16,48,512]{2,1,0:T(8,128)(2,1)S(1)}, u32[]{:S(2)}, u32[]{:S(2)}) async-start(bf16[16,48,512]{2,1,0:T(8,128)(2,1)} %get-tuple-element.77), calls=%async_computation.2 | async-start | bytes 1572864 | tf_op jit(solution)/shard_map/all_to_all | solution.py:190
  69.5 0.0 copy-done.3
  69.5 1.2 broadcast_select_fusion.3
  70.7 2.6 %collective-permute-start.5 = (bf16[768,256]{1,0:T(8,128)(2,1)S(1)}, bf16[768,256]{1,0:T(8,128)(2,1)S(1)}, u32[]{:S(2)}, u32[]{:S(2)}) collective-permute-start(bf16[768,256]{1,0:T(8,128)(2,1)S(1)} %get-tuple-element.72), channel_id=1, source_target_pairs={{0,8},{8,0},{16,24},{24,16},{1,9},{9,1},{17,25},{25,17},{2,10},{10... | collective-permute-start | bytes 1179656 | tf_op jit(solution)/shard_map/ppermute | solution.py:159
  73.3 1.3 %collective-permute-done.5 = bf16[768,256]{1,0:T(8,128)(2,1)S(1)} collective-permute-done((bf16[768,256]{1,0:T(8,128)(2,1)S(1)}, bf16[768,256]{1,0:T(8,128)(2,1)S(1)}, u32[]{:S(2)}, u32[]{:S(2)}) %collective-permute-start.5) | collective-permute-done | bytes 393248 | tf_op jit(solution)/shard_map/ppermute | solution.py:159
  74.6 1.1 broadcast_select_fusion.1
  75.6 16.2 %all-to-all-done.2 = bf16[16,48,512]{2,1,0:T(8,128)(2,1)S(1)} async-done(((bf16[16,48,512]{2,1,0:T(8,128)(2,1)}), bf16[16,48,512]{2,1,0:T(8,128)(2,1)S(1)}, u32[]{:S(2)}, u32[]{:S(2)}) %all-to-all-start.2) | async-done | bytes 786464 | tf_op jit(solution)/shard_map/all_to_all | solution.py:190
  91.9 0.6 convolution_convert_fusion
  92.5 5.4 %collective-permute-start.6 = (bf16[512,512]{1,0:T(8,128)(2,1)S(1)}, bf16[512,512]{1,0:T(8,128)(2,1)S(1)}, u32[]{:S(2)}, u32[]{:S(2)}) collective-permute-start(bf16[512,512]{1,0:T(8,128)(2,1)S(1)} %convolution_convert_fusion), channel_id=1, source_target_pairs={{0,8},{8,0},{1,9},{9,1},{2,10},{10,2},{3,11},{11,3},{4,12},{12,4},... | collective-permute-start | bytes 1572872 | tf_op jit(solution)/shard_map/ppermute | solution.py:200
  97.9 0.6 fusion.kept
  98.5 0.0 copy-start.10
  98.5 0.0 copy-start.9
  98.5 0.9 collective-permute-done.6.received
  99.4 0.9 shard_map.87
  100.3 10.9 %all-to-all-start.3 = ((bf16[16,64,256]{2,1,0:T(8,128)(2,1)}), bf16[16,64,256]{2,1,0:T(8,128)(2,1)S(1)}, u32[]{:S(2)}, u32[]{:S(2)}) async-start(bf16[16,64,256]{2,1,0:T(8,128)(2,1)} %bitcast.5), calls=%async_computation.3 | async-start | bytes 1048576 | tf_op jit(solution)/shard_map/all_to_all | solution.py:210
  111.2 0.0 copy-done.10
  111.3 9.4 %all-to-all-done.3 = bf16[16,64,256]{2,1,0:T(8,128)(2,1)S(1)} async-done(((bf16[16,64,256]{2,1,0:T(8,128)(2,1)}), bf16[16,64,256]{2,1,0:T(8,128)(2,1)S(1)}, u32[]{:S(2)}, u32[]{:S(2)}) %all-to-all-start.3) | async-done | bytes 524320 | tf_op jit(solution)/shard_map/all_to_all | solution.py:210
  120.7 0.1 convert_reduce_fusion
  120.7 0.0 copy-start.7
  120.8 0.7 fusion.8
  (11 shorter events, 0.0 us)
Async XLA Ops:
  0.6 22.2 %copy-start.1 = (bf16[3072,128]{1,0:T(8,128)(2,1)S(1)}, bf16[3072,128]{1,0:T(8,128)(2,1)}, u32[]{:S(2)}) copy-start(bf16[3072,128]{1,0:T(8,128)(2,1)} %own.1) | copy-start | bytes 2359300
  0.6 20.7 %collective-permute-start = (bf16[3072,128]{1,0:T(8,128)(2,1)}, bf16[3072,128]{1,0:T(8,128)(2,1)S(1)}, u32[]{:S(2)}, u32[]{:S(2)}) collective-permute-start(bf16[3072,128]{1,0:T(8,128)(2,1)} %own.1), channel_id=1, source_target_pairs={{0,8},{8,0},{1,9},{9,1},{2,10},{10,2},{3,11},{11,3},{4,12},{12,4},... | collective-permute-start | bytes 2359304 | tf_op jit(solution)/shard_map/ppermute | solution.py:88
  11.3 15.0 %collective-permute-start.3 = (bf16[768,256]{1,0:T(8,128)(2,1)}, bf16[768,256]{1,0:T(8,128)(2,1)S(1)}, u32[]{:S(2)}, u32[]{:S(2)}) collective-permute-start(bf16[768,256]{1,0:T(8,128)(2,1)} %constant_dynamic-slice_fusion.2), channel_id=1, source_target_pairs={{0,16},{8,24},{16,0},{24,8},{1,17},{9,25},{17,1},{25,9},{2,18},{10... | collective-permute-start | bytes 1179656 | tf_op jit(solution)/shard_map/ppermute | solution.py:159
  14.2 5.3 %collective-permute-start.1 = (bf16[256,128]{1,0:T(8,128)(2,1)S(1)}, bf16[256,128]{1,0:T(8,128)(2,1)S(1)}, u32[]{:S(2)}, u32[]{:S(2)}) collective-permute-start(bf16[256,128]{1,0:T(8,128)(2,1)S(1)} %get-tuple-element.76), channel_id=1, source_target_pairs={{0,1},{1,2},{2,3},{3,4},{4,5},{5,6},{6,7},{9,8},{10,9},{11,10},{12... | collective-permute-start | bytes 196616 | tf_op jit(solution)/shard_map/ppermute | solution.py:86
  15.5 5.9 %collective-permute-start.2 = (bf16[256,128]{1,0:T(8,128)(2,1)S(1)}, bf16[256,128]{1,0:T(8,128)(2,1)S(1)}, u32[]{:S(2)}, u32[]{:S(2)}) collective-permute-start(bf16[256,128]{1,0:T(8,128)(2,1)S(1)} %get-tuple-element.75), channel_id=1, source_target_pairs={{8,1},{9,2},{10,3},{11,4},{12,5},{13,6},{14,7},{1,8},{2,9},{3,10},... | collective-permute-start | bytes 196616 | tf_op jit(solution)/shard_map/ppermute | solution.py:87
  19.5 1.9 %copy-start.5 = (bf16[256,128]{1,0:T(8,128)(2,1)}, bf16[256,128]{1,0:T(8,128)(2,1)S(1)}, u32[]{:S(2)}) copy-start(bf16[256,128]{1,0:T(8,128)(2,1)S(1)} %collective-permute-done.1.own_edge) | copy-start | bytes 196612
  21.3 0.6 copy-start.6
  22.0 0.9 copy-start.2
  22.9 35.7 %copy-start = (bf16[24,3,128,128]{3,2,1,0:T(8,128)(2,1)S(1)}, bf16[24,3,128,128]{3,2,1,0:T(8,128)(2,1)}, u32[]{:S(2)}) copy-start(bf16[24,3,128,128]{3,2,1,0:T(8,128)(2,1)} %dipole.1) | copy-start | bytes 7077892
  26.4 17.7 %copy-start.8 = (s32[4]{0:T(128)S(1)}, s32[4]{0:T(128)}, u32[]{:S(2)}) copy-start(s32[4]{0:T(128)} %owners_ref.1) | copy-start | bytes 52
  26.4 0.8 copy-start.4
  27.2 31.4 %all-to-all-start.1 = ((bf16[32,48,128]{2,1,0:T(8,128)(2,1)}), bf16[32,48,128]{2,1,0:T(8,128)(2,1)S(1)}, u32[]{:S(2)}, u32[]{:S(2)}) async-start(bf16[32,48,128]{2,1,0:T(8,128)(2,1)} %bitcast.3), calls=%async_computation.1 | async-start | bytes 786432 | tf_op jit(solution)/shard_map/all_to_all | solution.py:174
  42.2 16.3 %collective-permute-start.4 = (bf16[768,256]{1,0:T(8,128)(2,1)}, bf16[768,256]{1,0:T(8,128)(2,1)}, u32[]{:S(2)}, u32[]{:S(2)}) collective-permute-start(bf16[768,256]{1,0:T(8,128)(2,1)} %constant_dynamic-slice_fusion.1), channel_id=1, source_target_pairs={{0,24},{8,16},{16,8},{24,0},{1,25},{9,17},{17,9},{25,1},{2,26},{10... | collective-permute-start | bytes 1179656 | tf_op jit(solution)/shard_map/ppermute | solution.py:159
  60.1 9.4 %copy-start.3 = (bf16[3072,256]{1,0:T(8,128)(2,1)S(1)}, bf16[3072,256]{1,0:T(8,128)(2,1)}, u32[]{:S(2)}) copy-start(bf16[3072,256]{1,0:T(8,128)(2,1)} %param.9) | copy-start | bytes 4718596
  60.1 31.7 %all-to-all-start.2 = ((bf16[16,48,512]{2,1,0:T(8,128)(2,1)}), bf16[16,48,512]{2,1,0:T(8,128)(2,1)S(1)}, u32[]{:S(2)}, u32[]{:S(2)}) async-start(bf16[16,48,512]{2,1,0:T(8,128)(2,1)} %get-tuple-element.77), calls=%async_computation.2 | async-start | bytes 1572864 | tf_op jit(solution)/shard_map/all_to_all | solution.py:190
  70.7 3.9 %collective-permute-start.5 = (bf16[768,256]{1,0:T(8,128)(2,1)S(1)}, bf16[768,256]{1,0:T(8,128)(2,1)S(1)}, u32[]{:S(2)}, u32[]{:S(2)}) collective-permute-start(bf16[768,256]{1,0:T(8,128)(2,1)S(1)} %get-tuple-element.72), channel_id=1, source_target_pairs={{0,8},{8,0},{16,24},{24,16},{1,9},{9,1},{17,25},{25,17},{2,10},{10... | collective-permute-start | bytes 1179656 | tf_op jit(solution)/shard_map/ppermute | solution.py:159
  92.5 7.0 %collective-permute-start.6 = (bf16[512,512]{1,0:T(8,128)(2,1)S(1)}, bf16[512,512]{1,0:T(8,128)(2,1)S(1)}, u32[]{:S(2)}, u32[]{:S(2)}) collective-permute-start(bf16[512,512]{1,0:T(8,128)(2,1)S(1)} %convolution_convert_fusion), channel_id=1, source_target_pairs={{0,8},{8,0},{1,9},{9,1},{2,10},{10,2},{3,11},{11,3},{4,12},{12,4},... | collective-permute-start | bytes 1572872 | tf_op jit(solution)/shard_map/ppermute | solution.py:200
  98.5 12.7 %copy-start.10 = (f32[64]{0:T(128)S(1)}, f32[64]{0:T(128)}, u32[]{:S(2)}) copy-start(f32[64]{0:T(128)} %param.14) | copy-start | bytes 772
  98.5 22.2 %copy-start.9 = (f32[256]{0:T(256)S(1)}, f32[256]{0:T(256)}, u32[]{:S(2)}) copy-start(f32[256]{0:T(256)} %param.15) | copy-start | bytes 3076
  100.3 20.3 %all-to-all-start.3 = ((bf16[16,64,256]{2,1,0:T(8,128)(2,1)}), bf16[16,64,256]{2,1,0:T(8,128)(2,1)S(1)}, u32[]{:S(2)}, u32[]{:S(2)}) async-start(bf16[16,64,256]{2,1,0:T(8,128)(2,1)} %bitcast.5), calls=%async_computation.3 | async-start | bytes 1048576 | tf_op jit(solution)/shard_map/all_to_all | solution.py:210
  120.7 0.7 copy-start.7

commit v11 on v9

--- a/solution.py
+++ b/solution.py
@@ -153,29 +153,31 @@
         start = ((core ^ flip_core) * 2 + (zlo ^ flip_zlo)) * quarter
         return lax.dynamic_slice_in_dim(rows, start, quarter, 0)
 
+    def swap(piece, flip_zlo, flip_core):
+        flip = 2 * flip_zlo + flip_core
+        return lax.ppermute(piece, SHARED, [(i, i ^ flip) for i in range(4)])
+
     def from_peer(rows, flip_zlo, flip_core):
-        flip = 2 * flip_zlo + flip_core
-        piece = mine(rows, flip_zlo, flip_core)
-        return lax.ppermute(piece, SHARED, [(i, i ^ flip) for i in range(4)])
+        return swap(mine(rows, flip_zlo, flip_core), flip_zlo, flip_core)
 
     def beside(near, far):
         low = zlo == 0
         return jnp.concatenate([jnp.where(low, near, far), jnp.where(low, far, near)], 1)
 
-    across_z = from_peer(upper_coef, 1, 0)
+    across_both = from_peer(upper_coef, 1, 1)
     panels = chip_panels(store, core)
     half = chip_half(False, state, owners, offsets, panels, dipole)
 
-    half, across_z, later = lax.optimization_barrier((half, across_z, upper_coef))
+    half, across_both, later = lax.optimization_barrier((half, across_both, upper_coef))
     across_cores = from_peer(later, 0, 1)
-    across_both = from_peer(later, 1, 1)
 
     def scatter(half):
         chips = lax.axis_size(CHIPS)
         return lax.all_to_all(half, CHIPS, 0, 0, tiled=True).reshape(chips, -1, width)
 
     pieces = scatter(half)
-    pieces, across_cores = lax.optimization_barrier((pieces, across_cores))
+    pieces, across_cores, sent = lax.optimization_barrier((pieces, across_cores, mine(later, 1, 0)))
+    across_z = swap(sent, 1, 0)
     chips_of = owners // 2
     shared = jnp.sum((chips_of[:, None] == chips_of[None, :]).astype(jnp.int32)) > PANELS
     copies = lax.cond(

time: 111 us -> 113 us (1.018)
  waiting for transfers between devices: 46.1 us -> 40.6 us
  starting transfers between devices: 46.7 us -> 51.2 us
  local copies, waits for them, and re-layouts: 1.85 us -> 6.34 us
  other arithmetic: 6.37 us -> 4.57 us
    ppermute x3, waiting for transfers between devices: 24.8 us -> 0.78 us  [swap(): return lax.ppermute(piece, SHARED, [(i, i ^ flip) for i in range(4)])]
    all_to_all x1, waiting for transfers between devices: 0.01 us -> 19.4 us  [on_device(): lax.all_to_all(copies.reshape(-1, lowers), GATHER, 0, 0, tiled=True)]
    dynamic_slice x1 -> x2, local copies, waits for them, and re-layouts: 1.03 us -> 3.87 us  [mine(): return lax.dynamic_slice_in_dim(rows, start, quarter, 0)]
    ppermute x1, starting transfers between devices: 2.31 us -> 4.61 us  [on_device(): received = lax.ppermute(share(upper_other).astype(BF16), 'core', SWAP)]
    all_to_all x1, starting transfers between devices: 7.38 us -> 9.16 us  [on_device(): shares = lax.all_to_all(added, BASIS + ('zlo',), 0, 0, tiled=True)]
    select_n x2, other arithmetic: 3.96 us -> 2.2 us  [beside(): jnp.where(low, near, far)]
    unnamed x27 -> x25, local copies, waits for them, and re-layouts: 0.83 us -> 2.47 us
  transfers between devices with their start and end apart: 10 -> 10, of which waited for: 7 -> 6; matrix products, arithmetic and copies ran while one was open for 7% -> 9% of each run, Pallas kernels for 3% -> 3%
where the time goes in v11:
time: 113 us; the launch traced here: 111 us
  starting transfers between devices  51.2 us (45%)
  waiting for transfers between devices  40.6 us (36%)
  local copies, waits for them, and re-layouts  6.34 us (6%)
  Pallas kernels  5.58 us (5%)
  other arithmetic  4.57 us (4%)
  between operations  1.48 us (1%)
  matrix products  1.19 us (1%)
    all_to_all x1, waiting for transfers between devices, on_device(): lax.all_to_all(copies.reshape(-1, lowers), GATHER, 0, 0, tiled=True)  19.4 us
    all_to_all x1, starting transfers between devices, scatter(): lax.all_to_all(half, CHIPS, 0, 0, tiled=True).reshape(chips, -1, width)  13.2 us
    all_to_all x1, waiting for transfers between devices, on_device(): shares = lax.all_to_all(added, BASIS + ('zlo',), 0, 0, tiled=True)  9.74 us
    all_to_all x1, starting transfers between devices, on_device(): shares = lax.all_to_all(added, BASIS + ('zlo',), 0, 0, tiled=True)  9.16 us
    ppermute x1, starting transfers between devices, chip_panels(): other = lax.ppermute(store, 'core', SWAP)  8.92 us
    all_to_all x1, waiting for transfers between devices, scatter(): lax.all_to_all(half, CHIPS, 0, 0, tiled=True).reshape(chips, -1, width)  7.85 us
    ppermute x3, starting transfers between devices, swap(): return lax.ppermute(piece, SHARED, [(i, i ^ flip) for i in range(4)])  6.57 us
    all_to_all x1, starting transfers between devices, on_device(): lax.all_to_all(copies.reshape(-1, lowers), GATHER, 0, 0, tiled=True)  5.22 us
  transfers between devices with their start and end apart: 10, of which 6 were waited for; matrix products, arithmetic and copies ran while one was open for 9% of the time, Pallas kernels for 3%

profile of v11, /device:TPU:1, one launch (start us, length us, event | category | flops | bytes accessed | tf_op | source)
XLA Modules:
  0.0 111.0 jit_solution(15821867297849404206)
XLA Ops:
  0.6 0.0 copy-start.1
  0.6 8.9 %collective-permute-start = (bf16[3072,128]{1,0:T(8,128)(2,1)}, bf16[3072,128]{1,0:T(8,128)(2,1)S(1)}, u32[]{:S(2)}, u32[]{:S(2)}) collective-permute-start(bf16[3072,128]{1,0:T(8,128)(2,1)} %own.1), channel_id=1, source_target_pairs={{0,8},{8,0},{1,9},{9,1},{2,10},{10,2},{3,11},{11,3},{4,12},{12,4},... | collective-permute-start | bytes 2359304 | tf_op jit(solution)/shard_map/ppermute | solution.py:88
  9.6 1.8 %constant_dynamic-slice_fusion.2 = bf16[768,256]{1,0:T(8,128)(2,1)} fusion(bf16[3072,256]{1,0:T(8,128)(2,1)} %param.9, s32[]{:T(128)S(6)} %select_n.53), kind=kLoop, calls=%fused_computation.28 | loop fusion | bytes 786436 | tf_op jit(solution)/shard_map/dynamic_slice | solution.py:154
  11.4 1.9 %collective-permute-start.3 = (bf16[768,256]{1,0:T(8,128)(2,1)}, bf16[768,256]{1,0:T(8,128)(2,1)S(1)}, u32[]{:S(2)}, u32[]{:S(2)}) collective-permute-start(bf16[768,256]{1,0:T(8,128)(2,1)} %constant_dynamic-slice_fusion.2), channel_id=1, source_target_pairs={{0,24},{8,16},{16,8},{24,0},{1,25},{9,17},{17,9},{25,1},{2,26},{10... | collective-permute-start | bytes 1179656 | tf_op jit(solution)/shard_map/ppermute | solution.py:158
  13.3 0.9 broadcast_select_fusion.4
  14.2 1.3 %collective-permute-start.1 = (bf16[256,128]{1,0:T(8,128)(2,1)S(1)}, bf16[256,128]{1,0:T(8,128)(2,1)S(1)}, u32[]{:S(2)}, u32[]{:S(2)}) collective-permute-start(bf16[256,128]{1,0:T(8,128)(2,1)S(1)} %get-tuple-element.75), channel_id=1, source_target_pairs={{0,1},{1,2},{2,3},{3,4},{4,5},{5,6},{6,7},{9,8},{10,9},{11,10},{12... | collective-permute-start | bytes 196616 | tf_op jit(solution)/shard_map/ppermute | solution.py:86
  15.5 2.2 %collective-permute-start.2 = (bf16[256,128]{1,0:T(8,128)(2,1)S(1)}, bf16[256,128]{1,0:T(8,128)(2,1)S(1)}, u32[]{:S(2)}, u32[]{:S(2)}) collective-permute-start(bf16[256,128]{1,0:T(8,128)(2,1)S(1)} %get-tuple-element.74), channel_id=1, source_target_pairs={{8,1},{9,2},{10,3},{11,4},{12,5},{13,6},{14,7},{1,8},{2,9},{3,10},... | collective-permute-start | bytes 196616 | tf_op jit(solution)/shard_map/ppermute | solution.py:87
  17.7 0.8 copy.11.offsets_ref
  18.5 1.0 collective-permute-done.1.own_edge
  19.5 1.9 %collective-permute-done.2.other_edge = bf16[256,128]{1,0:T(8,128)(2,1)S(1)} collective-permute-done((bf16[256,128]{1,0:T(8,128)(2,1)S(1)}, bf16[256,128]{1,0:T(8,128)(2,1)S(1)}, u32[]{:S(2)}, u32[]{:S(2)}) %collective-permute-start.2) | collective-permute-done | bytes 65568 | tf_op jit(solution)/shard_map/ppermute | solution.py:87
  21.4 0.0 collective-permute-done.other
  21.4 0.0 copy-done.6
  21.4 0.6 copy-done.7
  22.0 0.3 copy-done.2
  22.3 0.0 copy-done.1
  22.3 3.1 %shard_map.86 = bf16[1536,128]{1,0:T(8,128)(2,1)} custom-call(s32[1]{0:T(128)} %bitcast.2.state_ref, s32[4]{0:T(128)} %owners_ref.1, s32[24,3]{1,0:T(8,128)S(1)} %copy.11.offsets_ref, bf16[3072,128]{1,0:T(8,128)(2,1)S(1)} %copy-done.1, bf16[3072,128]{1,0:T(8,128)(2,1)S(1)} %collective-permute-done.other, ...), custom_call_target="tpu_custom_call" | custom-call | flops 150994944 | bytes 6291456 | tf_op jit(solution)/shard_map/pallas_call | solution.py:95
  25.3 0.0 collective-permute-done.3
  25.4 0.0 copy-start.3
  25.4 0.8 copy-done.3
  26.1 13.2 %all-to-all-start.1 = ((bf16[32,48,128]{2,1,0:T(8,128)(2,1)}), bf16[32,48,128]{2,1,0:T(8,128)(2,1)S(1)}, u32[]{:S(2)}, u32[]{:S(2)}) async-start(bf16[32,48,128]{2,1,0:T(8,128)(2,1)} %bitcast.3), calls=%async_computation.1 | async-start | bytes 786432 | tf_op jit(solution)/shard_map/all_to_all | solution.py:176
  39.3 2.1 %constant_dynamic-slice_fusion = (bf16[768,256]{1,0:T(8,128)(2,1)}, bf16[768,256]{1,0:T(8,128)(2,1)}) fusion(bf16[3072,256]{1,0:T(8,128)(2,1)} %param.9, s32[]{:T(128)S(6)} %select_n.55, s32[]{:T(128)S(6)} %select_n.54), kind=kLoop, calls=%fused_computation.26 | loop fusion | bytes 1572872 | tf_op jit(solution)/shard_map/dynamic_slice | solution.py:154
  41.4 1.9 %collective-permute-start.4 = (bf16[768,256]{1,0:T(8,128)(2,1)}, bf16[768,256]{1,0:T(8,128)(2,1)}, u32[]{:S(2)}, u32[]{:S(2)}) collective-permute-start(bf16[768,256]{1,0:T(8,128)(2,1)} %get-tuple-element.71), channel_id=1, source_target_pairs={{0,8},{8,0},{16,24},{24,16},{1,9},{9,1},{17,25},{25,17},{2,10},{10... | collective-permute-start | bytes 1179656 | tf_op jit(solution)/shard_map/ppermute | solution.py:158
  43.3 0.0 copy-done.9
  43.4 0.7 convert_reduce_fusion.1
  44.6 0.8 collective-permute-done.4
  45.4 7.8 %all-to-all-done.1 = bf16[32,48,128]{2,1,0:T(8,128)(2,1)S(1)} async-done(((bf16[32,48,128]{2,1,0:T(8,128)(2,1)}), bf16[32,48,128]{2,1,0:T(8,128)(2,1)S(1)}, u32[]{:S(2)}, u32[]{:S(2)}) %all-to-all-start.1) | async-done | bytes 393248 | tf_op jit(solution)/shard_map/all_to_all | solution.py:176
  53.2 0.0 copy-done
  53.2 1.6 %conditional.1 = (bf16[16,48,512]{2,1,0:T(8,128)(2,1)}) conditional(s32[]{:T(128)} %convert_element_type.13, (s32[4]{0:T(128)S(1)}, bf16[32,48,128]{2,1,0:T(8,128)(2,1)S(1)}) %tuple.34, (s32[]{:T(128)}, s32[4]{0:T(128)S(1)}, s32[24,3]{0,1:T(4,128)}, bf16[3072,128]{1,0:T(8,128)(2,1)S(1)}, bf16[3072,128]{1,0:T(8,128)(2,1)}, ...), branch_computations={%region_1.2_spmd, %region_2.3_spmd} | conditional | flops 150994944 | bytes 8127048 | solution.py:183
  53.2 1.6 %branch_0_fun.1 = bf16[16,48,512]{2,1,0:T(8,128)(2,1)} custom-call(s32[4]{0:T(128)S(1)} %get-tuple-element.12.owners_ref, bf16[32,48,128]{2,1,0:T(8,128)(2,1)S(1)} %get-tuple-element.26.pieces.seconds, bf16[32,48,128]{2,1,0:T(8,128)(2,1)S(1)} %get-tuple-element.26.pieces.seconds), custom_call_target="tpu_custom_call" | custom-call | bytes 1048576 | tf_op jit(solution)/shard_map/cond/branch_0_fun/pallas_call | solution.py:122
  54.9 5.2 %all-to-all-start.2 = ((bf16[16,48,512]{2,1,0:T(8,128)(2,1)}), bf16[16,48,512]{2,1,0:T(8,128)(2,1)S(1)}, u32[]{:S(2)}, u32[]{:S(2)}) async-start(bf16[16,48,512]{2,1,0:T(8,128)(2,1)} %get-tuple-element.76), calls=%async_computation.2 | async-start | bytes 1572864 | tf_op jit(solution)/shard_map/all_to_all | solution.py:190
  60.1 0.0 copy-done.5
  60.1 2.8 %collective-permute-start.5 = (bf16[768,256]{1,0:T(8,128)(2,1)S(1)}, bf16[768,256]{1,0:T(8,128)(2,1)S(1)}, u32[]{:S(2)}, u32[]{:S(2)}) collective-permute-start(bf16[768,256]{1,0:T(8,128)(2,1)S(1)} %copy-done.5), channel_id=1, source_target_pairs={{0,16},{8,24},{16,0},{24,8},{1,17},{9,25},{17,1},{25,9},{2,18},{10... | collective-permute-start | bytes 1179656 | tf_op jit(solution)/shard_map/ppermute | solution.py:158
  62.9 1.1 broadcast_select_fusion.1
  63.9 19.4 %all-to-all-done.2 = bf16[16,48,512]{2,1,0:T(8,128)(2,1)S(1)} async-done(((bf16[16,48,512]{2,1,0:T(8,128)(2,1)}), bf16[16,48,512]{2,1,0:T(8,128)(2,1)S(1)}, u32[]{:S(2)}, u32[]{:S(2)}) %all-to-all-start.2) | async-done | bytes 786464 | tf_op jit(solution)/shard_map/all_to_all | solution.py:190
  83.3 0.6 convolution_convert_fusion
  83.9 4.6 %collective-permute-start.6 = (bf16[512,512]{1,0:T(8,128)(2,1)S(1)}, bf16[512,512]{1,0:T(8,128)(2,1)S(1)}, u32[]{:S(2)}, u32[]{:S(2)}) collective-permute-start(bf16[512,512]{1,0:T(8,128)(2,1)S(1)} %convolution_convert_fusion), channel_id=1, source_target_pairs={{0,8},{8,0},{1,9},{9,1},{2,10},{10,2},{3,11},{11,3},{4,12},{12,4},... | collective-permute-start | bytes 1572872 | tf_op jit(solution)/shard_map/ppermute | solution.py:200
  88.5 0.0 collective-permute-done.5
  88.5 1.2 %broadcast_select_fusion.3 = (bf16[768,256]{1,0:T(8,128)(2,1)S(1)}, bf16[768,256]{1,0:T(8,128)(2,1)S(1)}) fusion(bf16[768,256]{1,0:T(8,128)(2,1)S(1)} %collective-permute-done.5, pred[]{:T(512)S(6)} %eq.24, bf16[3072,256]{1,0:T(8,128)(2,1)} %param.9, s32[]{:T(128)S(6)} %select_n.57), kind=kLoop, calls=%fused_computation.12 | loop fusion | flops 393216 | bytes 1572869 | tf_op jit(solution)/shard_map/jit(_where)/select_n | solution.py:165
  89.7 0.6 fusion.kept
  90.3 0.0 copy-start.11
  90.3 0.0 copy-start.10
  90.3 0.0 collective-permute-done.6.received
  90.3 0.9 shard_map.87
  91.2 9.2 %all-to-all-start.3 = ((bf16[16,64,256]{2,1,0:T(8,128)(2,1)}), bf16[16,64,256]{2,1,0:T(8,128)(2,1)S(1)}, u32[]{:S(2)}, u32[]{:S(2)}) async-start(bf16[16,64,256]{2,1,0:T(8,128)(2,1)} %bitcast.5), calls=%async_computation.3 | async-start | bytes 1048576 | tf_op jit(solution)/shard_map/all_to_all | solution.py:210
  100.4 9.7 %all-to-all-done.3 = bf16[16,64,256]{2,1,0:T(8,128)(2,1)S(1)} async-done(((bf16[16,64,256]{2,1,0:T(8,128)(2,1)}), bf16[16,64,256]{2,1,0:T(8,128)(2,1)S(1)}, u32[]{:S(2)}, u32[]{:S(2)}) %all-to-all-start.3) | async-done | bytes 524320 | tf_op jit(solution)/shard_map/all_to_all | solution.py:210
  110.1 0.1 convert_reduce_fusion
  110.2 0.0 copy-start.8
  110.2 0.7 fusion.8
  (13 shorter events, 0.0 us)
Async XLA Ops:
  0.6 21.6 %copy-start.1 = (bf16[3072,128]{1,0:T(8,128)(2,1)S(1)}, bf16[3072,128]{1,0:T(8,128)(2,1)}, u32[]{:S(2)}) copy-start(bf16[3072,128]{1,0:T(8,128)(2,1)} %own.1) | copy-start | bytes 2359300
  0.6 20.7 %collective-permute-start = (bf16[3072,128]{1,0:T(8,128)(2,1)}, bf16[3072,128]{1,0:T(8,128)(2,1)S(1)}, u32[]{:S(2)}, u32[]{:S(2)}) collective-permute-start(bf16[3072,128]{1,0:T(8,128)(2,1)} %own.1), channel_id=1, source_target_pairs={{0,8},{8,0},{1,9},{9,1},{2,10},{10,2},{3,11},{11,3},{4,12},{12,4},... | collective-permute-start | bytes 2359304 | tf_op jit(solution)/shard_map/ppermute | solution.py:88
  11.4 14.0 %collective-permute-start.3 = (bf16[768,256]{1,0:T(8,128)(2,1)}, bf16[768,256]{1,0:T(8,128)(2,1)S(1)}, u32[]{:S(2)}, u32[]{:S(2)}) collective-permute-start(bf16[768,256]{1,0:T(8,128)(2,1)} %constant_dynamic-slice_fusion.2), channel_id=1, source_target_pairs={{0,24},{8,16},{16,8},{24,0},{1,25},{9,17},{17,9},{25,1},{2,26},{10... | collective-permute-start | bytes 1179656 | tf_op jit(solution)/shard_map/ppermute | solution.py:158
  14.2 5.3 %collective-permute-start.1 = (bf16[256,128]{1,0:T(8,128)(2,1)S(1)}, bf16[256,128]{1,0:T(8,128)(2,1)S(1)}, u32[]{:S(2)}, u32[]{:S(2)}) collective-permute-start(bf16[256,128]{1,0:T(8,128)(2,1)S(1)} %get-tuple-element.75), channel_id=1, source_target_pairs={{0,1},{1,2},{2,3},{3,4},{4,5},{5,6},{6,7},{9,8},{10,9},{11,10},{12... | collective-permute-start | bytes 196616 | tf_op jit(solution)/shard_map/ppermute | solution.py:86
  15.5 5.9 %collective-permute-start.2 = (bf16[256,128]{1,0:T(8,128)(2,1)S(1)}, bf16[256,128]{1,0:T(8,128)(2,1)S(1)}, u32[]{:S(2)}, u32[]{:S(2)}) collective-permute-start(bf16[256,128]{1,0:T(8,128)(2,1)S(1)} %get-tuple-element.74), channel_id=1, source_target_pairs={{8,1},{9,2},{10,3},{11,4},{12,5},{13,6},{14,7},{1,8},{2,9},{3,10},... | collective-permute-start | bytes 196616 | tf_op jit(solution)/shard_map/ppermute | solution.py:87
  19.5 1.9 %copy-start.6 = (bf16[256,128]{1,0:T(8,128)(2,1)}, bf16[256,128]{1,0:T(8,128)(2,1)S(1)}, u32[]{:S(2)}) copy-start(bf16[256,128]{1,0:T(8,128)(2,1)S(1)} %collective-permute-done.1.own_edge) | copy-start | bytes 196612
  21.4 0.6 copy-start.7
  21.4 0.9 copy-start.2
  25.3 18.0 %copy-start.9 = (s32[4]{0:T(128)S(1)}, s32[4]{0:T(128)}, u32[]{:S(2)}) copy-start(s32[4]{0:T(128)} %owners_ref.1) | copy-start | bytes 52
  25.3 27.9 %copy-start = (bf16[24,3,128,128]{3,2,1,0:T(8,128)(2,1)S(1)}, bf16[24,3,128,128]{3,2,1,0:T(8,128)(2,1)}, u32[]{:S(2)}) copy-start(bf16[24,3,128,128]{3,2,1,0:T(8,128)(2,1)} %dipole.1) | copy-start | bytes 7077892
  25.4 0.8 copy-start.3
  26.1 27.1 %all-to-all-start.1 = ((bf16[32,48,128]{2,1,0:T(8,128)(2,1)}), bf16[32,48,128]{2,1,0:T(8,128)(2,1)S(1)}, u32[]{:S(2)}, u32[]{:S(2)}) async-start(bf16[32,48,128]{2,1,0:T(8,128)(2,1)} %bitcast.3), calls=%async_computation.1 | async-start | bytes 786432 | tf_op jit(solution)/shard_map/all_to_all | solution.py:176
  41.4 3.9 %collective-permute-start.4 = (bf16[768,256]{1,0:T(8,128)(2,1)}, bf16[768,256]{1,0:T(8,128)(2,1)}, u32[]{:S(2)}, u32[]{:S(2)}) collective-permute-start(bf16[768,256]{1,0:T(8,128)(2,1)} %get-tuple-element.71), channel_id=1, source_target_pairs={{0,8},{8,0},{16,24},{24,16},{1,9},{9,1},{17,25},{25,17},{2,10},{10... | collective-permute-start | bytes 1179656 | tf_op jit(solution)/shard_map/ppermute | solution.py:158
  54.9 5.2 %copy-start.5 = (bf16[768,256]{1,0:T(8,128)(2,1)S(1)}, bf16[768,256]{1,0:T(8,128)(2,1)}, u32[]{:S(2)}) copy-start(bf16[768,256]{1,0:T(8,128)(2,1)} %get-tuple-element.47) | copy-start | bytes 1179652
  54.9 8.0 %copy-start.4 = (bf16[768,256]{1,0:T(8,128)(2,1)S(1)}, bf16[768,256]{1,0:T(8,128)(2,1)}, u32[]{:S(2)}) copy-start(bf16[768,256]{1,0:T(8,128)(2,1)} %copy-done.3) | copy-start | bytes 1179652
  54.9 28.4 %all-to-all-start.2 = ((bf16[16,48,512]{2,1,0:T(8,128)(2,1)}), bf16[16,48,512]{2,1,0:T(8,128)(2,1)S(1)}, u32[]{:S(2)}, u32[]{:S(2)}) async-start(bf16[16,48,512]{2,1,0:T(8,128)(2,1)} %get-tuple-element.76), calls=%async_computation.2 | async-start | bytes 1572864 | tf_op jit(solution)/shard_map/all_to_all | solution.py:190
  60.1 28.4 %collective-permute-start.5 = (bf16[768,256]{1,0:T(8,128)(2,1)S(1)}, bf16[768,256]{1,0:T(8,128)(2,1)S(1)}, u32[]{:S(2)}, u32[]{:S(2)}) collective-permute-start(bf16[768,256]{1,0:T(8,128)(2,1)S(1)} %copy-done.5), channel_id=1, source_target_pairs={{0,16},{8,24},{16,0},{24,8},{1,17},{9,25},{17,1},{25,9},{2,18},{10... | collective-permute-start | bytes 1179656 | tf_op jit(solution)/shard_map/ppermute | solution.py:158
  83.9 6.4 %collective-permute-start.6 = (bf16[512,512]{1,0:T(8,128)(2,1)S(1)}, bf16[512,512]{1,0:T(8,128)(2,1)S(1)}, u32[]{:S(2)}, u32[]{:S(2)}) collective-permute-start(bf16[512,512]{1,0:T(8,128)(2,1)S(1)} %convolution_convert_fusion), channel_id=1, source_target_pairs={{0,8},{8,0},{1,9},{9,1},{2,10},{10,2},{3,11},{11,3},{4,12},{12,4},... | collective-permute-start | bytes 1572872 | tf_op jit(solution)/shard_map/ppermute | solution.py:200
  90.3 10.1 %copy-start.11 = (f32[64]{0:T(128)S(1)}, f32[64]{0:T(128)}, u32[]{:S(2)}) copy-start(f32[64]{0:T(128)} %param.14) | copy-start | bytes 772
  90.3 19.9 %copy-start.10 = (f32[256]{0:T(256)S(1)}, f32[256]{0:T(256)}, u32[]{:S(2)}) copy-start(f32[256]{0:T(256)} %param.15) | copy-start | bytes 3076
  91.2 18.9 %all-to-all-start.3 = ((bf16[16,64,256]{2,1,0:T(8,128)(2,1)}), bf16[16,64,256]{2,1,0:T(8,128)(2,1)S(1)}, u32[]{:S(2)}, u32[]{:S(2)}) async-start(bf16[16,64,256]{2,1,0:T(8,128)(2,1)} %bitcast.5), calls=%async_computation.3 | async-start | bytes 1048576 | tf_op jit(solution)/shard_map/all_to_all | solution.py:210
  110.2 0.7 copy-start.8

commit v12 on v9

--- a/solution.py
+++ b/solution.py
@@ -104,7 +104,7 @@
     )(state.reshape(1), owners, offsets, *panels, dipole)
 
 
-def pick_kernel(owners_ref, pieces, seconds, copies, chunk):
+def pick_kernel(owners_ref, pieces, seconds, copies, chunk, sems):
     width = pieces.shape[2]
     for p in range(PANELS):
         owner = owners_ref[p]
@@ -112,8 +112,13 @@
         chip = (zlo * SIZES["yhi"] + yhi) * SIZES["zhi"] + zhi
         late = (core == 1) & owned(owners_ref, owner - 1)
         chunk[:, pl.ds(p * width, width)] = jnp.where(late, seconds[chip], pieces[chip])
-    for i in range(copies.shape[0]):
-        copies[i] = chunk[...]
+    sends = [
+        pltpu.make_async_copy(chunk, copies.at[i], sems.at[i]) for i in range(copies.shape[0])
+    ]
+    for send in sends:
+        send.start()
+    for send in sends:
+        send.wait()
 
 
 def pick(owners, pieces, seconds):
@@ -123,8 +128,11 @@
         pick_kernel,
         out_shape=jax.ShapeDtypeStruct((peers, rows, PANELS * width), BF16),
         in_specs=[SMEM, VMEM, VMEM],
-        out_specs=VMEM,
-        scratch_shapes=[pltpu.VMEM((rows, PANELS * width), BF16)],
+        out_specs=pl.BlockSpec(memory_space=pl.ANY),
+        scratch_shapes=[
+            pltpu.VMEM((rows, PANELS * width), BF16),
+            pltpu.SemaphoreType.DMA((peers,)),
+        ],
         compiler_params=pltpu.CompilerParams(vmem_limit_bytes=8 << 20),
         cost_estimate=pl.CostEstimate(flops=0, bytes_accessed=1 << 20, transcendentals=0),
     )(owners, pieces, seconds)

time: 111 us -> 111 us (level)
  no operation moved by 1% of the time
where the time goes in v12:
time: 111 us; the launch traced here: 110 us
  starting transfers between devices  46.7 us (42%)
  waiting for transfers between devices  46.1 us (42%)
  other arithmetic  6.37 us (6%)
  Pallas kernels  5.99 us (5%)
  local copies, waits for them, and re-layouts  1.86 us (2%)
  between operations  1.61 us (1%)
  matrix products  1.19 us (1%)
    ppermute x3, waiting for transfers between devices, from_peer(): return lax.ppermute(piece, SHARED, [(i, i ^ flip) for i in range(4)])  24.8 us
    all_to_all x1, starting transfers between devices, scatter(): lax.all_to_all(half, CHIPS, 0, 0, tiled=True).reshape(chips, -1, width)  13.3 us
    all_to_all x1, waiting for transfers between devices, on_device(): shares = lax.all_to_all(added, BASIS + ('zlo',), 0, 0, tiled=True)  9.39 us
    ppermute x1, starting transfers between devices, chip_panels(): other = lax.ppermute(store, 'core', SWAP)  8.92 us
    all_to_all x1, waiting for transfers between devices, scatter(): lax.all_to_all(half, CHIPS, 0, 0, tiled=True).reshape(chips, -1, width)  8.03 us
    all_to_all x1, starting transfers between devices, on_device(): shares = lax.all_to_all(added, BASIS + ('zlo',), 0, 0, tiled=True)  7.38 us
    ppermute x3, starting transfers between devices, from_peer(): return lax.ppermute(piece, SHARED, [(i, i ^ flip) for i in range(4)])  7.14 us
    all_to_all x1, starting transfers between devices, on_device(): lax.all_to_all(copies.reshape(-1, lowers), GATHER, 0, 0, tiled=True)  4.27 us
  transfers between devices with their start and end apart: 10, of which 7 were waited for; matrix products, arithmetic and copies ran while one was open for 7% of the time, Pallas kernels for 3%

profile of v12, /device:TPU:1, one launch (start us, length us, event | category | flops | bytes accessed | tf_op | source)
XLA Modules:
  0.0 109.8 jit_solution(10130386733653412124)
XLA Ops:
  0.6 0.0 copy-start.1
  0.6 8.9 %collective-permute-start = (bf16[3072,128]{1,0:T(8,128)(2,1)}, bf16[3072,128]{1,0:T(8,128)(2,1)S(1)}, u32[]{:S(2)}, u32[]{:S(2)}) collective-permute-start(bf16[3072,128]{1,0:T(8,128)(2,1)} %own.1), channel_id=1, source_target_pairs={{0,8},{8,0},{1,9},{9,1},{2,10},{10,2},{3,11},{11,3},{4,12},{12,4},... | collective-permute-start | bytes 2359304 | tf_op jit(solution)/shard_map/ppermute | solution.py:88
  9.6 1.0 constant_dynamic-slice_fusion.2
  10.6 1.9 %collective-permute-start.3 = (bf16[768,256]{1,0:T(8,128)(2,1)S(1)}, bf16[768,256]{1,0:T(8,128)(2,1)S(1)}, u32[]{:S(2)}, u32[]{:S(2)}) collective-permute-start(bf16[768,256]{1,0:T(8,128)(2,1)S(1)} %constant_dynamic-slice_fusion.2), channel_id=1, source_target_pairs={{0,16},{8,24},{16,0},{24,8},{1,17},{9,25},{17,1},{25,9},{2,18},{10... | collective-permute-start | bytes 1179656 | tf_op jit(solution)/shard_map/ppermute | solution.py:167
  12.5 0.9 broadcast_select_fusion.4
  13.4 1.3 %collective-permute-start.1 = (bf16[256,128]{1,0:T(8,128)(2,1)S(1)}, bf16[256,128]{1,0:T(8,128)(2,1)S(1)}, u32[]{:S(2)}, u32[]{:S(2)}) collective-permute-start(bf16[256,128]{1,0:T(8,128)(2,1)S(1)} %get-tuple-element.73), channel_id=1, source_target_pairs={{0,1},{1,2},{2,3},{3,4},{4,5},{5,6},{6,7},{9,8},{10,9},{11,10},{12... | collective-permute-start | bytes 196616 | tf_op jit(solution)/shard_map/ppermute | solution.py:86
  14.7 2.1 %collective-permute-start.2 = (bf16[256,128]{1,0:T(8,128)(2,1)S(1)}, bf16[256,128]{1,0:T(8,128)(2,1)S(1)}, u32[]{:S(2)}, u32[]{:S(2)}) collective-permute-start(bf16[256,128]{1,0:T(8,128)(2,1)S(1)} %get-tuple-element.72), channel_id=1, source_target_pairs={{8,1},{9,2},{10,3},{11,4},{12,5},{13,6},{14,7},{1,8},{2,9},{3,10},... | collective-permute-start | bytes 196616 | tf_op jit(solution)/shard_map/ppermute | solution.py:87
  16.9 0.8 copy.11.offsets_ref
  17.6 1.1 %collective-permute-done.1.own_edge = bf16[256,128]{1,0:T(8,128)(2,1)S(1)} collective-permute-done((bf16[256,128]{1,0:T(8,128)(2,1)S(1)}, bf16[256,128]{1,0:T(8,128)(2,1)S(1)}, u32[]{:S(2)}, u32[]{:S(2)}) %collective-permute-start.1) | collective-permute-done | bytes 65568 | tf_op jit(solution)/shard_map/ppermute | solution.py:86
  18.7 1.9 %collective-permute-done.2.other_edge = bf16[256,128]{1,0:T(8,128)(2,1)S(1)} collective-permute-done((bf16[256,128]{1,0:T(8,128)(2,1)S(1)}, bf16[256,128]{1,0:T(8,128)(2,1)S(1)}, u32[]{:S(2)}, u32[]{:S(2)}) %collective-permute-start.2) | collective-permute-done | bytes 65568 | tf_op jit(solution)/shard_map/ppermute | solution.py:87
  20.6 0.0 collective-permute-done.other
  20.6 0.0 copy-done.1
  20.6 3.4 %shard_map.86 = bf16[1536,128]{1,0:T(8,128)(2,1)} custom-call(s32[1]{0:T(128)} %bitcast.2.state_ref, s32[4]{0:T(128)} %owners_ref.1, s32[24,3]{1,0:T(8,128)S(1)} %copy.11.offsets_ref, bf16[3072,128]{1,0:T(8,128)(2,1)S(1)} %copy-done.1, bf16[3072,128]{1,0:T(8,128)(2,1)S(1)} %collective-permute-done.other, ...), custom_call_target="tpu_custom_call" | custom-call | flops 150994944 | bytes 6291456 | tf_op jit(solution)/shard_map/pallas_call | solution.py:95
  24.0 0.0 copy-done.7
  24.0 0.0 copy-done.8
  24.0 0.0 copy-done.2
  24.0 0.0 collective-permute-done.3
  24.0 0.0 copy-start.3
  24.0 13.3 %all-to-all-start.1 = ((bf16[32,48,128]{2,1,0:T(8,128)(2,1)}), bf16[32,48,128]{2,1,0:T(8,128)(2,1)S(1)}, u32[]{:S(2)}, u32[]{:S(2)}) async-start(bf16[32,48,128]{2,1,0:T(8,128)(2,1)} %bitcast.3), calls=%async_computation.1 | async-start | bytes 786432 | tf_op jit(solution)/shard_map/all_to_all | solution.py:183
  37.3 0.0 copy-start.10
  37.4 0.0 copy-start
  37.4 2.9 %broadcast_select_fusion.3 = (bf16[768,256]{1,0:T(8,128)(2,1)}, bf16[768,256]{1,0:T(8,128)(2,1)}, bf16[768,256]{1,0:T(8,128)(2,1)}, bf16[768,256]{1,0:T(8,128)(2,1)}) fusion(bf16[768,256]{1,0:T(8,128)(2,1)} %copy-done.3, pred[]{:T(512)S(6)} %eq.24, bf16[3072,256]{1,0:T(8,128)(2,1)} %param.9, s32[]{:T(128)S(6)} %select_n.56, s32[]{:T(128)S(6)} %select_n.59, ...), kind=kLoop, calls=%fused_computation.12 | loop fusion | flops 393216 | bytes 3145741 | tf_op jit(solution)/shard_map/jit(_where)/select_n | solution.py:171
  40.3 1.9 %collective-permute-start.4 = (bf16[768,256]{1,0:T(8,128)(2,1)}, bf16[768,256]{1,0:T(8,128)(2,1)}, u32[]{:S(2)}, u32[]{:S(2)}) collective-permute-start(bf16[768,256]{1,0:T(8,128)(2,1)} %get-tuple-element.69), channel_id=1, source_target_pairs={{0,8},{8,0},{16,24},{24,16},{1,9},{9,1},{17,25},{25,17},{2,10},{10... | collective-permute-start | bytes 1179656 | tf_op jit(solution)/shard_map/ppermute | solution.py:167
  42.2 0.7 convert_reduce_fusion.1
  43.6 0.7 collective-permute-done.4
  44.2 8.0 %all-to-all-done.1 = bf16[32,48,128]{2,1,0:T(8,128)(2,1)S(1)} async-done(((bf16[32,48,128]{2,1,0:T(8,128)(2,1)}), bf16[32,48,128]{2,1,0:T(8,128)(2,1)S(1)}, u32[]{:S(2)}, u32[]{:S(2)}) %all-to-all-start.1) | async-done | bytes 393248 | tf_op jit(solution)/shard_map/all_to_all | solution.py:183
  52.3 0.0 copy-done
  52.3 1.7 %conditional.1 = (bf16[16,48,512]{2,1,0:T(8,128)(2,1)}) conditional(s32[]{:T(128)} %convert_element_type.13, (s32[4]{0:T(128)S(1)}, bf16[32,48,128]{2,1,0:T(8,128)(2,1)S(1)}) %tuple.35, (s32[]{:T(128)}, s32[4]{0:T(128)S(1)}, s32[24,3]{0,1:T(4,128)}, bf16[3072,128]{1,0:T(8,128)(2,1)S(1)}, bf16[3072,128]{1,0:T(8,128)(2,1)}, ...), branch_computations={%region_1.2_spmd, %region_2.3_spmd} | conditional | flops 150994944 | bytes 8127048 | solution.py:189
  52.3 1.7 %branch_0_fun.1 = bf16[16,48,512]{2,1,0:T(8,128)(2,1)} custom-call(s32[4]{0:T(128)S(1)} %get-tuple-element.12.owners_ref, bf16[32,48,128]{2,1,0:T(8,128)(2,1)S(1)} %get-tuple-element.26.pieces.seconds, bf16[32,48,128]{2,1,0:T(8,128)(2,1)S(1)} %get-tuple-element.26.pieces.seconds), custom_call_target="tpu_custom_call" | custom-call | bytes 1048576 | tf_op jit(solution)/shard_map/cond/branch_0_fun/pallas_call | solution.py:127
  54.0 4.3 %all-to-all-start.2 = ((bf16[16,48,512]{2,1,0:T(8,128)(2,1)}), bf16[16,48,512]{2,1,0:T(8,128)(2,1)S(1)}, u32[]{:S(2)}, u32[]{:S(2)}) async-start(bf16[16,48,512]{2,1,0:T(8,128)(2,1)} %get-tuple-element.74), calls=%async_computation.2 | async-start | bytes 1572864 | tf_op jit(solution)/shard_map/all_to_all | solution.py:196
  58.3 3.3 %collective-permute-start.5 = (bf16[768,256]{1,0:T(8,128)(2,1)S(1)}, bf16[768,256]{1,0:T(8,128)(2,1)S(1)}, u32[]{:S(2)}, u32[]{:S(2)}) collective-permute-start(bf16[768,256]{1,0:T(8,128)(2,1)S(1)} %copy-done.6), channel_id=1, source_target_pairs={{0,24},{8,16},{16,8},{24,0},{1,25},{9,17},{17,9},{25,1},{2,26},{10... | collective-permute-start | bytes 1179656 | tf_op jit(solution)/shard_map/ppermute | solution.py:167
  61.6 24.2 %collective-permute-done.5 = bf16[768,256]{1,0:T(8,128)(2,1)S(1)} collective-permute-done((bf16[768,256]{1,0:T(8,128)(2,1)S(1)}, bf16[768,256]{1,0:T(8,128)(2,1)S(1)}, u32[]{:S(2)}, u32[]{:S(2)}) %collective-permute-start.5) | collective-permute-done | bytes 393248 | tf_op jit(solution)/shard_map/ppermute | solution.py:167
  85.8 1.1 broadcast_select_fusion.1
  86.9 0.0 all-to-all-done.2
  86.9 0.6 convolution_convert_fusion
  87.5 2.3 %collective-permute-start.6 = (bf16[512,512]{1,0:T(8,128)(2,1)S(1)}, bf16[512,512]{1,0:T(8,128)(2,1)S(1)}, u32[]{:S(2)}, u32[]{:S(2)}) collective-permute-start(bf16[512,512]{1,0:T(8,128)(2,1)S(1)} %convolution_convert_fusion), channel_id=1, source_target_pairs={{0,8},{8,0},{1,9},{9,1},{2,10},{10,2},{3,11},{11,3},{4,12},{12,4},... | collective-permute-start | bytes 1572872 | tf_op jit(solution)/shard_map/ppermute | solution.py:206
  89.8 0.0 copy-done.4
  89.8 0.0 copy-done.5
  89.8 0.6 fusion.kept
  90.4 0.0 copy-start.12
  90.4 0.0 copy-start.11
  90.4 0.9 collective-permute-done.6.received
  91.3 0.9 shard_map.87
  92.2 7.4 %all-to-all-start.3 = ((bf16[16,64,256]{2,1,0:T(8,128)(2,1)}), bf16[16,64,256]{2,1,0:T(8,128)(2,1)S(1)}, u32[]{:S(2)}, u32[]{:S(2)}) async-start(bf16[16,64,256]{2,1,0:T(8,128)(2,1)} %bitcast.5), calls=%async_computation.3 | async-start | bytes 1048576 | tf_op jit(solution)/shard_map/all_to_all | solution.py:216
  99.6 9.4 %all-to-all-done.3 = bf16[16,64,256]{2,1,0:T(8,128)(2,1)S(1)} async-done(((bf16[16,64,256]{2,1,0:T(8,128)(2,1)}), bf16[16,64,256]{2,1,0:T(8,128)(2,1)S(1)}, u32[]{:S(2)}, u32[]{:S(2)}) %all-to-all-start.3) | async-done | bytes 524320 | tf_op jit(solution)/shard_map/all_to_all | solution.py:216
  109.0 0.1 convert_reduce_fusion
  109.1 0.0 copy-start.9
  109.1 0.7 fusion.8
  (14 shorter events, 0.0 us)
Async XLA Ops:
  0.6 20.0 %copy-start.1 = (bf16[3072,128]{1,0:T(8,128)(2,1)S(1)}, bf16[3072,128]{1,0:T(8,128)(2,1)}, u32[]{:S(2)}) copy-start(bf16[3072,128]{1,0:T(8,128)(2,1)} %own.1) | copy-start | bytes 2359300
  0.6 20.0 %collective-permute-start = (bf16[3072,128]{1,0:T(8,128)(2,1)}, bf16[3072,128]{1,0:T(8,128)(2,1)S(1)}, u32[]{:S(2)}, u32[]{:S(2)}) collective-permute-start(bf16[3072,128]{1,0:T(8,128)(2,1)} %own.1), channel_id=1, source_target_pairs={{0,8},{8,0},{1,9},{9,1},{2,10},{10,2},{3,11},{11,3},{4,12},{12,4},... | collective-permute-start | bytes 2359304 | tf_op jit(solution)/shard_map/ppermute | solution.py:88
  10.6 13.4 %collective-permute-start.3 = (bf16[768,256]{1,0:T(8,128)(2,1)S(1)}, bf16[768,256]{1,0:T(8,128)(2,1)S(1)}, u32[]{:S(2)}, u32[]{:S(2)}) collective-permute-start(bf16[768,256]{1,0:T(8,128)(2,1)S(1)} %constant_dynamic-slice_fusion.2), channel_id=1, source_target_pairs={{0,16},{8,24},{16,0},{24,8},{1,17},{9,25},{17,1},{25,9},{2,18},{10... | collective-permute-start | bytes 1179656 | tf_op jit(solution)/shard_map/ppermute | solution.py:167
  13.4 5.3 %collective-permute-start.1 = (bf16[256,128]{1,0:T(8,128)(2,1)S(1)}, bf16[256,128]{1,0:T(8,128)(2,1)S(1)}, u32[]{:S(2)}, u32[]{:S(2)}) collective-permute-start(bf16[256,128]{1,0:T(8,128)(2,1)S(1)} %get-tuple-element.73), channel_id=1, source_target_pairs={{0,1},{1,2},{2,3},{3,4},{4,5},{5,6},{6,7},{9,8},{10,9},{11,10},{12... | collective-permute-start | bytes 196616 | tf_op jit(solution)/shard_map/ppermute | solution.py:86
  14.7 5.9 %collective-permute-start.2 = (bf16[256,128]{1,0:T(8,128)(2,1)S(1)}, bf16[256,128]{1,0:T(8,128)(2,1)S(1)}, u32[]{:S(2)}, u32[]{:S(2)}) collective-permute-start(bf16[256,128]{1,0:T(8,128)(2,1)S(1)} %get-tuple-element.72), channel_id=1, source_target_pairs={{8,1},{9,2},{10,3},{11,4},{12,5},{13,6},{14,7},{1,8},{2,9},{3,10},... | collective-permute-start | bytes 196616 | tf_op jit(solution)/shard_map/ppermute | solution.py:87
  18.7 5.3 %copy-start.7 = (bf16[256,128]{1,0:T(8,128)(2,1)}, bf16[256,128]{1,0:T(8,128)(2,1)S(1)}, u32[]{:S(2)}) copy-start(bf16[256,128]{1,0:T(8,128)(2,1)S(1)} %collective-permute-done.1.own_edge) | copy-start | bytes 196612
  20.6 3.4 %copy-start.8 = (bf16[256,128]{1,0:T(8,128)(2,1)}, bf16[256,128]{1,0:T(8,128)(2,1)S(1)}, u32[]{:S(2)}) copy-start(bf16[256,128]{1,0:T(8,128)(2,1)S(1)} %collective-permute-done.2.other_edge) | copy-start | bytes 196612
  20.6 3.4 %copy-start.2 = (bf16[3072,128]{1,0:T(8,128)(2,1)}, bf16[3072,128]{1,0:T(8,128)(2,1)S(1)}, u32[]{:S(2)}) copy-start(bf16[3072,128]{1,0:T(8,128)(2,1)S(1)} %collective-permute-done.other) | copy-start | bytes 2359300
  24.0 13.3 %copy-start.3 = (bf16[768,256]{1,0:T(8,128)(2,1)}, bf16[768,256]{1,0:T(8,128)(2,1)S(1)}, u32[]{:S(2)}) copy-start(bf16[768,256]{1,0:T(8,128)(2,1)S(1)} %collective-permute-done.3) | copy-start | bytes 1179652
  24.0 28.2 %all-to-all-start.1 = ((bf16[32,48,128]{2,1,0:T(8,128)(2,1)}), bf16[32,48,128]{2,1,0:T(8,128)(2,1)S(1)}, u32[]{:S(2)}, u32[]{:S(2)}) async-start(bf16[32,48,128]{2,1,0:T(8,128)(2,1)} %bitcast.3), calls=%async_computation.1 | async-start | bytes 786432 | tf_op jit(solution)/shard_map/all_to_all | solution.py:183
  37.3 4.9 %copy-start.10 = (s32[4]{0:T(128)S(1)}, s32[4]{0:T(128)}, u32[]{:S(2)}) copy-start(s32[4]{0:T(128)} %owners_ref.1) | copy-start | bytes 52
  37.4 14.9 %copy-start = (bf16[24,3,128,128]{3,2,1,0:T(8,128)(2,1)S(1)}, bf16[24,3,128,128]{3,2,1,0:T(8,128)(2,1)}, u32[]{:S(2)}) copy-start(bf16[24,3,128,128]{3,2,1,0:T(8,128)(2,1)} %dipole.1) | copy-start | bytes 7077892
  40.3 3.9 %collective-permute-start.4 = (bf16[768,256]{1,0:T(8,128)(2,1)}, bf16[768,256]{1,0:T(8,128)(2,1)}, u32[]{:S(2)}, u32[]{:S(2)}) collective-permute-start(bf16[768,256]{1,0:T(8,128)(2,1)} %get-tuple-element.69), channel_id=1, source_target_pairs={{0,8},{8,0},{16,24},{24,16},{1,9},{9,1},{17,25},{25,17},{2,10},{10... | collective-permute-start | bytes 1179656 | tf_op jit(solution)/shard_map/ppermute | solution.py:167
  54.0 4.3 %copy-start.6 = (bf16[768,256]{1,0:T(8,128)(2,1)S(1)}, bf16[768,256]{1,0:T(8,128)(2,1)}, u32[]{:S(2)}) copy-start(bf16[768,256]{1,0:T(8,128)(2,1)} %get-tuple-element.68) | copy-start | bytes 1179652
  54.0 32.8 %all-to-all-start.2 = ((bf16[16,48,512]{2,1,0:T(8,128)(2,1)}), bf16[16,48,512]{2,1,0:T(8,128)(2,1)S(1)}, u32[]{:S(2)}, u32[]{:S(2)}) async-start(bf16[16,48,512]{2,1,0:T(8,128)(2,1)} %get-tuple-element.74), calls=%async_computation.2 | async-start | bytes 1572864 | tf_op jit(solution)/shard_map/all_to_all | solution.py:196
  58.3 27.5 %collective-permute-start.5 = (bf16[768,256]{1,0:T(8,128)(2,1)S(1)}, bf16[768,256]{1,0:T(8,128)(2,1)S(1)}, u32[]{:S(2)}, u32[]{:S(2)}) collective-permute-start(bf16[768,256]{1,0:T(8,128)(2,1)S(1)} %copy-done.6), channel_id=1, source_target_pairs={{0,24},{8,16},{16,8},{24,0},{1,25},{9,17},{17,9},{25,1},{2,26},{10... | collective-permute-start | bytes 1179656 | tf_op jit(solution)/shard_map/ppermute | solution.py:167
  86.9 2.9 %copy-start.4 = (bf16[768,256]{1,0:T(8,128)(2,1)S(1)}, bf16[768,256]{1,0:T(8,128)(2,1)}, u32[]{:S(2)}) copy-start(bf16[768,256]{1,0:T(8,128)(2,1)} %get-tuple-element.66) | copy-start | bytes 1179652
  86.9 2.9 %copy-start.5 = (bf16[768,256]{1,0:T(8,128)(2,1)S(1)}, bf16[768,256]{1,0:T(8,128)(2,1)}, u32[]{:S(2)}) copy-start(bf16[768,256]{1,0:T(8,128)(2,1)} %get-tuple-element.67) | copy-start | bytes 1179652
  87.5 3.8 %collective-permute-start.6 = (bf16[512,512]{1,0:T(8,128)(2,1)S(1)}, bf16[512,512]{1,0:T(8,128)(2,1)S(1)}, u32[]{:S(2)}, u32[]{:S(2)}) collective-permute-start(bf16[512,512]{1,0:T(8,128)(2,1)S(1)} %convolution_convert_fusion), channel_id=1, source_target_pairs={{0,8},{8,0},{1,9},{9,1},{2,10},{10,2},{3,11},{11,3},{4,12},{12,4},... | collective-permute-start | bytes 1572872 | tf_op jit(solution)/shard_map/ppermute | solution.py:206
  90.4 9.2 %copy-start.12 = (f32[64]{0:T(128)S(1)}, f32[64]{0:T(128)}, u32[]{:S(2)}) copy-start(f32[64]{0:T(128)} %param.14) | copy-start | bytes 772
  90.4 18.7 %copy-start.11 = (f32[256]{0:T(256)S(1)}, f32[256]{0:T(256)}, u32[]{:S(2)}) copy-start(f32[256]{0:T(256)} %param.15) | copy-start | bytes 3076
  92.2 16.8 %all-to-all-start.3 = ((bf16[16,64,256]{2,1,0:T(8,128)(2,1)}), bf16[16,64,256]{2,1,0:T(8,128)(2,1)S(1)}, u32[]{:S(2)}, u32[]{:S(2)}) async-start(bf16[16,64,256]{2,1,0:T(8,128)(2,1)} %bitcast.5), calls=%async_computation.3 | async-start | bytes 1048576 | tf_op jit(solution)/shard_map/all_to_all | solution.py:216
  109.1 0.7 copy-start.9
